TPU v7x, 32 devices: a whole 2x2x4 slice. The times are simulated.
32 devices in a mesh: dp: 8 (over y, x, core), band: 4 (over z).
Axes of the slice: x: 2, y: 2, z: 4, core: 2. Of those that a mesh axis runs over, the one named last changes fastest.
Arguments:
- latents: bfloat16 [32, 24, 24, 1536], P('dp', 'band'), may hold values from -13 to 13
- clip_text: bfloat16 [32, 77, 1280], P('dp'), may hold values from -6 to 6
- embedding: bfloat16 [32, 64], P('dp'), may hold values from -6 to 6
- lengths: int32 [32], P('dp'), may hold values from 5 to 77, as said below
- conv_weight: bfloat16 [9, 1536], P(None, ('dp', 'band')), may hold values from -2 to 2
- up_weight: bfloat16 [1536, 6144], P(('dp', 'band')), may hold values from -0.15625 to 0.15625
- down_weight: bfloat16 [6144, 1536], P(('dp', 'band')), may hold values from -0.078125 to 0.078125
- hidden_vecs: bfloat16 [3, 6144], P(None, ('dp', 'band')), may hold values from -3 to 3
- vectors: bfloat16 [8, 1536], P(None, ('dp', 'band')), may hold values from -2 to 2
- time_weight: bfloat16 [64, 3072], P(None, ('dp', 'band')), may hold values from -0.375 to 0.375
- map_weight: bfloat16 [1280, 1536], P(('dp', 'band')), may hold values from -0.15625 to 0.15625
- attn_in: bfloat16 [3, 1536, 1536], P(None, ('dp', 'band')), may hold values from -0.15625 to 0.15625
- out_weight: bfloat16 [1536, 1536], P(('dp', 'band')), may hold values from -1.25 to 1.25
- grad_out: bfloat16 [32, 24, 24, 1536], P('dp', 'band'), may hold values from -6 to 6
Outputs:
- layer_out: bfloat16 [32, 24, 24, 1536], P('dp', 'band')
- latent_grad: bfloat16 [32, 24, 24, 1536], P('dp', 'band')
- text_grad: bfloat16 [32, 77, 1280], P('dp', None, 'band')
- conv_grad: float32 [9, 1536], P(None, ('dp', 'band'))
- up_grad: float32 [1536, 6144], P(('dp', 'band'))
- down_grad: float32 [6144, 1536], P(('dp', 'band'))
- hidden_grad: float32 [3, 6144], P(None, ('dp', 'band'))
- vector_grad: float32 [8, 1536], P(None, ('dp', 'band'))
- time_grad: float32 [64, 3072], P(None, ('dp', 'band'))
- map_grad: float32 [1280, 1536], P(('dp', 'band'))
- attn_grad: float32 [3, 1536, 1536], P(None, ('dp', 'band'))
- out_grad: float32 [1536, 1536], P(('dp', 'band'))
Inputs may be any that keep to these rules, and one draw needn't show every extreme that they name: `lengths`: in every draw some latent uses all 77 text tokens and another uses 5.
All inputs are finite; a program needn't handle non-finite values.
Results may differ from a plain program's by a relative error of at most 0.024.
Values may be sent and summed in bfloat16 or wider, within the bound.
A program may use at most 448 MiB of HBM per device.

v0:
```python
import jax
import jax.numpy as jnp
from jax import lax
from jax.sharding import PartitionSpec as P

HEAD_DIM = 64


def with_halo(array, sides, width):
    for axis, dim in sides:
        size, length = (lax.axis_size(axis), array.shape[dim])
        up = [(i, (i + 1) % size) for i in range(size - 1)]
        down = [(j, i) for i, j in up]
        last = lax.slice_in_dim(array, length - width, length, axis=dim)
        first = lax.slice_in_dim(array, 0, width, axis=dim)
        before = lax.ppermute(last, axis, up)
        after = lax.ppermute(first, axis, down)
        array = jnp.concatenate([before, array, after], axis=dim)
    return array


def product(left_op, right_op):
    return jnp.dot(left_op, right_op, preferred_element_type=jnp.float32)


def product_tn(left_op, right_op):
    return lax.dot_general(
        left_op, right_op, (((0,), (0,)), ((), ())), preferred_element_type=jnp.float32
    )


def product_nt(left_op, right_op):
    return lax.dot_general(
        left_op, right_op, (((1,), (1,)), ((), ())), preferred_element_type=jnp.float32
    )


def norm_parts(array_in):
    center = array_in - jnp.mean(array_in, axis=-1, keepdims=True)
    spread = jnp.mean(center * center, axis=-1, keepdims=True)
    inverse = lax.rsqrt(spread + 1e-06)
    return (center * inverse, inverse)


def norm_back(incoming, normed, inverse):
    return inverse * (
        incoming
        - jnp.mean(incoming, axis=-1, keepdims=True)
        - normed * jnp.mean(incoming * normed, axis=-1, keepdims=True)
    )


def column_sums(array_in):
    return jnp.sum(array_in.astype(jnp.float32), axis=0)


def gelu_exact(array_in):
    return jax.nn.gelu(array_in, approximate=False)


def masked_scores(query_one, key_one, valid_one):
    raw_scores = jnp.einsum(
        "qhd,khd->hqk", query_one, key_one, preferred_element_type=jnp.float32
    ) * HEAD_DIM ** (-0.5)
    return jnp.where(valid_one[None, None, :], raw_scores, -1000000000.0)


def attend_one(items):
    query_one, key_one, value_one, valid_one = items
    scores = masked_scores(query_one, key_one, valid_one)
    top_score = jnp.max(scores, axis=-1, keepdims=True)
    exponent = jnp.exp(scores - top_score)
    row_total = jnp.sum(exponent, axis=-1, keepdims=True)
    log_total = top_score + jnp.log(row_total)
    probs_low = (exponent / row_total).astype(jnp.bfloat16)
    mixed_one = jnp.einsum(
        "hqk,khd->qhd", probs_low, value_one, preferred_element_type=jnp.float32
    ).astype(jnp.bfloat16)
    return (mixed_one, log_total)


def attend_back(items):
    query_one, key_one, value_one, valid_one, log_one, gmix_one = items
    weights_again = jnp.exp(masked_scores(query_one, key_one, valid_one) - log_one)
    g_probs = jnp.einsum("qhd,khd->hqk", gmix_one, value_one, preferred_element_type=jnp.float32)
    inner_sum = jnp.sum(weights_again * g_probs, axis=-1, keepdims=True)
    g_score = (weights_again * (g_probs - inner_sum)).astype(jnp.bfloat16)
    probs_again = weights_again.astype(jnp.bfloat16)
    g_query = (
        jnp.einsum("hqk,khd->qhd", g_score, key_one, preferred_element_type=jnp.float32)
        * HEAD_DIM ** (-0.5)
    ).astype(jnp.bfloat16)
    g_key = jnp.einsum(
        "hqk,qhd->khd", g_score, query_one, preferred_element_type=jnp.float32
    ) * HEAD_DIM ** (-0.5)
    g_value = jnp.einsum("hqk,qhd->khd", probs_again, gmix_one, preferred_element_type=jnp.float32)
    return (g_query, g_key, g_value)


def per_device(
    latents,
    clip_text,
    embedding,
    lengths,
    conv_weight,
    up_weight,
    down_weight,
    hidden_vecs,
    vectors,
    time_weight,
    map_weight,
    attn_in,
    out_weight,
    grad_out,
):
    lat_count, band_rows, columns, channels = latents.shape
    tokens_lat = band_rows * columns
    tok_rows = lat_count * tokens_lat
    hidden_width = up_weight.shape[1]
    text_len = clip_text.shape[1]
    clip_width = clip_text.shape[2]
    band_size = lax.axis_size("band")
    band_index = lax.axis_index("band")
    pixel_count = tokens_lat * band_size
    head_count = channels // HEAD_DIM
    band_share = 1.0 / band_size
    res_shards = (conv_weight, up_weight, down_weight, hidden_vecs, vectors)
    attn_shards = (time_weight, map_weight, attn_in, out_weight)
    res_full = (
        lax.all_gather(res_shards[0], ("dp", "band"), axis=1, tiled=True),
        lax.all_gather(res_shards[1], ("dp", "band"), axis=0, tiled=True),
        lax.all_gather(res_shards[2], ("dp", "band"), axis=0, tiled=True),
        lax.all_gather(res_shards[3], ("dp", "band"), axis=1, tiled=True),
        lax.all_gather(res_shards[4], ("dp", "band"), axis=1, tiled=True),
    )
    attn_full = (
        lax.all_gather(attn_shards[0], ("dp", "band"), axis=1, tiled=True),
        lax.all_gather(attn_shards[1], ("dp", "band"), axis=0, tiled=True),
        lax.all_gather(attn_shards[2], ("dp", "band"), axis=1, tiled=True),
        lax.all_gather(attn_shards[3], ("dp", "band"), axis=0, tiled=True),
    )
    hidden_values = res_full[3].astype(jnp.float32)
    vec_values = res_full[4].astype(jnp.float32)
    framed = with_halo(latents, (("band", 1),), 1)
    framed = jnp.pad(framed, ((0, 0), (0, 0), (1, 1), (0, 0)))
    conv_taps = res_full[0].astype(jnp.float32)
    conv_out = jnp.broadcast_to(vec_values[0], latents.shape)
    for offset in range(9):
        row_shift = offset // 3
        col_shift = offset % 3
        conv_out = conv_out + conv_taps[offset] * framed[
            :, row_shift : row_shift + band_rows, col_shift : col_shift + columns
        ].astype(jnp.float32)
    first_norm, first_inv = norm_parts(conv_out.reshape(tok_rows, channels))
    first_in = first_norm.astype(jnp.bfloat16)
    up_out = product(first_in, res_full[1]) + hidden_values[0]
    active = gelu_exact(up_out)
    active_lat = active.reshape(lat_count, tokens_lat, hidden_width)
    square_sums = lax.psum(
        jnp.sum(active_lat * active_lat, axis=1).astype(jnp.bfloat16), "band"
    ).astype(jnp.float32)
    strength = jnp.sqrt(square_sums)
    grn_denom = jnp.mean(strength, axis=-1, keepdims=True) + 1e-06
    grn_ratio = strength / grn_denom
    gamma_vec = hidden_values[1]
    grn_out = (
        (gamma_vec * (active_lat * grn_ratio[:, None]) + hidden_values[2] + active_lat)
        .astype(jnp.bfloat16)
        .reshape(tok_rows, hidden_width)
    )
    first_sum = latents.reshape(tok_rows, channels).astype(jnp.float32) + (
        product(grn_out, res_full[2]) + vec_values[1]
    )
    modulation = product(embedding, attn_full[0])
    scale_vec = modulation[:, :channels] + vec_values[2]
    shift_vec = modulation[:, channels:] + vec_values[3]
    first_lat = first_sum.reshape(lat_count, tokens_lat, channels)
    second = first_lat * (1.0 + scale_vec[:, None]) + shift_vec[:, None]
    second_norm, second_inv = norm_parts(second)
    second_in = second_norm.astype(jnp.bfloat16).reshape(tok_rows, channels)
    clip_words = (
        jax.nn.silu(clip_text.astype(jnp.float32))
        .astype(jnp.bfloat16)
        .reshape(lat_count * text_len, clip_width)
    )
    mapped = (product(clip_words, attn_full[1]) + vec_values[4]).astype(jnp.bfloat16)
    projections = attn_full[2]
    query_rows = (product(second_in, projections[0]) + vec_values[5]).astype(jnp.bfloat16)
    pixel_key = (
        product(second_in, projections[1])
        .astype(jnp.bfloat16)
        .reshape(lat_count, tokens_lat, channels)
    )
    pixel_value = (
        (product(second_in, projections[2]) + vec_values[6])
        .astype(jnp.bfloat16)
        .reshape(lat_count, tokens_lat, channels)
    )
    all_key, all_value = (
        lax.all_gather(pixel_key, "band", axis=1, tiled=True),
        lax.all_gather(pixel_value, "band", axis=1, tiled=True),
    )
    text_key = (
        product(mapped, projections[1]).astype(jnp.bfloat16).reshape(lat_count, text_len, channels)
    )
    text_value = (
        (product(mapped, projections[2]) + vec_values[6])
        .astype(jnp.bfloat16)
        .reshape(lat_count, text_len, channels)
    )
    key_rows = jnp.concatenate([all_key, text_key], axis=1).reshape(
        lat_count, pixel_count + text_len, head_count, HEAD_DIM
    )
    value_rows = jnp.concatenate([all_value, text_value], axis=1).reshape(
        lat_count, pixel_count + text_len, head_count, HEAD_DIM
    )
    query_heads = query_rows.reshape(lat_count, tokens_lat, head_count, HEAD_DIM)
    key_places = jnp.arange(pixel_count + text_len, dtype=jnp.int32)
    valid_keys = key_places[None, :] < pixel_count + lengths[:, None]
    mixed_heads, log_totals = lax.map(attend_one, (query_heads, key_rows, value_rows, valid_keys))
    mixed_out = mixed_heads.reshape(tok_rows, channels)
    attended = product(mixed_out, attn_full[3]) + vec_values[7]
    layer_out = (
        (second.reshape(tok_rows, channels) + attended).astype(jnp.bfloat16).reshape(latents.shape)
    )
    res_back = (
        lax.all_gather(res_shards[0], ("dp", "band"), axis=1, tiled=True),
        lax.all_gather(res_shards[1], ("dp", "band"), axis=0, tiled=True),
        lax.all_gather(res_shards[2], ("dp", "band"), axis=0, tiled=True),
        lax.all_gather(res_shards[3], ("dp", "band"), axis=1, tiled=True),
        lax.all_gather(res_shards[4], ("dp", "band"), axis=1, tiled=True),
    )
    attn_back = (
        lax.all_gather(attn_shards[0], ("dp", "band"), axis=1, tiled=True),
        lax.all_gather(attn_shards[1], ("dp", "band"), axis=0, tiled=True),
        lax.all_gather(attn_shards[2], ("dp", "band"), axis=1, tiled=True),
        lax.all_gather(attn_shards[3], ("dp", "band"), axis=0, tiled=True),
    )
    proj_back = attn_back[2]
    grad_rows = grad_out.reshape(tok_rows, channels)
    grad_float = grad_rows.astype(jnp.float32)
    out_grad_w = product_tn(mixed_out, grad_rows)
    g_mixed = (
        product_nt(grad_rows, attn_back[3])
        .astype(jnp.bfloat16)
        .reshape(lat_count, tokens_lat, head_count, HEAD_DIM)
    )
    g_query_heads, g_key, g_value = lax.map(
        attend_back, (query_heads, key_rows, value_rows, valid_keys, log_totals, g_mixed)
    )
    g_query = g_query_heads.reshape(tok_rows, channels)
    g_key = g_key.reshape(lat_count, pixel_count + text_len, channels)
    g_value = g_value.reshape(lat_count, pixel_count + text_len, channels)
    pixel_gkey, pixel_gvalue = (
        lax.psum_scatter(
            g_key[:, :pixel_count].astype(jnp.bfloat16), "band", scatter_dimension=1, tiled=True
        ).astype(jnp.float32),
        lax.psum_scatter(
            g_value[:, :pixel_count].astype(jnp.bfloat16), "band", scatter_dimension=1, tiled=True
        ).astype(jnp.float32),
    )
    text_gkey, text_gvalue = (
        lax.psum(g_key[:, pixel_count:].astype(jnp.bfloat16), "band").astype(jnp.float32),
        lax.psum(g_value[:, pixel_count:].astype(jnp.bfloat16), "band").astype(jnp.float32),
    )
    pixel_kb = pixel_gkey.astype(jnp.bfloat16).reshape(tok_rows, channels)
    pixel_vb = pixel_gvalue.astype(jnp.bfloat16).reshape(tok_rows, channels)
    text_kb = text_gkey.astype(jnp.bfloat16).reshape(lat_count * text_len, channels)
    text_vb = text_gvalue.astype(jnp.bfloat16).reshape(lat_count * text_len, channels)
    g_second_in = (
        product_nt(g_query, proj_back[0])
        + product_nt(pixel_kb, proj_back[1])
        + product_nt(pixel_vb, proj_back[2])
    )
    grad_query_w = product_tn(second_in, g_query)
    grad_key_w = product_tn(second_in, pixel_kb) + band_share * product_tn(mapped, text_kb)
    grad_value_w = product_tn(second_in, pixel_vb) + band_share * product_tn(mapped, text_vb)
    g_mapped = (product_nt(text_kb, proj_back[1]) + product_nt(text_vb, proj_back[2])).astype(
        jnp.bfloat16
    )
    grad_map_w = band_share * product_tn(clip_words, g_mapped)
    clip_slice = clip_width // band_size
    map_rows = lax.dynamic_slice_in_dim(attn_back[1], band_index * clip_slice, clip_slice, 0)
    text_part = lax.dynamic_slice_in_dim(clip_text, band_index * clip_slice, clip_slice, 2).astype(
        jnp.float32
    )
    sigmoid_text = jax.nn.sigmoid(text_part)
    g_words = product_nt(g_mapped, map_rows).reshape(lat_count, text_len, clip_slice)
    text_grad = (g_words * (sigmoid_text * (1.0 + text_part * (1.0 - sigmoid_text)))).astype(
        jnp.bfloat16
    )
    g_second = grad_float.reshape(lat_count, tokens_lat, channels) + norm_back(
        g_second_in.reshape(lat_count, tokens_lat, channels), second_norm, second_inv
    )
    g_scale = jnp.sum(g_second * first_lat, axis=1)
    g_shift = jnp.sum(g_second, axis=1)
    grad_time_w = lax.dot_general(
        embedding.astype(jnp.float32),
        jnp.concatenate([g_scale, g_shift], axis=1),
        (((0,), (0,)), ((), ())),
        precision=lax.Precision.HIGHEST,
        preferred_element_type=jnp.float32,
    )
    attn_grads = (
        lax.psum_scatter(grad_time_w, ("dp", "band"), scatter_dimension=1, tiled=True),
        lax.psum_scatter(grad_map_w, ("dp", "band"), scatter_dimension=0, tiled=True),
        lax.psum_scatter(
            jnp.stack([grad_query_w, grad_key_w, grad_value_w]),
            ("dp", "band"),
            scatter_dimension=1,
            tiled=True,
        ),
        lax.psum_scatter(out_grad_w, ("dp", "band"), scatter_dimension=0, tiled=True),
    )
    g_first = g_second * (1.0 + scale_vec[:, None])
    g_down = g_first.astype(jnp.bfloat16).reshape(tok_rows, channels)
    grad_down_w = product_tn(grn_out, g_down)
    g_grn = product_nt(g_down, res_back[2]).reshape(lat_count, tokens_lat, hidden_width)
    grad_gamma = jnp.sum(g_grn * active_lat * grn_ratio[:, None], axis=(0, 1))
    grad_beta = jnp.sum(g_grn, axis=(0, 1))
    g_ratio = lax.psum(
        jnp.sum(g_grn * gamma_vec * active_lat, axis=1).astype(jnp.bfloat16), "band"
    ).astype(jnp.float32)
    g_strength = g_ratio / grn_denom - jnp.sum(g_ratio * strength, axis=-1, keepdims=True) / (
        hidden_width * grn_denom * grn_denom
    )
    g_active = (
        g_grn * (1.0 + gamma_vec * grn_ratio[:, None])
        + active_lat * (g_strength / strength)[:, None]
    )
    gelu_value, gelu_pull = jax.vjp(gelu_exact, up_out)
    g_up = gelu_pull(g_active.reshape(tok_rows, hidden_width))[0].astype(jnp.bfloat16)
    grad_up_w = product_tn(first_in, g_up)
    g_conv = (
        norm_back(product_nt(g_up, res_back[1]), first_norm, first_inv)
        .astype(jnp.bfloat16)
        .reshape(latents.shape)
    )
    g_framed = with_halo(g_conv, (("band", 1),), 1)
    g_framed = jnp.pad(g_framed, ((0, 0), (0, 0), (1, 1), (0, 0)))
    conv_back = res_back[0].astype(jnp.float32)
    g_conv_f = g_conv.astype(jnp.float32)
    back_sum = g_first.reshape(latents.shape)
    tap_grads = []
    for offset in range(9):
        row_shift = offset // 3
        col_shift = offset % 3
        window = framed[
            :, row_shift : row_shift + band_rows, col_shift : col_shift + columns
        ].astype(jnp.float32)
        tap_grads.append(jnp.sum(g_conv_f * window, axis=(0, 1, 2)))
        back_sum = back_sum + conv_back[offset] * g_framed[
            :, 2 - row_shift : 2 - row_shift + band_rows, 2 - col_shift : 2 - col_shift + columns
        ].astype(jnp.float32)
    latent_grad = back_sum.astype(jnp.bfloat16)
    grad_vectors = jnp.stack(
        [
            jnp.sum(g_conv_f, axis=(0, 1, 2)),
            column_sums(g_down),
            jnp.sum(g_scale, axis=0),
            jnp.sum(g_shift, axis=0),
            band_share * column_sums(g_mapped),
            column_sums(g_query),
            column_sums(pixel_vb) + band_share * column_sums(text_vb),
            jnp.sum(grad_float, axis=0),
        ]
    )
    grad_hidden = jnp.stack([column_sums(g_up), grad_gamma, grad_beta])
    grad_conv_w = jnp.stack(tap_grads)
    res_grads = (
        lax.psum_scatter(grad_conv_w, ("dp", "band"), scatter_dimension=1, tiled=True),
        lax.psum_scatter(grad_up_w, ("dp", "band"), scatter_dimension=0, tiled=True),
        lax.psum_scatter(grad_down_w, ("dp", "band"), scatter_dimension=0, tiled=True),
        lax.psum_scatter(grad_hidden, ("dp", "band"), scatter_dimension=1, tiled=True),
        lax.psum_scatter(grad_vectors, ("dp", "band"), scatter_dimension=1, tiled=True),
    )
    return (
        layer_out,
        latent_grad,
        text_grad,
        res_grads[0],
        res_grads[1],
        res_grads[2],
        res_grads[3],
        res_grads[4],
        attn_grads[0],
        attn_grads[1],
        attn_grads[2],
        attn_grads[3],
    )


def solution(mesh):
    placed = (
        P("dp", "band", None, None),
        P("dp", None, None),
        P("dp", None),
        P("dp"),
        P(None, ("dp", "band")),
        P(("dp", "band"), None),
        P(("dp", "band"), None),
        P(None, ("dp", "band")),
        P(None, ("dp", "band")),
        P(None, ("dp", "band")),
        P(("dp", "band"), None),
        P(None, ("dp", "band"), None),
        P(("dp", "band"), None),
        P("dp", "band", None, None),
    )
    return jax.shard_map(
        per_device,
        mesh=mesh,
        in_specs=placed,
        out_specs=(
            P("dp", "band", None, None),
            P("dp", "band", None, None),
            P("dp", None, "band"),
            P(None, ("dp", "band")),
            P(("dp", "band"), None),
            P(("dp", "band"), None),
            P(None, ("dp", "band")),
            P(None, ("dp", "band")),
            P(None, ("dp", "band")),
            P(("dp", "band"), None),
            P(None, ("dp", "band"), None),
            P(("dp", "band"), None),
        ),
        check_vma=False,
    )
```

profile of v0, /device:TPU:0, one launch (start us, length us, event | category | flops | bytes accessed | tf_op | source)
XLA Modules:
  0.0 3073.5 jit_solution(16898498243577482338)
XLA Ops:
  19.0 84.4 %all-gather.3 = bf16[32,96,64]{1,2,0:T(8,128)(2,1)S(1)} all-gather(bf16[1,96,64]{1,2,0:T(8,128)(2,1)} %bitcast.371), channel_id=1, replica_groups=mesh['dp'=8,'band'=4] {'dp','band'}, dimensions={0}, use_global_device_ids=true | all-gather | bytes 405504 | tf_op jit(solution)/shard_map/all_gather | solution.py:137
  104.4 69.2 %all-gather.1 = bf16[32,48,8]{1,2,0:T(8,128)(2,1)S(1)} all-gather(bf16[1,48,8]{1,2,0:T(8,128)(2,1)S(1)} %bitcast.373), channel_id=1, replica_groups=mesh['dp'=8,'band'=4] {'dp','band'}, dimensions={0}, use_global_device_ids=true | all-gather | bytes 25344 | tf_op jit(solution)/shard_map/all_gather | solution.py:134
  174.5 67.5 %all-gather = bf16[32,192,3]{1,2,0:T(4,128)(2,1)S(1)} all-gather(bf16[1,192,3]{1,2,0:T(4,128)(2,1)S(1)} %bitcast.374), channel_id=1, replica_groups=mesh['dp'=8,'band'=4] {'dp','band'}, dimensions={0}, use_global_device_ids=true | all-gather | bytes 38016 | tf_op jit(solution)/shard_map/all_gather | solution.py:133
  242.8 69.0 %all-gather.2 = bf16[32,48,9]{1,2,0:T(8,128)(2,1)S(1)} all-gather(bf16[1,48,9]{1,2,0:T(8,128)(2,1)S(1)} %bitcast.372), channel_id=1, replica_groups=mesh['dp'=8,'band'=4] {'dp','band'}, dimensions={0}, use_global_device_ids=true | all-gather | bytes 28512 | tf_op jit(solution)/shard_map/all_gather | solution.py:130
  328.3 46.0 %multiply_multiply_fusion.5 = (f32[576,6144]{1,0:T(8,128)}, f32[576,6144]{1,0:T(8,128)}, f32[576,6144]{1,0:T(8,128)}) fusion(f32[6144]{0:T(1024)} %bitcast.361, bf16[1536,6144]{1,0:T(8,128)(2,1)} %all-gather.12.cloned.1.call-done, f32[576,1536]{1,0:T(8,128)} %fusion.118), kind=kOutput, calls=%fused_computation.100 | convolution fusion | flops 11102552064 | bytes 64905216 | tf_op jit(solution)/shard_map/dot_general | solution.py:23
  451.2 52.2 %all-gather.24.cloned.1.call-done = bf16[1536,1536]{1,0:T(8,128)(2,1)} async-done(((bf16[48,1536]{1,0:T(8,128)(2,1)}), bf16[1536,1536]{1,0:T(8,128)(2,1)}) %all-gather.24.cloned.1.call-update) | async-done | bytes 4718608 | tf_op jit(solution)/shard_map/all_gather | solution.py:140
  551.4 80.6 %all-gather.18.cloned.1.call-done = bf16[4,576,1536]{2,1,0:T(8,128)(2,1)} async-done(((bf16[4,144,1536]{2,1,0:T(8,128)(2,1)}), bf16[4,576,1536]{2,1,0:T(8,128)(2,1)}) %all-gather.18.cloned.1.call-update) | async-done | bytes 7077904 | tf_op jit(solution)/shard_map/all_gather | solution.py:201
  642.3 118.3 %all-gather.22.cloned.1.call-done = bf16[4,576,1536]{2,1,0:T(8,128)(2,1)} async-done(((bf16[4,144,1536]{2,1,0:T(8,128)(2,1)}), bf16[4,576,1536]{2,1,0:T(8,128)(2,1)}) %all-gather.22.cloned.1.call-update) | async-done | bytes 7077904 | tf_op jit(solution)/shard_map/all_gather | solution.py:200
  791.0 47.5 %while.26 = (s32[]{:T(128)}, bf16[4,144,24,64]{1,3,2,0:T(8,128)(2,1)}, f32[4,24,144,1]{2,1,3,0:T(8,128)S(1)}, bf16[4,653,24,64]{1,3,2,0:T(8,128)(2,1)}, pred[4,6...) while((s32[]{:T(128)}, ...), condition=%wide.region_10.11_spmd, body=%wide.region_7.10_spmd.sunk | while | flops 605031552 | bytes 33521304 | solution.py:220
  840.6 109.9 %while.27 = (s32[]{:T(128)}, bf16[4,144,24,64]{1,3,2,0:T(8,128)(2,1)}, bf16[4,653,24,64]{1,3,2,0:T(8,128)(2,1)}, bf16[4,653,24,64]{1,3,2,0:T(8,128)(2,1)}, bf16[...) while((s32[]{:T(128)}, ...), condition=%wide.region_13.14_spmd, body=%wide.region_11.13_spmd.sunk | while | flops 1479624960 | bytes 99330112 | solution.py:248
  1009.2 29.7 all-reduce.5.cloned.1.call-done
  1052.4 111.4 %reduce-scatter.22.cloned.1.call-done = bf16[4,144,1536]{2,1,0:T(8,128)(2,1)} async-done(((bf16[4,576,1536]{2,1,0:T(8,128)(2,1)}), bf16[4,144,1536]{2,1,0:T(8,128)(2,1)}) %reduce-scatter.22.cloned.1.call-update) | async-done | bytes 1769488 | tf_op jit(solution)/shard_map/reduce_scatter | solution.py:258
  1171.6 118.5 %reduce-scatter.20.cloned.1.call-done = bf16[4,144,1536]{2,1,0:T(8,128)(2,1)} async-done(((bf16[4,576,1536]{2,1,0:T(8,128)(2,1)}), bf16[4,144,1536]{2,1,0:T(8,128)(2,1)}) %reduce-scatter.20.cloned.1.call-update) | async-done | bytes 1769488 | tf_op jit(solution)/shard_map/reduce_scatter | solution.py:255
  1312.8 23.6 multiply_reduce_fusion.1
  1509.1 22.4 fusion.139
  1534.6 22.2 convolution_bitcast_fusion
  1580.4 30.5 reduce-scatter.34.cloned.1.call-done
  1612.3 105.3 %reduce-scatter.36.cloned.1.call-done = f32[192,3]{1,0:T(8,128)} async-done(((f32[6144,3]{1,0:T(8,128)}), f32[192,3]{1,0:T(8,128)}) %reduce-scatter.36.cloned.1.call-update) | async-done | bytes 2320
  1726.6 93.1 %reduce-scatter.40.cloned.1.call-done = f32[96,64]{1,0:T(8,128)} async-done(((f32[3072,64]{1,0:T(8,128)}), f32[96,64]{1,0:T(8,128)}) %reduce-scatter.40.cloned.1.call-update) | async-done | bytes 24592
  1821.2 126.8 %reduce-scatter.28.cloned.1.call-done = f32[40,1536]{1,0:T(8,128)} async-done(((f32[1280,1536]{1,0:T(8,128)}), f32[40,1536]{1,0:T(8,128)}) %reduce-scatter.28.cloned.1.call-update) | async-done | bytes 245776 | tf_op jit(solution)/shard_map/reduce_scatter | solution.py:306
  1948.0 141.4 %reduce-scatter.32.cloned.1.call-done = f32[48,1536]{1,0:T(8,128)} async-done(((f32[1536,1536]{1,0:T(8,128)}), f32[48,1536]{1,0:T(8,128)}) %reduce-scatter.32.cloned.1.call-update) | async-done | bytes 294928 | tf_op jit(solution)/shard_map/reduce_scatter | solution.py:313
  2089.4 266.9 %reduce-scatter.30.cloned.1.call-done = f32[3,48,1536]{2,1,0:T(8,128)} async-done(((f32[3,1536,1536]{2,1,0:T(8,128)}), f32[3,48,1536]{2,1,0:T(8,128)}) %reduce-scatter.30.cloned.1.call-update) | async-done | bytes 884752 | tf_op jit(solution)/shard_map/reduce_scatter | solution.py:307
  2356.3 355.2 %reduce-scatter.24.cloned.1.call-done = f32[48,6144]{1,0:T(8,128)} async-done(((f32[1536,6144]{1,0:T(8,128)}), f32[48,6144]{1,0:T(8,128)}) %reduce-scatter.24.cloned.1.call-update) | async-done | bytes 1179664 | tf_op jit(solution)/shard_map/reduce_scatter | solution.py:372
  2711.5 355.2 %reduce-scatter.26.cloned.1.call-done = f32[192,1536]{1,0:T(8,128)} async-done(((f32[6144,1536]{1,0:T(8,128)}), f32[192,1536]{1,0:T(8,128)}) %reduce-scatter.26.cloned.1.call-update) | async-done | bytes 1179664 | tf_op jit(solution)/shard_map/reduce_scatter | solution.py:373
  (487 shorter events, 667.8 us)
Async XLA Ops:
  7.2 304.9 %copy-start = (bf16[4,64]{1,0:T(4,128)(2,1)S(1)}, bf16[4,64]{1,0:T(4,128)(2,1)}, u32[]{:S(2)}) copy-start(bf16[4,64]{1,0:T(4,128)(2,1)} %param.20) | copy-start | bytes 1540
  7.2 321.0 %all-gather.12.cloned.1.call-start = ((), (), s32[]{:S(2)}) async-start(), calls=%async_computation.11 | async-start | bytes 19464192 | tf_op jit(solution)/shard_map/all_gather | solution.py:131
  8.0 401.4 %all-gather.14.cloned.1.call-start = ((), (), s32[]{:S(2)}) async-start(), calls=%async_computation.12 | async-start | bytes 19464192 | tf_op jit(solution)/shard_map/all_gather | solution.py:132
  8.7 422.8 %all-gather.16.cloned.1.call-start = ((), (), s32[]{:S(2)}) async-start(), calls=%async_computation.13 | async-start | bytes 14598144 | tf_op jit(solution)/shard_map/all_gather | solution.py:139
  9.5 437.0 %all-gather.20.cloned.1.call-start = ((), (), s32[]{:S(2)}) async-start(), calls=%async_computation.15 | async-start | bytes 4055040 | tf_op jit(solution)/shard_map/all_gather | solution.py:138
  10.0 493.5 %all-gather.24.cloned.1.call-start = ((), (), s32[]{:S(2)}) async-start(), calls=%async_computation.17 | async-start | bytes 4866048 | tf_op jit(solution)/shard_map/all_gather | solution.py:140
  12.0 301.0 %collective-permute-start.1 = (bf16[4,1,24,1536]{3,2,1,0:T(8,128)(2,1)}, bf16[4,1,24,1536]{3,2,1,0:T(8,128)(2,1)S(1)}, u32[]{:S(2)}, u32[]{:S(2)}) collective-permute-start(bf16[4,1,24,1536]{3,2,1,0:T(8,128)(2,1)} %get-tuple-element.312), channel_id=1, source_target_pairs={{1,0},{2,1},{3,2},{5,4},{6,5},{7,6},{9,8},{10,9},{11,10},{13,12},{... | collective-permute-start | bytes 884744 | tf_op jit(solution)/shard_map/ppermute | solution.py:17
  13.3 299.7 %collective-permute-start = (bf16[4,1,24,1536]{3,2,1,0:T(8,128)(2,1)}, bf16[4,1,24,1536]{3,2,1,0:T(8,128)(2,1)S(1)}, u32[]{:S(2)}, u32[]{:S(2)}) collective-permute-start(bf16[4,1,24,1536]{3,2,1,0:T(8,128)(2,1)} %get-tuple-element.311), channel_id=1, source_target_pairs={{0,1},{1,2},{2,3},{4,5},{5,6},{6,7},{8,9},{9,10},{10,11},{12,13},{... | collective-permute-start | bytes 884744 | tf_op jit(solution)/shard_map/ppermute | solution.py:16
  18.9 613.1 %all-gather.18.cloned.1.call-start = ((), (), s32[]{:S(2)}) async-start(), calls=%async_computation.14 | async-start | bytes 8847360 | tf_op jit(solution)/shard_map/all_gather | solution.py:201
  438.5 322.0 %all-gather.22.cloned.1.call-start = ((), (), s32[]{:S(2)}) async-start(), calls=%async_computation.16 | async-start | bytes 8847360 | tf_op jit(solution)/shard_map/all_gather | solution.py:200
  445.1 593.8 %all-reduce.5.cloned.1.call-start = ((), (), s32[]{:S(2)}) async-start(), calls=%async_computation.29 | async-start | bytes 3883008 | tf_op jit(solution)/shard_map/psum | solution.py:264
  959.0 204.8 %reduce-scatter.22.cloned.1.call-start = ((), (), s32[]{:S(2)}) async-start(), calls=%async_computation.19 | async-start | bytes 8847360 | tf_op jit(solution)/shard_map/reduce_scatter | solution.py:258
  976.4 313.6 %reduce-scatter.20.cloned.1.call-start = ((), (), s32[]{:S(2)}) async-start(), calls=%async_computation.18 | async-start | bytes 8847360 | tf_op jit(solution)/shard_map/reduce_scatter | solution.py:255
  993.7 585.2 %reduce-scatter.38.cloned.1.call-start = ((), (), s32[]{:S(2)}) async-start(), calls=%async_computation.27 | async-start | bytes 811008
  1415.6 195.4 %reduce-scatter.34.cloned.1.call-start = ((), (), s32[]{:S(2)}) async-start(), calls=%async_computation.25 | async-start | bytes 811008
  1424.0 293.7 %reduce-scatter.36.cloned.1.call-start = ((), (), s32[]{:S(2)}) async-start(), calls=%async_computation.26 | async-start | bytes 3244032
  1430.1 389.6 %reduce-scatter.40.cloned.1.call-start = ((), (), s32[]{:S(2)}) async-start(), calls=%async_computation.28 | async-start | bytes 1622016
  1438.3 509.7 %reduce-scatter.28.cloned.1.call-start = ((), (), s32[]{:S(2)}) async-start(), calls=%async_computation.22 | async-start | bytes 8110080 | tf_op jit(solution)/shard_map/reduce_scatter | solution.py:306
  1445.2 644.2 %reduce-scatter.32.cloned.1.call-start = ((), (), s32[]{:S(2)}) async-start(), calls=%async_computation.24 | async-start | bytes 9732096 | tf_op jit(solution)/shard_map/reduce_scatter | solution.py:313
  1467.5 888.8 %reduce-scatter.30.cloned.1.call-start = ((), (), s32[]{:S(2)}) async-start(), calls=%async_computation.23 | async-start | bytes 29196288 | tf_op jit(solution)/shard_map/reduce_scatter | solution.py:307
  1507.1 1204.4 %reduce-scatter.24.cloned.1.call-start = ((), (), s32[]{:S(2)}) async-start(), calls=%async_computation.20 | async-start | bytes 38928384 | tf_op jit(solution)/shard_map/reduce_scatter | solution.py:372
  1531.5 1535.2 %reduce-scatter.26.cloned.1.call-start = ((), (), s32[]{:S(2)}) async-start(), calls=%async_computation.21 | async-start | bytes 38928384 | tf_op jit(solution)/shard_map/reduce_scatter | solution.py:373
  1568.1 151.1 %collective-permute-start.3 = (bf16[4,1,24,1536]{3,2,1,0:T(8,128)(2,1)}, bf16[4,1,24,1536]{3,2,1,0:T(8,128)(2,1)S(1)}, u32[]{:S(2)}, u32[]{:S(2)}) collective-permute-start(bf16[4,1,24,1536]{3,2,1,0:T(8,128)(2,1)} %get-tuple-element.310), channel_id=1, source_target_pairs={{1,0},{2,1},{3,2},{5,4},{6,5},{7,6},{9,8},{10,9},{11,10},{13,12},{... | collective-permute-start | bytes 884744 | tf_op jit(solution)/shard_map/ppermute | solution.py:17
  1569.5 149.7 %collective-permute-start.2 = (bf16[4,1,24,1536]{3,2,1,0:T(8,128)(2,1)S(1)}, bf16[4,1,24,1536]{3,2,1,0:T(8,128)(2,1)S(1)}, u32[]{:S(2)}, u32[]{:S(2)}) collective-permute-start(bf16[4,1,24,1536]{3,2,1,0:T(8,128)(2,1)S(1)} %get-tuple-element.309), channel_id=1, source_target_pairs={{0,1},{1,2},{2,3},{4,5},{5,6},{6,7},{8,9},{9,10},{10,11},{12,13},{... | collective-permute-start | bytes 884744 | tf_op jit(solution)/shard_map/ppermute | solution.py:16
  (111 other events, 3243.3 us)
Sparse Core Ops, SparseCore 0:
  10.8 134.4 all-gather.11
  148.1 123.9 all-gather.13
  275.2 101.0 all-gather.15
  378.9 59.3 all-gather.19
  441.0 62.4 all-gather.23
  505.5 126.4 all-gather.17
  634.2 126.3 all-gather.21
  959.1 79.7 all-reduce.4
  1041.2 122.5 reduce-scatter.21
  1166.0 124.0 reduce-scatter.19
  1415.7 94.6 reduce-scatter.37
  1515.3 95.5 reduce-scatter.33
  1616.3 101.2 reduce-scatter.35
  1722.7 96.8 reduce-scatter.39
  1825.8 122.1 reduce-scatter.27
  1954.3 135.0 reduce-scatter.31
  2096.3 259.9 reduce-scatter.29
  2363.1 348.3 reduce-scatter.23
  2718.5 348.1 reduce-scatter.25
where the time goes:
time: 3080 us; the launch traced here: 3070 us
  waiting for transfers between devices  1990 us (65%)
  matrix products  400 us (13%)
  blocking collectives  325 us (11%)
  local copies, waits for them, and re-layouts  165 us (5%)
  other arithmetic  165 us (5%)
    reduce_scatter x1, waiting for transfers between devices, per_device(): lax.psum_scatter(grad_up_w, ('dp', 'band'), scatter_dimension=0, tiled=True)  355 us
    reduce_scatter x1, waiting for transfers between devices, per_device(): lax.psum_scatter(grad_down_w, ('dp', 'band'), scatter_dimension=0, tiled=...  355 us
    reduce_scatter x1, waiting for transfers between devices, per_device(): lax.psum_scatter(jnp.stack([grad_query_w, grad_key_w, grad_value_w]), ('d...  267 us
    unnamed x23, waiting for transfers between devices  232 us
    reduce_scatter x1, waiting for transfers between devices, per_device(): lax.psum_scatter(out_grad_w, ('dp', 'band'), scatter_dimension=0, tiled=T...  141 us
    reduce_scatter x1, waiting for transfers between devices, per_device(): lax.psum_scatter(grad_map_w, ('dp', 'band'), scatter_dimension=0, tiled=T...  127 us
    reduce_scatter x1, waiting for transfers between devices, per_device(): lax.psum_scatter(g_key[:, :pixel_count].astype(jnp.bfloat16), 'band', sca...  118 us
    all_gather x1, waiting for transfers between devices, per_device(): lax.all_gather(pixel_key, 'band', axis=1, tiled=True)  118 us
  transfers between devices with their start and end apart: 23, of which 14 were waited for; matrix products, arithmetic and copies ran while one was open for 14% of the time, Pallas kernels for 0%

commit v1 on v0

--- a/solution.py
+++ b/solution.py
@@ -390,6 +390,449 @@
     )
 
 
+PLANE = 4
+LINE = 4
+
+
+def swap(value, bit):
+    return lax.ppermute(value, "dp", [(i, i ^ bit) for i in range(2 * PLANE)])
+
+
+def rotate(value, step):
+    return lax.ppermute(value, "band", [(i, (i + step) % LINE) for i in range(LINE)])
+
+
+def pick(value, index, axis=0):
+    return lax.dynamic_index_in_dim(value, index, axis, keepdims=False)
+
+
+def put(buffer, value, index, axis=0):
+    return lax.dynamic_update_index_in_dim(buffer, value, index, axis)
+
+
+def spread_line(blocks, place):
+    result = jnp.zeros(blocks.shape, blocks.dtype)
+    result = put(result, pick(blocks, place), place)
+    for step in range(1, LINE):
+        moved = rotate(pick(blocks, (place + step) % LINE), step)
+        result = put(result, moved, (place - step) % LINE)
+    return result
+
+
+def gather_line(shard, place):
+    parts, rows, cols = shard.shape
+    result = jnp.zeros((parts, LINE, rows, cols), shard.dtype)
+    result = put(result, shard, place, 1)
+    for step in range(1, LINE):
+        result = put(result, rotate(shard, step), (place - step) % LINE, 1)
+    return result
+
+
+def gather_plane(block, plane):
+    rows, cols = block.shape
+    half = rows // 2
+    by_x, by_y = (swap(block, 2), swap(block, 4))
+    upper = swap(by_y[:half], 2)
+    lower = swap(by_x[half:], 4)
+    result = jnp.zeros((PLANE, rows, cols), block.dtype)
+    result = put(result, block, plane)
+    result = put(result, by_x, plane ^ 1)
+    result = put(result, by_y, plane ^ 2)
+    zero = jnp.int32(0)
+    result = lax.dynamic_update_slice(result, upper[None], (plane ^ 3, zero, zero))
+    result = lax.dynamic_update_slice(result, lower[None], (plane ^ 3, zero + half, zero))
+    return (result, (by_x, by_y))
+
+
+def gather_all(shards, plane, place):
+    results = []
+    line_done, plane_done = (None, None)
+    for shard in shards:
+        if line_done is not None:
+            shard, _ = lax.optimization_barrier((shard, line_done))
+        parts, rows, cols = shard.shape
+        line = gather_line(shard, place).reshape(parts * LINE * rows, cols)
+        line_done = line
+        if plane_done is not None:
+            line, _ = lax.optimization_barrier((line, plane_done))
+        full, plane_done = gather_plane(line, plane)
+        results.append(full.reshape(PLANE * parts * LINE * rows, cols))
+    return results
+
+
+def reduce_owner(piece, parts, plane, place):
+    low = jnp.bfloat16
+    far = [piece(plane ^ 3, half).astype(low) for half in range(2)]
+    via_x, via_y = (swap(far[0], 2), swap(far[1], 4))
+    out_x = [piece(plane ^ 1, 0).astype(low), None]
+    out_y = [None, piece(plane ^ 2, 1).astype(low)]
+    got_x, got_y = ([swap(out_x[0], 2), None], [None, swap(out_y[1], 4)])
+    out_x[1] = (piece(plane ^ 1, 1) + via_y.astype(jnp.float32)).astype(low)
+    out_y[0] = (piece(plane ^ 2, 0) + via_x.astype(jnp.float32)).astype(low)
+    got_x[1], got_y[0] = (swap(out_x[1], 2), swap(out_y[0], 4))
+    results = []
+    for half in range(2):
+        total = (
+            piece(plane, half)
+            + got_x[half].astype(jnp.float32)
+            + got_y[half].astype(jnp.float32)
+        )
+        rows, cols = total.shape
+        total = total.reshape(parts, LINE, rows // (parts * LINE), cols)
+        summed = pick(total, place, 1)
+        for step in range(1, LINE):
+            sent = pick(total, (place + step) % LINE, 1).astype(low)
+            summed = summed + rotate(sent, step).astype(jnp.float32)
+        results.append(summed)
+    return jnp.concatenate(results, axis=-1)
+
+
+def gather_small(value, plane, core, place):
+    cores = jnp.zeros((2,) + value.shape, value.dtype)
+    cores = put(put(cores, value, core), swap(value, 1), 1 - core)
+    line = jnp.zeros((2, LINE) + value.shape, value.dtype)
+    line = put(line, cores, place, 1)
+    for step in range(1, LINE):
+        line = put(line, rotate(cores, step), (place - step) % LINE, 1)
+    return gather_small_plane(line, plane)
+
+
+def gather_small_line(value, plane, place):
+    line = jnp.zeros((LINE,) + value.shape, value.dtype)
+    line = put(line, value, place)
+    for step in range(1, LINE):
+        line = put(line, rotate(value, step), (place - step) % LINE)
+    return gather_small_plane(line, plane)
+
+
+def gather_small_plane(line, plane):
+    by_x = swap(line, 2)
+    both = jnp.stack([line, by_x])
+    by_y = swap(both, 4)
+    full = jnp.zeros((PLANE,) + line.shape, line.dtype)
+    full = put(put(full, line, plane), by_x, plane ^ 1)
+    return put(put(full, by_y[0], plane ^ 2), by_y[1], plane ^ 3)
+
+
+def reduce_small(value, plane, place):
+    both = jnp.stack([pick(value, plane ^ 1), pick(value, plane ^ 3)])
+    by_x = swap(both, 2)
+    mine = pick(value, plane) + by_x[0]
+    other = pick(value, plane ^ 2) + by_x[1]
+    mine = mine + swap(other, 4)
+    summed = pick(mine, place)
+    for step in range(1, LINE):
+        summed = summed + rotate(pick(mine, (place + step) % LINE), step)
+    return summed
+
+
+def pair(value):
+    return jnp.stack([value, swap(value, 1)])
+
+
+def pair_sum(value):
+    return value + swap(value, 1)[::-1]
+
+
+def own_sum(own, partner):
+    return own + swap(partner.astype(jnp.bfloat16), 1).astype(jnp.float32)
+
+
+def core_half(value, axis, core, chips=PLANE):
+    shape = value.shape
+    split = shape[:axis] + (chips, 2, shape[axis] // (2 * chips)) + shape[axis + 1 :]
+    half = pick(value.reshape(split), core, axis + 1)
+    return half.reshape(shape[:axis] + (shape[axis] // 2,) + shape[axis + 1 :])
+
+
+def core_merge(own, other, axis, core):
+    shape = own.shape
+    split = shape[:axis] + (PLANE, 1, shape[axis] // PLANE) + shape[axis + 1 :]
+    own, other = (own.reshape(split), other.reshape(split))
+    first = jnp.where(core == 0, own, other)
+    second = jnp.where(core == 0, other, own)
+    merged = jnp.concatenate([first, second], axis=axis + 1)
+    return merged.reshape(shape[:axis] + (2 * shape[axis],) + shape[axis + 1 :])
+
+
+def paired_device(
+    latents,
+    clip_text,
+    embedding,
+    lengths,
+    conv_weight,
+    up_weight,
+    down_weight,
+    hidden_vecs,
+    vectors,
+    time_weight,
+    map_weight,
+    attn_in,
+    out_weight,
+    grad_out,
+):
+    lat_count, band_rows, columns, channels = latents.shape
+    height = band_rows * LINE
+    pixels = height * columns
+    text_len, clip_width = clip_text.shape[1:]
+    hidden_width = up_weight.shape[1]
+    time_rank = time_weight.shape[0]
+    share = up_weight.shape[0]
+    half_channels, half_hidden = (channels // 2, hidden_width // 2)
+    head_count = half_channels // HEAD_DIM
+    dp_index = lax.axis_index("dp")
+    place = lax.axis_index("band")
+    plane, core = (dp_index // 2, dp_index % 2)
+    f32, low = (jnp.float32, jnp.bfloat16)
+
+    latent = spread_line(latents, place).reshape(height, columns, channels)
+    small_cols = jnp.concatenate([conv_weight, vectors], axis=0)
+    small_all = gather_small(small_cols, plane, core, place)
+    small_all = small_all.reshape((-1,) + small_cols.shape).transpose(1, 0, 2)
+    small_all = small_all.reshape(small_cols.shape[0], channels).astype(f32)
+    taps, vecs = (small_all[:9], small_all[9:])
+    hidden_all = gather_small_line(hidden_vecs, plane, place)
+    hidden_all = hidden_all.reshape((-1,) + hidden_vecs.shape).transpose(1, 0, 2)
+    hidden_all = hidden_all.reshape(3, half_hidden).astype(f32)
+    time_all = gather_small(time_weight, plane, core, place)
+    time_all = time_all.reshape((-1,) + time_weight.shape).transpose(1, 0, 2)
+    time_all = time_all.reshape(time_rank, 2 * channels)
+
+    def with_partner(value, axis):
+        kept = core_half(value, axis, core)
+        got = swap(core_half(value, axis, 1 - core), 1)
+        both = jnp.zeros((2,) + kept.shape, kept.dtype)
+        return put(put(both, kept, core), got, 1 - core)
+
+    up_shard = with_partner(up_weight, 1)
+    attn_shard = with_partner(attn_in, 2).transpose(0, 2, 1, 3)
+    attn_shard = attn_shard.reshape(2, share, 3 * half_channels)
+    up_full, down_full, attn_full, map_full, out_full = gather_all(
+        (up_shard, down_weight[None], attn_shard, map_weight[None], out_weight[None]),
+        plane,
+        place,
+    )
+
+    clip_own = pick(clip_text, place).astype(f32)
+    words = pair(jax.nn.silu(clip_own).astype(low)).reshape(2 * text_len, clip_width)
+    words_half = core_half(words, 1, core)
+    lengths_two = pair(pick(lengths, place))
+    embed_own = pick(embedding, place)
+
+    framed = jnp.pad(latent, ((1, 1), (1, 1), (0, 0)))
+    conv_out = jnp.broadcast_to(vecs[0], latent.shape)
+    for offset in range(9):
+        row_shift, col_shift = (offset // 3, offset % 3)
+        conv_out = conv_out + taps[offset] * framed[
+            row_shift : row_shift + height, col_shift : col_shift + columns
+        ].astype(f32)
+    first_norm, first_inv = norm_parts(conv_out.reshape(pixels, channels))
+    first_in = pair(first_norm.astype(low)).reshape(2 * pixels, channels)
+    up_out = product(first_in, up_full) + hidden_all[0]
+    active = gelu_exact(up_out)
+    active_lat = active.reshape(2, pixels, half_hidden)
+    strength = jnp.sqrt(jnp.sum(active_lat * active_lat, axis=1))
+    strength_sum = pair_sum(jnp.sum(strength, axis=-1, keepdims=True))
+    grn_denom = strength_sum / hidden_width + 1e-06
+    grn_ratio = strength / grn_denom
+    gamma_vec = hidden_all[1]
+    grn_out = (
+        gamma_vec * (active_lat * grn_ratio[:, None]) + hidden_all[2] + active_lat
+    ).astype(low)
+    lowered = own_sum(product(grn_out[0], down_full), product(grn_out[1], down_full))
+    first_sum = latent.reshape(pixels, channels).astype(f32) + (lowered + vecs[1])
+    modulation = product(embed_own[None], time_all)[0]
+    scale_vec = modulation[:channels] + vecs[2]
+    shift_vec = modulation[channels:] + vecs[3]
+    second = first_sum * (1.0 + scale_vec) + shift_vec
+    second_norm, second_inv = norm_parts(second)
+    second_in = pair(second_norm.astype(low)).reshape(2 * pixels, channels)
+
+    mapped = pair_sum(product(words_half, map_full).reshape(2, text_len, channels))
+    mapped = (mapped + vecs[4]).astype(low).reshape(2 * text_len, channels)
+    bias = jnp.concatenate(
+        [
+            core_half(vecs[5], 0, core),
+            jnp.zeros((half_channels,), f32),
+            core_half(vecs[6], 0, core),
+        ]
+    )
+    pixel_qkv = (product(second_in, attn_full) + bias).astype(low)
+    text_kv = (
+        product(mapped, attn_full[:, half_channels:]) + bias[half_channels:]
+    ).astype(low)
+    pixel_qkv = pixel_qkv.reshape(2, pixels, 3, head_count, HEAD_DIM)
+    text_kv = text_kv.reshape(2, text_len, 2, head_count, HEAD_DIM)
+    query = pixel_qkv[:, :, 0]
+    key_rows = jnp.concatenate([pixel_qkv[:, :, 1], text_kv[:, :, 0]], axis=1)
+    value_rows = jnp.concatenate([pixel_qkv[:, :, 2], text_kv[:, :, 1]], axis=1)
+    key_places = jnp.arange(pixels + text_len, dtype=jnp.int32)
+    valid_keys = key_places[None] < pixels + lengths_two[:, None]
+    mixed, log_totals = lax.map(attend_one, (query, key_rows, value_rows, valid_keys))
+    mixed = mixed.reshape(2, pixels, half_channels)
+    attended = own_sum(product(mixed[0], out_full), product(mixed[1], out_full))
+    layer_own = (second + (attended + vecs[7])).astype(low)
+    layer_out = spread_line(layer_own.reshape(latents.shape), place)
+
+    grad_own = spread_line(grad_out, place).reshape(pixels, channels)
+    grad_two = pair(grad_own)
+    g_mixed = product_nt(grad_two.reshape(2 * pixels, channels), out_full).astype(low)
+    g_mixed = g_mixed.reshape(2, pixels, head_count, HEAD_DIM)
+
+    def owner_sums(left, right, parts):
+        block = left.shape[1] // PLANE
+        half = right.shape[1] // 2
+
+        def piece(chip, which):
+            cut = lax.dynamic_slice_in_dim(left, chip * block, block, 1)
+            return product_tn(cut, right[:, which * half : (which + 1) * half])
+
+        return reduce_owner(piece, parts, plane, place)
+
+    out_grad = owner_sums(
+        mixed.reshape(2 * pixels, half_channels), grad_two.reshape(2 * pixels, channels), 1
+    )[0]
+    g_query, g_key, g_value = lax.map(
+        attend_back, (query, key_rows, value_rows, valid_keys, log_totals, g_mixed)
+    )
+    g_key, g_value = (g_key.astype(low), g_value.astype(low))
+    g_pixel = jnp.stack([g_query, g_key[:, :pixels], g_value[:, :pixels]], axis=2)
+    g_pixel = g_pixel.reshape(2, pixels, 3 * half_channels)
+    g_text = jnp.stack([g_key[:, pixels:], g_value[:, pixels:]], axis=2)
+    g_text = g_text.reshape(2 * text_len, 2 * half_channels)
+    g_second_in = own_sum(product_nt(g_pixel[0], attn_full), product_nt(g_pixel[1], attn_full))
+    g_mapped = pair_sum(
+        product_nt(g_text, attn_full[:, half_channels:]).reshape(2, text_len, channels)
+    )
+    g_mapped = g_mapped.astype(low).reshape(2 * text_len, channels)
+    padded_text = jnp.concatenate([jnp.zeros((2 * text_len, half_channels), low), g_text], axis=1)
+    attn_grad = owner_sums(
+        jnp.concatenate([second_in, mapped], axis=0),
+        jnp.concatenate([g_pixel.reshape(2 * pixels, 3 * half_channels), padded_text], axis=0),
+        2,
+    )
+    map_grad = owner_sums(words_half, g_mapped, 1)[0]
+    g_words = product_nt(g_mapped, map_full).reshape(2, text_len, clip_width // 2)
+    g_words = core_merge(g_words[0], swap(g_words[1], 1), 1, core)
+    sigmoid_text = jax.nn.sigmoid(clip_own)
+    text_own = (g_words * (sigmoid_text * (1.0 + clip_own * (1.0 - sigmoid_text)))).astype(low)
+    text_own = text_own.reshape(text_len, LINE, clip_width // LINE).transpose(1, 0, 2)
+    text_grad = spread_line(text_own, place)
+
+    grad_float = grad_own.astype(f32)
+    g_second = grad_float + norm_back(g_second_in, second_norm, second_inv)
+    g_scale = jnp.sum(g_second * first_sum, axis=0)
+    g_shift = jnp.sum(g_second, axis=0)
+    g_modulation = jnp.concatenate([g_scale, g_shift])
+    time_part = embed_own.astype(f32)[:, None] * g_modulation[None]
+    g_first = g_second * (1.0 + scale_vec)
+    g_down_own = g_first.astype(low)
+    g_down = pair(g_down_own).reshape(2 * pixels, channels)
+    down_grad = owner_sums(grn_out.reshape(2 * pixels, half_hidden), g_down, 1)[0]
+    g_grn = product_nt(g_down, down_full).reshape(2, pixels, half_hidden)
+    g_grn_active = jnp.sum(g_grn * active_lat, axis=1)
+    grad_gamma = jnp.sum(g_grn_active * grn_ratio, axis=0)
+    grad_beta = jnp.sum(g_grn, axis=(0, 1))
+    g_ratio = g_grn_active * gamma_vec
+    ratio_sum = pair_sum(jnp.sum(g_ratio * strength, axis=-1, keepdims=True))
+    g_strength = g_ratio / grn_denom - ratio_sum / (hidden_width * grn_denom * grn_denom)
+    g_active = (
+        g_grn * (1.0 + gamma_vec * grn_ratio[:, None])
+        + active_lat * (g_strength / strength)[:, None]
+    )
+    gelu_value, gelu_pull = jax.vjp(gelu_exact, up_out)
+    g_up = gelu_pull(g_active.reshape(2 * pixels, half_hidden))[0].astype(low)
+    g_first_in = own_sum(
+        product_nt(g_up[:pixels], up_full), product_nt(g_up[pixels:], up_full)
+    )
+    g_conv = norm_back(g_first_in, first_norm, first_inv).astype(low).reshape(latent.shape)
+    up_grad = owner_sums(first_in, g_up, 2)
+    g_framed = jnp.pad(g_conv, ((1, 1), (1, 1), (0, 0)))
+    g_conv_f = g_conv.astype(f32)
+    back_sum = g_first.reshape(latent.shape)
+    tap_grads = []
+    for offset in range(9):
+        row_shift, col_shift = (offset // 3, offset % 3)
+        window = framed[
+            row_shift : row_shift + height, col_shift : col_shift + columns
+        ].astype(f32)
+        tap_grads.append(jnp.sum(g_conv_f * window, axis=(0, 1)))
+        back_sum = back_sum + taps[offset] * g_framed[
+            2 - row_shift : 2 - row_shift + height, 2 - col_shift : 2 - col_shift + columns
+        ].astype(f32)
+    latent_grad = spread_line(back_sum.astype(low).reshape(latents.shape), place)
+
+    up_grad = core_merge(
+        pick(up_grad, core), swap(pick(up_grad, 1 - core), 1), 1, core
+    )
+    attn_grad = attn_grad.reshape(2, share, 3, half_channels)
+    attn_grad = core_merge(
+        pick(attn_grad, core), swap(pick(attn_grad, 1 - core), 1), 2, core
+    ).transpose(1, 0, 2)
+
+    own_zero = jnp.zeros((half_channels,), f32)
+    vec_parts = jnp.stack(
+        [
+            jnp.sum(g_conv_f, axis=(0, 1)),
+            column_sums(g_down_own),
+            g_scale,
+            g_shift,
+            column_sums(g_mapped[:text_len]),
+            core_merge(column_sums(g_pixel.reshape(2 * pixels, -1)[:, :half_channels]), own_zero, 0, core),
+            core_merge(
+                column_sums(g_pixel.reshape(2 * pixels, -1)[:, 2 * half_channels :])
+                + column_sums(g_text[:, half_channels:]),
+                own_zero,
+                0,
+                core,
+            ),
+            jnp.sum(grad_float, axis=0),
+        ]
+    )
+    col_parts = jnp.concatenate([jnp.stack(tap_grads), vec_parts])
+    col_parts = col_parts.reshape(col_parts.shape[0], PLANE, 2, LINE, -1).transpose(1, 2, 3, 0, 4)
+    col_parts = col_parts.reshape(PLANE, 2, LINE, -1)
+    time_part = time_part.reshape(time_rank, PLANE, 2, LINE, -1).transpose(1, 2, 3, 0, 4)
+    time_part = time_part.reshape(PLANE, 2, LINE, -1)
+    core_parts = jnp.concatenate([col_parts, time_part], axis=-1)
+    core_sum = pick(core_parts, core, 1) + swap(pick(core_parts, 1 - core, 1), 1)
+    hidden_parts = jnp.stack([column_sums(g_up), grad_gamma, grad_beta])
+    hidden_parts = hidden_parts.reshape(3, PLANE, LINE, -1).transpose(1, 2, 0, 3)
+    hidden_parts = hidden_parts.reshape(PLANE, LINE, -1)
+    small_sum = reduce_small(
+        jnp.concatenate([core_sum, hidden_parts], axis=-1), plane, place
+    )
+    col_size, time_size = (17 * (channels // 32), time_rank * (channels // 16))
+    col_grads = small_sum[:col_size].reshape(17, -1)
+    time_grad = small_sum[col_size : col_size + time_size].reshape(time_rank, -1)
+    hidden_grad = small_sum[col_size + time_size :].reshape(3, -1)
+    return (
+        layer_out,
+        latent_grad,
+        text_grad,
+        col_grads[:9],
+        up_grad,
+        down_grad,
+        hidden_grad,
+        col_grads[9:],
+        time_grad,
+        map_grad,
+        attn_grad,
+        out_grad,
+    )
+
+
+def choose(latents, *rest):
+    shape = {axis: lax.axis_size(axis) for axis in ("dp", "band")}
+    fits = (
+        shape["dp"] == 2 * PLANE
+        and shape["band"] == LINE
+        and latents.shape[0] == LINE
+        and latents.shape[3] % (2 * PLANE * HEAD_DIM) == 0
+    )
+    return (paired_device if fits else per_device)(latents, *rest)
+
+
 def solution(mesh):
     placed = (
         P("dp", "band", None, None),
@@ -408,7 +851,7 @@
         P("dp", "band", None, None),
     )
     return jax.shard_map(
-        per_device,
+        choose,
         mesh=mesh,
         in_specs=placed,
         out_specs=(

time: 3080 us -> 1660 us (0.54)
  waiting for transfers between devices: 1990 us -> 552 us
  blocking collectives: 325 us -> 0 us
  starting transfers between devices: 14.5 us -> 213 us
  local copies, waits for them, and re-layouts: 165 us -> 268 us
  other arithmetic: 165 us -> 209 us
    reduce_scatter x7 -> x0, waiting for transfers between devices: 1480 us -> none  [the longest x1 355 us: per_device(): lax.psum_scatter(grad_up_w, ('dp', 'band'), scatter_dimension=0, tiled=True)]
    ppermute x4 -> x152, waiting for transfers between devices: 0.01 us -> 552 us  [the longest x72 284 us: rotate(): lax.ppermute(value, 'band', [(i, (i + step) % LINE) for i in range(LINE)])]
    all_gather x4 -> x0, blocking collectives: 290 us -> none  [the longest x1 84.4 us: per_device(): lax.all_gather(attn_shards[0], ('dp', 'band'), axis=1, tiled=True)]
    all_gather x7 -> x0, waiting for transfers between devices: 251 us -> none  [the longest x1 118 us: per_device(): lax.all_gather(pixel_key, 'band', axis=1, tiled=True)]
    unnamed x23 -> x0, waiting for transfers between devices: 232 us -> none
    ppermute x4 -> x152, starting transfers between devices: 12.9 us -> 213 us  [the longest x72 153 us: rotate(): lax.ppermute(value, 'band', [(i, (i + step) % LINE) for i in range(LINE)])]
    dynamic_update_slice x0 -> x94, local copies, waits for them, and re-layouts: none -> 64.2 us  [the longest x84 59.7 us: put(): return lax.dynamic_update_index_in_dim(buffer, value, index, axis)]
    psum x2 -> x0, blocking collectives: 35.1 us -> none  [the longest x1 18.6 us: per_device(): lax.psum(jnp.sum(g_grn * gamma_vec * active_lat, axis=1).astype(jnp.bfloa...]
  transfers between devices with their start and end apart: 23 -> 152, of which waited for: 14 -> 62; matrix products, arithmetic and copies ran while one was open for 14% -> 32% of each run, Pallas kernels for 0% -> 0%
where the time goes in v1:
time: 1660 us; the launch traced here: 1640 us
  waiting for transfers between devices  552 us (33%)
  matrix products  398 us (24%)
  local copies, waits for them, and re-layouts  268 us (16%)
  starting transfers between devices  213 us (13%)
  other arithmetic  209 us (13%)
    ppermute x72, waiting for transfers between devices, rotate(): lax.ppermute(value, 'band', [(i, (i + step) % LINE) for i in range(LINE)])  284 us
    ppermute x80, waiting for transfers between devices, swap(): return lax.ppermute(value, 'dp', [(i, i ^ bit) for i in range(2 * PLANE)])  268 us
    ppermute x72, starting transfers between devices, rotate(): lax.ppermute(value, 'band', [(i, (i + step) % LINE) for i in range(LINE)])  153 us
    dot_general x40, matrix products, product_tn(): lax.dot_general(left_op, right_op, (((0,), (0,)), ((), ())), preferred_el...  108 us
    dot_general x9, matrix products, product(): return jnp.dot(left_op, right_op, preferred_element_type=jnp.float32)  87.9 us
    dot_general x8, matrix products, product_nt(): lax.dot_general(left_op, right_op, (((1,), (1,)), ((), ())), preferred_el...  60.8 us
    ppermute x80, starting transfers between devices, swap(): return lax.ppermute(value, 'dp', [(i, i ^ bit) for i in range(2 * PLANE)])  60.2 us
    dynamic_update_slice x84, local copies, waits for them, and re-layouts, put(): return lax.dynamic_update_index_in_dim(buffer, value, index, axis)  59.7 us
  transfers between devices with their start and end apart: 152, of which 62 were waited for; matrix products, arithmetic and copies ran while one was open for 32% of the time, Pallas kernels for 0%

profile of v1, /device:TPU:0, one launch (start us, length us, event | category | flops | bytes accessed | tf_op | source)
XLA Modules:
  0.0 1644.6 jit_solution(14694530114290323679)
XLA Ops:
  59.5 16.7 %collective-permute-done.33 = bf16[2,64,96]{2,1,0:T(8,128)(2,1)S(1)} collective-permute-done((bf16[2,64,96]{2,1,0:T(8,128)(2,1)S(1)}, bf16[2,64,96]{2,1,0:T(8,128)(2,1)S(1)}, u32[]{:S(2)}, u32[]{:S(2)}) %collective-permute-start.33) | collective-permute-done | bytes 24608 | tf_op jit(solution)/shard_map/ppermute | solution.py:402
  177.9 22.4 %collective-permute-done.17 = bf16[2,48,3072]{2,1,0:T(8,128)(2,1)} collective-permute-done((bf16[2,48,3072]{2,1,0:T(8,128)(2,1)S(1)}, bf16[2,48,3072]{2,1,0:T(8,128)(2,1)}, u32[]{:S(2)}, u32[]{:S(2)}) %collective-permute-start.17) | collective-permute-done | bytes 589856 | tf_op jit(solution)/shard_map/ppermute | solution.py:402
  234.9 21.5 %collective-permute-done.25 = bf16[1,192,1536]{2,1,0:T(8,128)(2,1)S(1)} collective-permute-done((bf16[1,192,1536]{2,1,0:T(8,128)(2,1)S(1)}, bf16[1,192,1536]{2,1,0:T(8,128)(2,1)S(1)}, u32[]{:S(2)}, u32[]{:S(2)}) %collective-permute-start.25) | collective-permute-done | bytes 589856 | tf_op jit(solution)/shard_map/ppermute | solution.py:402
  281.0 19.9 %collective-permute-done.41 = bf16[2,48,2304]{2,1,0:T(8,128)(2,1)S(1)} collective-permute-done((bf16[2,48,2304]{2,1,0:T(8,128)(2,1)S(1)}, bf16[2,48,2304]{2,1,0:T(8,128)(2,1)S(1)}, u32[]{:S(2)}, u32[]{:S(2)}) %collective-permute-start.41) | collective-permute-done | bytes 442400 | tf_op jit(solution)/shard_map/ppermute | solution.py:402
  376.5 55.6 %collective-permute-done.21 = bf16[192,3072]{1,0:T(8,128)(2,1)S(1)} collective-permute-done((bf16[192,3072]{1,0:T(8,128)(2,1)S(1)}, bf16[192,3072]{1,0:T(8,128)(2,1)S(1)}, u32[]{:S(2)}, u32[]{:S(2)}) %collective-permute-start.21) | collective-permute-done | bytes 1179680 | tf_op jit(solution)/shard_map/ppermute | solution.py:398
  433.5 43.3 %multiply_multiply_fusion.5 = (f32[1152,3072]{1,0:T(8,128)}, f32[1152,3072]{1,0:T(8,128)}, f32[1152,3072]{1,0:T(8,128)}) fusion(f32[3072]{0:T(1024)S(1)} %copy-done.128, bf16[1152,1536]{1,0:T(8,128)(2,1)S(1)} %bitcast.796, bf16[1536,3072]{1,0:T(8,128)(2,1)S(1)} %bitcast.749), kind=kOutput, calls=%fused_computation.94 | convolution fusion | flops 11101667328 | bytes 55455744 | tf_op jit(solution)/shard_map/dot_general | solution.py:23
  520.9 51.7 %collective-permute-done.29 = bf16[384,1536]{1,0:T(8,128)(2,1)S(1)} collective-permute-done((bf16[384,1536]{1,0:T(8,128)(2,1)S(1)}, bf16[384,1536]{1,0:T(8,128)(2,1)S(1)}, u32[]{:S(2)}, u32[]{:S(2)}) %collective-permute-start.29) | collective-permute-done | bytes 1179680 | tf_op jit(solution)/shard_map/ppermute | solution.py:398
  600.6 21.1 %collective-permute-done.53 = bf16[80,1536]{1,0:T(8,128)(2,1)S(1)} collective-permute-done((bf16[80,1536]{1,0:T(8,128)(2,1)S(1)}, bf16[80,1536]{1,0:T(8,128)(2,1)S(1)}, u32[]{:S(2)}, u32[]{:S(2)}) %collective-permute-start.53) | collective-permute-done | bytes 245792 | tf_op jit(solution)/shard_map/ppermute | solution.py:398
  735.9 73.4 %while.26 = (s32[]{:T(128)}, bf16[2,576,12,64]{1,3,2,0:T(8,128)(2,1)}, f32[2,12,576,1]{2,1,3,0:T(8,128)S(1)}, bf16[2,653,12,64]{1,3,2,0:T(8,128)(2,1)}, pred[2,6...) while((s32[]{:T(128)}, ...), condition=%wide.region_9.10_spmd, body=%wide.region_6.9_spmd.sunk | while | flops 1210063104 | bytes 60852880 | solution.py:671
  796.0 13.3 fusion.465
  826.4 118.8 %while.27 = (s32[]{:T(128)}, bf16[2,576,12,64]{1,3,2,0:T(8,128)(2,1)}, bf16[2,653,12,64]{1,3,2,0:T(8,128)(2,1)}, bf16[2,653,12,64]{1,3,2,0:T(8,128)(2,1)}, bf16[...) while((s32[]{:T(128)}, ...), condition=%wide.region_12.13_spmd, body=%wide.region_10.12_spmd.sunk | while | flops 2957745408 | bytes 176576112 | solution.py:695
  837.8 14.2 multiply_reduce_fusion.11
  852.1 14.4 multiply_convert_fusion.7
  897.0 14.2 multiply_reduce_fusion.11
  911.2 14.4 multiply_convert_fusion.7
  1147.6 16.0 collective-permute-done.129
  1201.2 17.6 %collective-permute-done.137 = bf16[2,48,1152]{2,1,0:T(8,128)(2,1)S(1)} collective-permute-done((bf16[2,48,1152]{2,1,0:T(8,128)(2,1)}, bf16[2,48,1152]{2,1,0:T(8,128)(2,1)S(1)}, u32[]{:S(2)}, u32[]{:S(2)}) %collective-permute-start.137) | collective-permute-done | bytes 221216 | tf_op jit(solution)/shard_map/ppermute | solution.py:402
  1270.3 19.6 %fusion.404 = (f32[3072]{0:T(1024)S(1)}, f32[2,3072]{1,0:T(2,128)S(1)}, f32[2,576,3072]{2,1,0:T(8,128)}) fusion(f32[2,576,3072]{2,1,0:T(8,128)} %bitcast.732, bf16[3072,1536,1]{1,0,2:T(8,128)(2,1)} %bitcast.757, bf16[1,576,1536]{2,1,0:T(8,128)(2,1)} %bitcast.176, bf16[1,576,1536]{2,1,0:T(8,128)(2,1)S(1)} %bitcast.780), kind=kOutput, calls=%fused_computation.728 | convolution fusion | flops 10884013056 | bytes 41324544 | tf_op jit(solution)/shard_map/dot_general | solution.py:33
  1412.0 18.7 %collective-permute-done.77 = bf16[6,24,1536]{2,1,0:T(8,128)(2,1)S(1)} collective-permute-done((bf16[6,24,1536]{2,1,0:T(8,128)(2,1)S(1)}, bf16[6,24,1536]{2,1,0:T(8,128)(2,1)S(1)}, u32[]{:S(2)}, u32[]{:S(2)}) %collective-permute-start.77) | collective-permute-done | bytes 442400 | tf_op jit(solution)/shard_map/ppermute | solution.py:402
  1451.3 22.4 %collective-permute-done.110 = bf16[768,768]{1,0:T(8,128)(2,1)S(1)} collective-permute-done((bf16[768,768]{1,0:T(8,128)(2,1)S(1)}, bf16[768,768]{1,0:T(8,128)(2,1)S(1)}, u32[]{:S(2)}, u32[]{:S(2)}) %collective-permute-start.110) | collective-permute-done | bytes 1179680 | tf_op jit(solution)/shard_map/ppermute | solution.py:398
  1478.6 20.3 %collective-permute-done.97 = bf16[384,1536]{1,0:T(8,128)(2,1)S(1)} collective-permute-done((bf16[384,1536]{1,0:T(8,128)(2,1)S(1)}, bf16[384,1536]{1,0:T(8,128)(2,1)S(1)}, u32[]{:S(2)}, u32[]{:S(2)}) %collective-permute-start.97) | collective-permute-done | bytes 1179680 | tf_op jit(solution)/shard_map/ppermute | solution.py:398
  1502.4 26.2 %collective-permute-done.85 = f32[2,4,7536]{2,1,0:T(4,128)S(1)} collective-permute-done((f32[2,4,7536]{2,1,0:T(4,128)S(1)}, f32[2,4,7536]{2,1,0:T(4,128)S(1)}, u32[]{:S(2)}, u32[]{:S(2)}) %collective-permute-start.85) | collective-permute-done | bytes 241184 | tf_op jit(solution)/shard_map/ppermute | solution.py:398
  1539.4 14.8 collective-permute-done.87
  1585.0 17.3 %collective-permute-done.94 = bf16[2,48,1536]{2,1,0:T(8,128)(2,1)S(1)} collective-permute-done((bf16[2,48,1536]{2,1,0:T(8,128)(2,1)}, bf16[2,48,1536]{2,1,0:T(8,128)(2,1)S(1)}, u32[]{:S(2)}, u32[]{:S(2)}) %collective-permute-start.94) | collective-permute-done | bytes 294944 | tf_op jit(solution)/shard_map/ppermute | solution.py:402
  (1140 shorter events, 1143.8 us)
Async XLA Ops:
  33.2 87.4 %collective-permute-start.15 = (bf16[48,3072]{1,0:T(8,128)(2,1)}, bf16[48,3072]{1,0:T(8,128)(2,1)}, u32[]{:S(2)}, u32[]{:S(2)}) collective-permute-start(bf16[48,3072]{1,0:T(8,128)(2,1)} %bitcast.292), channel_id=1, source_target_pairs={{0,4},{4,0},{8,12},{12,8},{16,20},{20,16},{24,28},{28,24},{1,5},{5... | collective-permute-start | bytes 884744 | tf_op jit(solution)/shard_map/ppermute | solution.py:398
  43.4 94.0 %collective-permute-start = (bf16[6,24,1536]{2,1,0:T(8,128)(2,1)}, bf16[6,24,1536]{2,1,0:T(8,128)(2,1)}, u32[]{:S(2)}, u32[]{:S(2)}) collective-permute-start(bf16[6,24,1536]{2,1,0:T(8,128)(2,1)} %get-tuple-element.361), channel_id=1, source_target_pairs={{0,1},{1,2},{2,3},{3,0},{4,5},{5,6},{6,7},{7,4},{8,9},{9,10},{10,1... | collective-permute-start | bytes 1327112 | tf_op jit(solution)/shard_map/ppermute | solution.py:402
  43.5 98.5 %collective-permute-start.1 = (bf16[6,24,1536]{2,1,0:T(8,128)(2,1)}, bf16[6,24,1536]{2,1,0:T(8,128)(2,1)}, u32[]{:S(2)}, u32[]{:S(2)}) collective-permute-start(bf16[6,24,1536]{2,1,0:T(8,128)(2,1)} %get-tuple-element.363), channel_id=1, source_target_pairs={{0,2},{1,3},{2,0},{3,1},{4,6},{5,7},{6,4},{7,5},{8,10},{9,11},{10,... | collective-permute-start | bytes 1327112 | tf_op jit(solution)/shard_map/ppermute | solution.py:402
  47.9 96.1 %collective-permute-start.2 = (bf16[6,24,1536]{2,1,0:T(8,128)(2,1)}, bf16[6,24,1536]{2,1,0:T(8,128)(2,1)}, u32[]{:S(2)}, u32[]{:S(2)}) collective-permute-start(bf16[6,24,1536]{2,1,0:T(8,128)(2,1)} %get-tuple-element.360), channel_id=1, source_target_pairs={{0,3},{1,0},{2,1},{3,2},{4,7},{5,4},{6,5},{7,6},{8,11},{9,8},{10,9... | collective-permute-start | bytes 1327112 | tf_op jit(solution)/shard_map/ppermute | solution.py:402
  170.7 183.0 %collective-permute-start.14 = (bf16[576,1536]{1,0:T(8,128)(2,1)}, bf16[576,1536]{1,0:T(8,128)(2,1)}, u32[]{:S(2)}, u32[]{:S(2)}) collective-permute-start(bf16[576,1536]{1,0:T(8,128)(2,1)} %get-tuple-element.315), channel_id=1, source_target_pairs={{0,4},{4,0},{8,12},{12,8},{16,20},{20,16},{24,28},{28,24},{1,5},{5... | collective-permute-start | bytes 5308424 | tf_op jit(solution)/shard_map/ppermute | solution.py:398
  172.2 185.3 %collective-permute-start.71 = (bf16[576,1536]{1,0:T(8,128)(2,1)S(1)}, bf16[576,1536]{1,0:T(8,128)(2,1)}, u32[]{:S(2)}, u32[]{:S(2)}) collective-permute-start(bf16[576,1536]{1,0:T(8,128)(2,1)S(1)} %bitcast.739), channel_id=1, source_target_pairs={{0,4},{4,0},{8,12},{12,8},{16,20},{20,16},{24,28},{28,24},{1,5},{5... | collective-permute-start | bytes 5308424 | tf_op jit(solution)/shard_map/ppermute | solution.py:398
  204.2 156.9 %collective-permute-start.19 = (bf16[384,3072]{1,0:T(8,128)(2,1)}, bf16[384,3072]{1,0:T(8,128)(2,1)}, u32[]{:S(2)}, u32[]{:S(2)}) collective-permute-start(bf16[384,3072]{1,0:T(8,128)(2,1)} %bitcast.59), channel_id=1, source_target_pairs={{0,8},{4,12},{8,0},{12,4},{16,24},{20,28},{24,16},{28,20},{1,9},{5... | collective-permute-start | bytes 7077896 | tf_op jit(solution)/shard_map/ppermute | solution.py:398
  256.4 104.7 %collective-permute-start.20 = (bf16[384,3072]{1,0:T(8,128)(2,1)}, bf16[384,3072]{1,0:T(8,128)(2,1)S(1)}, u32[]{:S(2)}, u32[]{:S(2)}) collective-permute-start(bf16[384,3072]{1,0:T(8,128)(2,1)} %bitcast.59), channel_id=1, source_target_pairs={{0,16},{4,20},{8,24},{12,28},{16,0},{20,4},{24,8},{28,12},{1,17},{... | collective-permute-start | bytes 7077896 | tf_op jit(solution)/shard_map/ppermute | solution.py:398
  361.1 145.5 %collective-permute-start.27 = (bf16[768,1536]{1,0:T(8,128)(2,1)}, bf16[768,1536]{1,0:T(8,128)(2,1)}, u32[]{:S(2)}, u32[]{:S(2)}) collective-permute-start(bf16[768,1536]{1,0:T(8,128)(2,1)} %bitcast.75), channel_id=1, source_target_pairs={{0,8},{4,12},{8,0},{12,4},{16,24},{20,28},{24,16},{28,20},{1,9},{5... | collective-permute-start | bytes 7077896 | tf_op jit(solution)/shard_map/ppermute | solution.py:398
  362.6 144.0 %collective-permute-start.28 = (bf16[768,1536]{1,0:T(8,128)(2,1)}, bf16[768,1536]{1,0:T(8,128)(2,1)}, u32[]{:S(2)}, u32[]{:S(2)}) collective-permute-start(bf16[768,1536]{1,0:T(8,128)(2,1)} %bitcast.75), channel_id=1, source_target_pairs={{0,16},{4,20},{8,24},{12,28},{16,0},{20,4},{24,8},{28,12},{1,17},{... | collective-permute-start | bytes 7077896 | tf_op jit(solution)/shard_map/ppermute | solution.py:398
  362.7 69.5 %collective-permute-start.21 = (bf16[192,3072]{1,0:T(8,128)(2,1)S(1)}, bf16[192,3072]{1,0:T(8,128)(2,1)S(1)}, u32[]{:S(2)}, u32[]{:S(2)}) collective-permute-start(bf16[192,3072]{1,0:T(8,128)(2,1)S(1)} %slice.528), channel_id=1, source_target_pairs={{0,8},{4,12},{8,0},{12,4},{16,24},{20,28},{24,16},{28,20},{1,9},{5... | collective-permute-start | bytes 3538952 | tf_op jit(solution)/shard_map/ppermute | solution.py:398
  364.6 68.7 %collective-permute-start.22 = (bf16[192,3072]{1,0:T(8,128)(2,1)S(1)}, bf16[192,3072]{1,0:T(8,128)(2,1)S(1)}, u32[]{:S(2)}, u32[]{:S(2)}) collective-permute-start(bf16[192,3072]{1,0:T(8,128)(2,1)S(1)} %slice.529), channel_id=1, source_target_pairs={{0,16},{4,20},{8,24},{12,28},{16,0},{20,4},{24,8},{28,12},{1,17},{... | collective-permute-start | bytes 3538952 | tf_op jit(solution)/shard_map/ppermute | solution.py:398
  506.6 76.7 %collective-permute-start.43 = (bf16[384,2304]{1,0:T(8,128)(2,1)S(1)}, bf16[384,2304]{1,0:T(8,128)(2,1)S(1)}, u32[]{:S(2)}, u32[]{:S(2)}) collective-permute-start(bf16[384,2304]{1,0:T(8,128)(2,1)S(1)} %bitcast.776), channel_id=1, source_target_pairs={{0,8},{4,12},{8,0},{12,4},{16,24},{20,28},{24,16},{28,20},{1,9},{5... | collective-permute-start | bytes 5308424 | tf_op jit(solution)/shard_map/ppermute | solution.py:398
  507.2 76.1 %collective-permute-start.44 = (bf16[384,2304]{1,0:T(8,128)(2,1)S(1)}, bf16[384,2304]{1,0:T(8,128)(2,1)S(1)}, u32[]{:S(2)}, u32[]{:S(2)}) collective-permute-start(bf16[384,2304]{1,0:T(8,128)(2,1)S(1)} %bitcast.777), channel_id=1, source_target_pairs={{0,16},{4,20},{8,24},{12,28},{16,0},{20,4},{24,8},{28,12},{1,17},{... | collective-permute-start | bytes 5308424 | tf_op jit(solution)/shard_map/ppermute | solution.py:398
  508.8 63.8 %collective-permute-start.29 = (bf16[384,1536]{1,0:T(8,128)(2,1)S(1)}, bf16[384,1536]{1,0:T(8,128)(2,1)S(1)}, u32[]{:S(2)}, u32[]{:S(2)}) collective-permute-start(bf16[384,1536]{1,0:T(8,128)(2,1)S(1)} %slice.533), channel_id=1, source_target_pairs={{0,8},{4,12},{8,0},{12,4},{16,24},{20,28},{24,16},{28,20},{1,9},{5... | collective-permute-start | bytes 3538952 | tf_op jit(solution)/shard_map/ppermute | solution.py:398
  1057.4 73.8 %collective-permute-start.72 = (bf16[576,1536]{1,0:T(8,128)(2,1)}, bf16[576,1536]{1,0:T(8,128)(2,1)}, u32[]{:S(2)}, u32[]{:S(2)}) collective-permute-start(bf16[576,1536]{1,0:T(8,128)(2,1)} %convolution_convert_fusion.2), channel_id=1, source_target_pairs={{0,4},{4,0},{8,12},{12,8},{16,20},{20,16},{24,28},{28,24},{1,5},{5... | collective-permute-start | bytes 5308424 | tf_op jit(solution)/shard_map/ppermute | solution.py:398
  1261.9 183.3 %collective-permute-start.103 = (bf16[768,768]{1,0:T(8,128)(2,1)}, bf16[768,768]{1,0:T(8,128)(2,1)}, u32[]{:S(2)}, u32[]{:S(2)}) collective-permute-start(bf16[768,768]{1,0:T(8,128)(2,1)} %fusion.165), channel_id=1, source_target_pairs={{0,8},{4,12},{8,0},{12,4},{16,24},{20,28},{24,16},{28,20},{1,9},{5... | collective-permute-start | bytes 3538952 | tf_op jit(solution)/shard_map/ppermute | solution.py:398
  1265.1 79.0 %collective-permute-start.104 = (bf16[768,768]{1,0:T(8,128)(2,1)}, bf16[768,768]{1,0:T(8,128)(2,1)}, u32[]{:S(2)}, u32[]{:S(2)}) collective-permute-start(bf16[768,768]{1,0:T(8,128)(2,1)} %fusion.171), channel_id=1, source_target_pairs={{0,8},{4,12},{8,0},{12,4},{16,24},{20,28},{24,16},{28,20},{1,9},{5... | collective-permute-start | bytes 3538952 | tf_op jit(solution)/shard_map/ppermute | solution.py:398
  1267.2 81.3 %collective-permute-start.109 = (bf16[768,768]{1,0:T(8,128)(2,1)}, bf16[768,768]{1,0:T(8,128)(2,1)}, u32[]{:S(2)}, u32[]{:S(2)}) collective-permute-start(bf16[768,768]{1,0:T(8,128)(2,1)} %fusion.174), channel_id=1, source_target_pairs={{0,16},{4,20},{8,24},{12,28},{16,0},{20,4},{24,8},{28,12},{1,17},{... | collective-permute-start | bytes 3538952 | tf_op jit(solution)/shard_map/ppermute | solution.py:398
  1348.4 102.3 %collective-permute-start.111 = (bf16[768,768]{1,0:T(8,128)(2,1)}, bf16[768,768]{1,0:T(8,128)(2,1)}, u32[]{:S(2)}, u32[]{:S(2)}) collective-permute-start(bf16[768,768]{1,0:T(8,128)(2,1)} %fusion.168), channel_id=1, source_target_pairs={{0,16},{4,20},{8,24},{12,28},{16,0},{20,4},{24,8},{28,12},{1,17},{... | collective-permute-start | bytes 3538952 | tf_op jit(solution)/shard_map/ppermute | solution.py:398
  1357.4 121.2 %collective-permute-start.98 = (bf16[384,1536]{1,0:T(8,128)(2,1)}, bf16[384,1536]{1,0:T(8,128)(2,1)}, u32[]{:S(2)}, u32[]{:S(2)}) collective-permute-start(bf16[384,1536]{1,0:T(8,128)(2,1)} %convolution_convert_fusion.7), channel_id=1, source_target_pairs={{0,16},{4,20},{8,24},{12,28},{16,0},{20,4},{24,8},{28,12},{1,17},{... | collective-permute-start | bytes 3538952 | tf_op jit(solution)/shard_map/ppermute | solution.py:398
  1363.5 83.9 %collective-permute-start.105 = (bf16[768,768]{1,0:T(8,128)(2,1)}, bf16[768,768]{1,0:T(8,128)(2,1)}, u32[]{:S(2)}, u32[]{:S(2)}) collective-permute-start(bf16[768,768]{1,0:T(8,128)(2,1)} %add_convert_fusion.3), channel_id=1, source_target_pairs={{0,16},{4,20},{8,24},{12,28},{16,0},{20,4},{24,8},{28,12},{1,17},{... | collective-permute-start | bytes 3538952 | tf_op jit(solution)/shard_map/ppermute | solution.py:398
  1447.4 87.5 %collective-permute-start.90 = (bf16[384,1536]{1,0:T(8,128)(2,1)S(1)}, bf16[384,1536]{1,0:T(8,128)(2,1)S(1)}, u32[]{:S(2)}, u32[]{:S(2)}) collective-permute-start(bf16[384,1536]{1,0:T(8,128)(2,1)S(1)} %copy-done.147), channel_id=1, source_target_pairs={{0,8},{4,12},{8,0},{12,4},{16,24},{20,28},{24,16},{28,20},{1,9},{5... | collective-permute-start | bytes 3538952 | tf_op jit(solution)/shard_map/ppermute | solution.py:398
  1450.7 86.3 %collective-permute-start.92 = (bf16[384,1536]{1,0:T(8,128)(2,1)S(1)}, bf16[384,1536]{1,0:T(8,128)(2,1)S(1)}, u32[]{:S(2)}, u32[]{:S(2)}) collective-permute-start(bf16[384,1536]{1,0:T(8,128)(2,1)S(1)} %copy-done.148), channel_id=1, source_target_pairs={{0,16},{4,20},{8,24},{12,28},{16,0},{20,4},{24,8},{28,12},{1,17},{... | collective-permute-start | bytes 3538952 | tf_op jit(solution)/shard_map/ppermute | solution.py:398
  (310 other events, 6449.8 us)

commit v2 on v1

--- a/solution.py
+++ b/solution.py
@@ -1,6 +1,10 @@
+import functools
+
 import jax
 import jax.numpy as jnp
 from jax import lax
+from jax.experimental import pallas as pl
+from jax.experimental.pallas import tpu as pltpu
 from jax.sharding import PartitionSpec as P
 
 HEAD_DIM = 64
@@ -392,6 +396,118 @@
 
 PLANE = 4
 LINE = 4
+PAIR = 2 * HEAD_DIM
+
+
+def key_bias(length, keys, pixels):
+    rows = lax.broadcasted_iota(jnp.int32, (keys, 1), 0)
+    return jnp.where(rows < pixels + length, 0.0, -1000000000.0)
+
+
+def one_head(value, head):
+    lanes = lax.broadcasted_iota(jnp.int32, value.shape, 1)
+    return jnp.where((lanes // HEAD_DIM) == head, value, jnp.zeros_like(value))
+
+
+def attend_kernel(pixels, length_ref, rows_ref, mixed_ref, log_ref):
+    keys = rows_ref.shape[1]
+    bias = key_bias(length_ref[pl.program_id(0)], keys, pixels)
+    query = rows_ref[0, :pixels, :PAIR] * HEAD_DIM ** (-0.5)
+    key = rows_ref[0, :, PAIR : 2 * PAIR]
+    value = rows_ref[0, :, 2 * PAIR :]
+    total = jnp.zeros((pixels, PAIR), jnp.float32)
+    for head in range(PAIR // HEAD_DIM):
+        scores = product_nt(key, one_head(query, head)) + bias
+        top = jnp.max(scores, axis=0, keepdims=True)
+        exponent = jnp.exp(scores - top)
+        row_total = jnp.sum(exponent, axis=0, keepdims=True)
+        probs = (exponent * (1.0 / row_total)).astype(jnp.bfloat16)
+        total = total + product_tn(probs, one_head(value, head))
+        log_ref[0, 0, head : head + 1, :] = top + jnp.log(row_total)
+    mixed_ref[0] = total.astype(jnp.bfloat16)
+
+
+def attend_back_kernel(pixels, length_ref, rows_ref, gmix_ref, log_ref, grad_ref):
+    keys = rows_ref.shape[1]
+    bias = key_bias(length_ref[pl.program_id(0)], keys, pixels)
+    query = rows_ref[0, :pixels, :PAIR] * HEAD_DIM ** (-0.5)
+    key = rows_ref[0, :, PAIR : 2 * PAIR]
+    value = rows_ref[0, :, 2 * PAIR :]
+    g_query = jnp.zeros((pixels, PAIR), jnp.float32)
+    g_key = jnp.zeros((keys, PAIR), jnp.float32)
+    g_value = jnp.zeros((keys, PAIR), jnp.float32)
+    for head in range(PAIR // HEAD_DIM):
+        query_one = one_head(query, head)
+        gmix_one = one_head(gmix_ref[0], head)
+        scores = product_nt(key, query_one) + bias
+        weights = jnp.exp(scores - log_ref[0, 0, head : head + 1, :])
+        g_probs = product_nt(value, gmix_one)
+        inner = jnp.sum(weights * g_probs, axis=0, keepdims=True)
+        g_score = (weights * (g_probs - inner)).astype(jnp.bfloat16)
+        g_key = g_key + product(g_score, query_one)
+        g_value = g_value + product(weights.astype(jnp.bfloat16), gmix_one)
+        g_query = g_query + product_tn(g_score, one_head(key, head))
+    g_query = (g_query * HEAD_DIM ** (-0.5)).astype(jnp.bfloat16)
+    grad_ref[0, :pixels, :PAIR] = g_query
+    grad_ref[0, pixels:, :PAIR] = jnp.zeros((keys - pixels, PAIR), jnp.bfloat16)
+    grad_ref[0, :, PAIR : 2 * PAIR] = g_key.astype(jnp.bfloat16)
+    grad_ref[0, :, 2 * PAIR :] = g_value.astype(jnp.bfloat16)
+
+
+def attend_specs(keys, pixels):
+    rows = pl.BlockSpec((1, keys, 3 * PAIR), lambda i, j, n: (i, 0, j))
+    narrow = pl.BlockSpec((1, pixels, PAIR), lambda i, j, n: (i, 0, j))
+    logs = pl.BlockSpec((1, 1, PAIR // HEAD_DIM, pixels), lambda i, j, n: (i, j, 0, 0))
+    return (rows, narrow, logs)
+
+
+def attend(rows, lengths, pixels):
+    count, keys, width = rows.shape
+    groups = width // (3 * PAIR)
+    rows_spec, narrow, logs = attend_specs(keys, pixels)
+    return pl.pallas_call(
+        functools.partial(attend_kernel, pixels),
+        out_shape=(
+            jax.ShapeDtypeStruct((count, pixels, groups * PAIR), jnp.bfloat16),
+            jax.ShapeDtypeStruct((count, groups, PAIR // HEAD_DIM, pixels), jnp.float32),
+        ),
+        grid_spec=pltpu.PrefetchScalarGridSpec(
+            num_scalar_prefetch=1,
+            grid=(count, groups),
+            in_specs=[rows_spec],
+            out_specs=[narrow, logs],
+        ),
+        compiler_params=pltpu.CompilerParams(vmem_limit_bytes=40 << 20),
+        cost_estimate=pl.CostEstimate(
+            flops=count * groups * 8 * pixels * keys * PAIR,
+            bytes_accessed=rows.size * 3,
+            transcendentals=2 * count * groups * pixels * keys,
+        ),
+        name="attend",
+    )(lengths, rows)
+
+
+def attend_back_pairs(rows, g_mixed, logs_in, lengths, pixels):
+    count, keys, width = rows.shape
+    groups = width // (3 * PAIR)
+    rows_spec, narrow, logs = attend_specs(keys, pixels)
+    return pl.pallas_call(
+        functools.partial(attend_back_kernel, pixels),
+        out_shape=jax.ShapeDtypeStruct(rows.shape, jnp.bfloat16),
+        grid_spec=pltpu.PrefetchScalarGridSpec(
+            num_scalar_prefetch=1,
+            grid=(count, groups),
+            in_specs=[rows_spec, narrow, logs],
+            out_specs=rows_spec,
+        ),
+        compiler_params=pltpu.CompilerParams(vmem_limit_bytes=40 << 20),
+        cost_estimate=pl.CostEstimate(
+            flops=count * groups * 20 * pixels * keys * PAIR,
+            bytes_accessed=rows.size * 5,
+            transcendentals=2 * count * groups * pixels * keys,
+        ),
+        name="attend_back",
+    )(lengths, rows, g_mixed, logs_in)
 
 
 def swap(value, bit):
@@ -444,20 +560,18 @@
     return (result, (by_x, by_y))
 
 
-def gather_all(shards, plane, place):
-    results = []
-    line_done, plane_done = (None, None)
-    for shard in shards:
-        if line_done is not None:
-            shard, _ = lax.optimization_barrier((shard, line_done))
-        parts, rows, cols = shard.shape
-        line = gather_line(shard, place).reshape(parts * LINE * rows, cols)
-        line_done = line
-        if plane_done is not None:
-            line, _ = lax.optimization_barrier((line, plane_done))
-        full, plane_done = gather_plane(line, plane)
-        results.append(full.reshape(PLANE * parts * LINE * rows, cols))
-    return results
+def held(*values):
+    return lax.optimization_barrier(values)
+
+
+def flat_line(shard, place):
+    parts, rows, cols = shard.shape
+    return gather_line(shard, place).reshape(parts * LINE * rows, cols)
+
+
+def flat_plane(line, plane):
+    full, _ = gather_plane(line, plane)
+    return full.reshape(-1, line.shape[1])
 
 
 def reduce_owner(piece, parts, plane, place):
@@ -490,19 +604,12 @@
 def gather_small(value, plane, core, place):
     cores = jnp.zeros((2,) + value.shape, value.dtype)
     cores = put(put(cores, value, core), swap(value, 1), 1 - core)
-    line = jnp.zeros((2, LINE) + value.shape, value.dtype)
-    line = put(line, cores, place, 1)
+    full = gather_small_plane(cores, plane)
+    line = jnp.zeros((LINE,) + full.shape, value.dtype)
+    line = put(line, full, place)
     for step in range(1, LINE):
-        line = put(line, rotate(cores, step), (place - step) % LINE, 1)
-    return gather_small_plane(line, plane)
-
-
-def gather_small_line(value, plane, place):
-    line = jnp.zeros((LINE,) + value.shape, value.dtype)
-    line = put(line, value, place)
-    for step in range(1, LINE):
-        line = put(line, rotate(value, step), (place - step) % LINE)
-    return gather_small_plane(line, plane)
+        line = put(line, rotate(full, step), (place - step) % LINE)
+    return line
 
 
 def gather_small_plane(line, plane):
@@ -577,26 +684,24 @@
     text_len, clip_width = clip_text.shape[1:]
     hidden_width = up_weight.shape[1]
     time_rank = time_weight.shape[0]
-    share = up_weight.shape[0]
     half_channels, half_hidden = (channels // 2, hidden_width // 2)
-    head_count = half_channels // HEAD_DIM
     dp_index = lax.axis_index("dp")
     place = lax.axis_index("band")
     plane, core = (dp_index // 2, dp_index % 2)
     f32, low = (jnp.float32, jnp.bfloat16)
 
-    latent = spread_line(latents, place).reshape(height, columns, channels)
-    small_cols = jnp.concatenate([conv_weight, vectors], axis=0)
-    small_all = gather_small(small_cols, plane, core, place)
-    small_all = small_all.reshape((-1,) + small_cols.shape).transpose(1, 0, 2)
-    small_all = small_all.reshape(small_cols.shape[0], channels).astype(f32)
-    taps, vecs = (small_all[:9], small_all[9:])
-    hidden_all = gather_small_line(hidden_vecs, plane, place)
-    hidden_all = hidden_all.reshape((-1,) + hidden_vecs.shape).transpose(1, 0, 2)
-    hidden_all = hidden_all.reshape(3, half_hidden).astype(f32)
-    time_all = gather_small(time_weight, plane, core, place)
-    time_all = time_all.reshape((-1,) + time_weight.shape).transpose(1, 0, 2)
-    time_all = time_all.reshape(time_rank, 2 * channels)
+    small = jnp.concatenate(
+        [conv_weight.reshape(-1), vectors.reshape(-1), hidden_vecs.reshape(-1)]
+    )
+    small_all = gather_small(small, plane, core, place).astype(f32)
+    col_rows, col_width = (9 + vectors.shape[0], conv_weight.shape[1])
+    col_all = small_all[..., : col_rows * col_width]
+    col_all = col_all.reshape(LINE, PLANE, 2, col_rows, col_width).transpose(3, 1, 2, 0, 4)
+    col_all = col_all.reshape(col_rows, channels)
+    taps, vecs = (col_all[:9], col_all[9:])
+    hidden_all = pick(small_all[..., col_rows * col_width :], core, 2)
+    hidden_all = hidden_all.reshape(LINE, PLANE, 3, -1).transpose(2, 1, 0, 3)
+    hidden_all = hidden_all.reshape(3, half_hidden)
 
     def with_partner(value, axis):
         kept = core_half(value, axis, core)
@@ -604,17 +709,32 @@
         both = jnp.zeros((2,) + kept.shape, kept.dtype)
         return put(put(both, kept, core), got, 1 - core)
 
+    def attn_order(value):
+        groups = jnp.moveaxis(value.reshape(value.shape[:-1] + (-1, PAIR)), 0, -2)
+        return groups.reshape(groups.shape[:-3] + (-1,))
+
+    def attn_back_order(value):
+        groups = jnp.moveaxis(value.reshape(value.shape[:-1] + (-1, 3, PAIR)), -2, 0)
+        return groups.reshape(groups.shape[:-2] + (-1,))
+
     up_shard = with_partner(up_weight, 1)
-    attn_shard = with_partner(attn_in, 2).transpose(0, 2, 1, 3)
-    attn_shard = attn_shard.reshape(2, share, 3 * half_channels)
-    up_full, down_full, attn_full, map_full, out_full = gather_all(
-        (up_shard, down_weight[None], attn_shard, map_weight[None], out_weight[None]),
-        plane,
-        place,
-    )
-
+    attn_shard = attn_order(jnp.moveaxis(with_partner(attn_in, 2), 1, 0))
+
+    latent = spread_line(latents, place).reshape(height, columns, channels)
+    up_line = flat_line(up_shard, place)
+    up_line, latent, down_shard, map_shard, time_shard = held(
+        up_line, latent, down_weight[None], map_weight[None], time_weight
+    )
+    up_full = flat_plane(up_line, plane)
+    down_line = flat_line(down_shard, place)
+    map_line = flat_line(map_shard, place)
+    time_all = gather_small(time_shard, plane, core, place).transpose(3, 1, 2, 0, 4)
+    time_all = time_all.reshape(time_rank, 2 * channels)
     clip_own = pick(clip_text, place).astype(f32)
-    words = pair(jax.nn.silu(clip_own).astype(low)).reshape(2 * text_len, clip_width)
+    words_own = jax.nn.silu(clip_own).astype(low)
+    text_pad = -(-text_len // 16) * 16
+    words_own = jnp.pad(words_own, ((0, text_pad - text_len), (0, 0)))
+    words = pair(words_own).reshape(2 * text_pad, clip_width)
     words_half = core_half(words, 1, core)
     lengths_two = pair(pick(lengths, place))
     embed_own = pick(embedding, place)
@@ -628,9 +748,17 @@
         ].astype(f32)
     first_norm, first_inv = norm_parts(conv_out.reshape(pixels, channels))
     first_in = pair(first_norm.astype(low)).reshape(2 * pixels, channels)
+    up_full, down_line, map_line, first_in, words_half, attn_shard = held(
+        up_full, down_line, map_line, first_in, words_half, attn_shard
+    )
+    down_full = flat_plane(down_line, plane)
+    map_full = flat_plane(map_line, plane)
+    attn_line = flat_line(attn_shard, place)
     up_out = product(first_in, up_full) + hidden_all[0]
-    active = gelu_exact(up_out)
-    active_lat = active.reshape(2, pixels, half_hidden)
+    below = 0.5 + 0.5 * lax.erf(up_out * 0.5**0.5)
+    slope = below + up_out * ((0.5 / jnp.pi) ** 0.5 * jnp.exp(-0.5 * up_out * up_out))
+    active, slope = held((up_out * below).astype(low), slope.astype(low))
+    active_lat = active.reshape(2, pixels, half_hidden).astype(f32)
     strength = jnp.sqrt(jnp.sum(active_lat * active_lat, axis=1))
     strength_sum = pair_sum(jnp.sum(strength, axis=-1, keepdims=True))
     grn_denom = strength_sum / hidden_width + 1e-06
@@ -639,6 +767,11 @@
     grn_out = (
         gamma_vec * (active_lat * grn_ratio[:, None]) + hidden_all[2] + active_lat
     ).astype(low)
+    grn_out, down_full, map_full, attn_line, out_shard = held(
+        grn_out, down_full, map_full, attn_line, out_weight[None]
+    )
+    attn_full = flat_plane(attn_line, plane)
+    out_line = flat_line(out_shard, place)
     lowered = own_sum(product(grn_out[0], down_full), product(grn_out[1], down_full))
     first_sum = latent.reshape(pixels, channels).astype(f32) + (lowered + vecs[1])
     modulation = product(embed_own[None], time_all)[0]
@@ -646,38 +779,26 @@
     shift_vec = modulation[channels:] + vecs[3]
     second = first_sum * (1.0 + scale_vec) + shift_vec
     second_norm, second_inv = norm_parts(second)
-    second_in = pair(second_norm.astype(low)).reshape(2 * pixels, channels)
-
-    mapped = pair_sum(product(words_half, map_full).reshape(2, text_len, channels))
-    mapped = (mapped + vecs[4]).astype(low).reshape(2 * text_len, channels)
-    bias = jnp.concatenate(
-        [
-            core_half(vecs[5], 0, core),
-            jnp.zeros((half_channels,), f32),
-            core_half(vecs[6], 0, core),
-        ]
-    )
-    pixel_qkv = (product(second_in, attn_full) + bias).astype(low)
-    text_kv = (
-        product(mapped, attn_full[:, half_channels:]) + bias[half_channels:]
-    ).astype(low)
-    pixel_qkv = pixel_qkv.reshape(2, pixels, 3, head_count, HEAD_DIM)
-    text_kv = text_kv.reshape(2, text_len, 2, head_count, HEAD_DIM)
-    query = pixel_qkv[:, :, 0]
-    key_rows = jnp.concatenate([pixel_qkv[:, :, 1], text_kv[:, :, 0]], axis=1)
-    value_rows = jnp.concatenate([pixel_qkv[:, :, 2], text_kv[:, :, 1]], axis=1)
-    key_places = jnp.arange(pixels + text_len, dtype=jnp.int32)
-    valid_keys = key_places[None] < pixels + lengths_two[:, None]
-    mixed, log_totals = lax.map(attend_one, (query, key_rows, value_rows, valid_keys))
-    mixed = mixed.reshape(2, pixels, half_channels)
+    mapped = pair_sum(product(words_half, map_full).reshape(2, text_pad, channels))
+    mapped = (mapped + vecs[4]).astype(low)
+    sources = jnp.concatenate([pair(second_norm.astype(low)), mapped], axis=1)
+    keys = pixels + text_pad
+    sources, attn_full, out_line, grad_shard = held(sources, attn_full, out_line, grad_out)
+    sources = sources.reshape(2 * keys, channels)
+    out_full = flat_plane(out_line, plane)
+    grad_own = spread_line(grad_shard, place).reshape(pixels, channels)
+    bias = jnp.stack([vecs[5], jnp.zeros((channels,), f32), vecs[6]])
+    bias = attn_order(core_half(bias, 1, core))
+    rows_qkv = (product(sources, attn_full) + bias).astype(low)
+    rows_qkv = rows_qkv.reshape(2, keys, 3 * half_channels)
+    mixed, log_totals = attend(rows_qkv, lengths_two, pixels)
     attended = own_sum(product(mixed[0], out_full), product(mixed[1], out_full))
     layer_own = (second + (attended + vecs[7])).astype(low)
     layer_out = spread_line(layer_own.reshape(latents.shape), place)
 
-    grad_own = spread_line(grad_out, place).reshape(pixels, channels)
     grad_two = pair(grad_own)
     g_mixed = product_nt(grad_two.reshape(2 * pixels, channels), out_full).astype(low)
-    g_mixed = g_mixed.reshape(2, pixels, head_count, HEAD_DIM)
+    g_mixed = g_mixed.reshape(2, pixels, half_channels)
 
     def owner_sums(left, right, parts):
         block = left.shape[1] // PLANE
@@ -692,27 +813,17 @@
     out_grad = owner_sums(
         mixed.reshape(2 * pixels, half_channels), grad_two.reshape(2 * pixels, channels), 1
     )[0]
-    g_query, g_key, g_value = lax.map(
-        attend_back, (query, key_rows, value_rows, valid_keys, log_totals, g_mixed)
-    )
-    g_key, g_value = (g_key.astype(low), g_value.astype(low))
-    g_pixel = jnp.stack([g_query, g_key[:, :pixels], g_value[:, :pixels]], axis=2)
-    g_pixel = g_pixel.reshape(2, pixels, 3 * half_channels)
-    g_text = jnp.stack([g_key[:, pixels:], g_value[:, pixels:]], axis=2)
-    g_text = g_text.reshape(2 * text_len, 2 * half_channels)
-    g_second_in = own_sum(product_nt(g_pixel[0], attn_full), product_nt(g_pixel[1], attn_full))
-    g_mapped = pair_sum(
-        product_nt(g_text, attn_full[:, half_channels:]).reshape(2, text_len, channels)
-    )
-    g_mapped = g_mapped.astype(low).reshape(2 * text_len, channels)
-    padded_text = jnp.concatenate([jnp.zeros((2 * text_len, half_channels), low), g_text], axis=1)
-    attn_grad = owner_sums(
-        jnp.concatenate([second_in, mapped], axis=0),
-        jnp.concatenate([g_pixel.reshape(2 * pixels, 3 * half_channels), padded_text], axis=0),
-        2,
-    )
+    g_rows = attend_back_pairs(rows_qkv, g_mixed, log_totals, lengths_two, pixels)
+    g_second_in = own_sum(
+        product_nt(g_rows[0, :pixels], attn_full), product_nt(g_rows[1, :pixels], attn_full)
+    )
+    g_text = g_rows[:, pixels:].reshape(2 * text_pad, 3 * half_channels)
+    g_mapped = pair_sum(product_nt(g_text, attn_full).reshape(2, text_pad, channels))
+    g_mapped = g_mapped.astype(low).reshape(2 * text_pad, channels)
+    g_flat = g_rows.reshape(2 * keys, 3 * half_channels)
+    attn_grad = owner_sums(sources, g_flat, 2)
     map_grad = owner_sums(words_half, g_mapped, 1)[0]
-    g_words = product_nt(g_mapped, map_full).reshape(2, text_len, clip_width // 2)
+    g_words = product_nt(g_mapped, map_full).reshape(2, text_pad, -1)[:, :text_len]
     g_words = core_merge(g_words[0], swap(g_words[1], 1), 1, core)
     sigmoid_text = jax.nn.sigmoid(clip_own)
     text_own = (g_words * (sigmoid_text * (1.0 + clip_own * (1.0 - sigmoid_text)))).astype(low)
@@ -731,8 +842,10 @@
     down_grad = owner_sums(grn_out.reshape(2 * pixels, half_hidden), g_down, 1)[0]
     g_grn = product_nt(g_down, down_full).reshape(2, pixels, half_hidden)
     g_grn_active = jnp.sum(g_grn * active_lat, axis=1)
+    g_grn_sum = jnp.sum(g_grn, axis=(0, 1))
+    g_grn, g_grn_active, grad_beta = held(g_grn.astype(low), g_grn_active, g_grn_sum)
+    g_grn = g_grn.astype(f32)
     grad_gamma = jnp.sum(g_grn_active * grn_ratio, axis=0)
-    grad_beta = jnp.sum(g_grn, axis=(0, 1))
     g_ratio = g_grn_active * gamma_vec
     ratio_sum = pair_sum(jnp.sum(g_ratio * strength, axis=-1, keepdims=True))
     g_strength = g_ratio / grn_denom - ratio_sum / (hidden_width * grn_denom * grn_denom)
@@ -740,8 +853,7 @@
         g_grn * (1.0 + gamma_vec * grn_ratio[:, None])
         + active_lat * (g_strength / strength)[:, None]
     )
-    gelu_value, gelu_pull = jax.vjp(gelu_exact, up_out)
-    g_up = gelu_pull(g_active.reshape(2 * pixels, half_hidden))[0].astype(low)
+    g_up = (g_active.reshape(2 * pixels, half_hidden) * slope.astype(f32)).astype(low)
     g_first_in = own_sum(
         product_nt(g_up[:pixels], up_full), product_nt(g_up[pixels:], up_full)
     )
@@ -765,11 +877,13 @@
     up_grad = core_merge(
         pick(up_grad, core), swap(pick(up_grad, 1 - core), 1), 1, core
     )
-    attn_grad = attn_grad.reshape(2, share, 3, half_channels)
     attn_grad = core_merge(
-        pick(attn_grad, core), swap(pick(attn_grad, 1 - core), 1), 2, core
-    ).transpose(1, 0, 2)
-
+        attn_back_order(pick(attn_grad, core)),
+        attn_back_order(swap(pick(attn_grad, 1 - core), 1)),
+        2,
+        core,
+    )
+    column_grads = attn_back_order(column_sums(g_flat))
     own_zero = jnp.zeros((half_channels,), f32)
     vec_parts = jnp.stack(
         [
@@ -777,15 +891,9 @@
             column_sums(g_down_own),
             g_scale,
             g_shift,
-            column_sums(g_mapped[:text_len]),
-            core_merge(column_sums(g_pixel.reshape(2 * pixels, -1)[:, :half_channels]), own_zero, 0, core),
-            core_merge(
-                column_sums(g_pixel.reshape(2 * pixels, -1)[:, 2 * half_channels :])
-                + column_sums(g_text[:, half_channels:]),
-                own_zero,
-                0,
-                core,
-            ),
+            column_sums(g_mapped[:text_pad]),
+            core_merge(column_grads[0], own_zero, 0, core),
+            core_merge(column_grads[2], own_zero, 0, core),
             jnp.sum(grad_float, axis=0),
         ]
     )

time: 1660 us -> 1290 us (0.78)
  matrix products: 398 us -> 222 us
  waiting for transfers between devices: 552 us -> 445 us
  other arithmetic: 209 us -> 106 us
  Pallas kernels: 0 us -> 76.2 us
  local copies, waits for them, and re-layouts: 268 us -> 218 us
    dot_general x14 -> x0, matrix products: 141 us -> none  [the longest x4 46.5 us: masked_scores(): jnp.einsum('qhd,khd->hqk', query_one, key_one, preferred_element_type=jnp...]
    pallas_call x0 -> x2, Pallas kernels: none -> 76.2 us  [the longest x1 47.2 us: attend_back_pairs(): pl.pallas_call(functools.partial(attend_back_kernel, pixels), out_shape=j...]
    ppermute x72 -> x69, waiting for transfers between devices: 284 us -> 208 us  [rotate(): lax.ppermute(value, 'band', [(i, (i + step) % LINE) for i in range(LINE)])]
    dot_general x9 -> x8, matrix products: 87.9 us -> 53.5 us  [product(): return jnp.dot(left_op, right_op, preferred_element_type=jnp.float32)]
    ppermute x80 -> x78, waiting for transfers between devices: 268 us -> 238 us  [swap(): return lax.ppermute(value, 'dp', [(i, i ^ bit) for i in range(2 * PLANE)])]
    convert_element_type x9 -> x4, other arithmetic: 32.4 us -> 1.66 us  [the longest x1 0.8 us: paired_device(): words_own = jax.nn.silu(clip_own).astype(low)]
    dynamic_update_slice x84 -> x75, local copies, waits for them, and re-layouts: 59.7 us -> 89.4 us  [put(): return lax.dynamic_update_index_in_dim(buffer, value, index, axis)]
    another operation x15 -> x10, local copies, waits for them, and re-layouts: 33.1 us -> 4.09 us  [the longest x1 12.3 us: paired_device(): g_pixel.reshape(2 * pixels, -1)[:, :half_channels]]
  transfers between devices with their start and end apart: 152 -> 147, of which waited for: 62 -> 54; matrix products, arithmetic and copies ran while one was open for 32% -> 38% of each run, Pallas kernels for 0% -> 6%
where the time goes in v2:
time: 1290 us; the launch traced here: 1270 us
  waiting for transfers between devices  445 us (34%)
  matrix products  222 us (17%)
  local copies, waits for them, and re-layouts  218 us (17%)
  starting transfers between devices  202 us (16%)
  other arithmetic  106 us (8%)
  Pallas kernels  76.2 us (6%)
    ppermute x78, waiting for transfers between devices, swap(): return lax.ppermute(value, 'dp', [(i, i ^ bit) for i in range(2 * PLANE)])  238 us
    ppermute x69, waiting for transfers between devices, rotate(): lax.ppermute(value, 'band', [(i, (i + step) % LINE) for i in range(LINE)])  208 us
    ppermute x69, starting transfers between devices, rotate(): lax.ppermute(value, 'band', [(i, (i + step) % LINE) for i in range(LINE)])  137 us
    dot_general x40, matrix products, product_tn(): lax.dot_general(left_op, right_op, (((0,), (0,)), ((), ())), preferred_el...  113 us
    dynamic_update_slice x75, local copies, waits for them, and re-layouts, put(): return lax.dynamic_update_index_in_dim(buffer, value, index, axis)  89.4 us
    ppermute x78, starting transfers between devices, swap(): return lax.ppermute(value, 'dp', [(i, i ^ bit) for i in range(2 * PLANE)])  65.1 us
    dot_general x8, matrix products, product_nt(): lax.dot_general(left_op, right_op, (((1,), (1,)), ((), ())), preferred_el...  55.3 us
    dot_general x8, matrix products, product(): return jnp.dot(left_op, right_op, preferred_element_type=jnp.float32)  53.5 us
  transfers between devices with their start and end apart: 147, of which 54 were waited for; matrix products, arithmetic and copies ran while one was open for 38% of the time, Pallas kernels for 6%

profile of v2, /device:TPU:0, one launch (start us, length us, event | category | flops | bytes accessed | tf_op | source)
XLA Modules:
  0.0 1273.0 jit_solution(13531839012356232531)
XLA Ops:
  100.3 23.5 %collective-permute-done.2 = bf16[2,48,3072]{2,1,0:T(8,128)(2,1)S(1)} collective-permute-done((bf16[2,48,3072]{2,1,0:T(8,128)(2,1)S(1)}, bf16[2,48,3072]{2,1,0:T(8,128)(2,1)S(1)}, u32[]{:S(2)}, u32[]{:S(2)}) %collective-permute-start.2) | collective-permute-done | bytes 589856 | tf_op jit(solution)/shard_map/ppermute | solution.py:518
  125.5 11.4 collective-permute-start.20
  229.1 15.5 %collective-permute-start.19 = (bf16[1,192,1536]{2,1,0:T(8,128)(2,1)}, bf16[1,192,1536]{2,1,0:T(8,128)(2,1)S(1)}, u32[]{:S(2)}, u32[]{:S(2)}) collective-permute-start(bf16[1,192,1536]{2,1,0:T(8,128)(2,1)} %bitcast.16), channel_id=1, source_target_pairs={{0,3},{1,0},{2,1},{3,2},{4,7},{5,4},{6,5},{7,6},{8,11},{9,8},{10,9... | collective-permute-start | bytes 1769480 | tf_op jit(solution)/shard_map/ppermute | solution.py:518
  246.9 12.5 collective-permute-done.19
  273.6 18.8 %collective-permute-done.15 = bf16[192,3072]{1,0:T(8,128)(2,1)S(1)} collective-permute-done((bf16[192,3072]{1,0:T(8,128)(2,1)S(1)}, bf16[192,3072]{1,0:T(8,128)(2,1)S(1)}, u32[]{:S(2)}, u32[]{:S(2)}) %collective-permute-start.15) | collective-permute-done | bytes 1179680 | tf_op jit(solution)/shard_map/ppermute | solution.py:514
  301.0 18.5 %fusion.4 = (bf16[1152,3072]{1,0:T(8,128)(2,1)}, bf16[1152,3072]{1,0:T(8,128)(2,1)S(1)}) fusion(f32[3072]{0:T(1024)S(1)} %copy-done.102, bf16[1152,1536]{1,0:T(8,128)(2,1)S(1)} %bitcast.675, bf16[1536,3072]{1,0:T(8,128)(2,1)} %bitcast.31), kind=kOutput, calls=%fused_computation.10 | convolution fusion | flops 10914103296 | bytes 27144192 | tf_op jit(solution)/shard_map/dot_general | solution.py:27
  350.2 44.7 %collective-permute-done.33 = bf16[80,1536]{1,0:T(8,128)(2,1)S(1)} collective-permute-done((bf16[80,1536]{1,0:T(8,128)(2,1)S(1)}, bf16[80,1536]{1,0:T(8,128)(2,1)S(1)}, u32[]{:S(2)}, u32[]{:S(2)}) %collective-permute-start.33) | collective-permute-done | bytes 245792 | tf_op jit(solution)/shard_map/ppermute | solution.py:514
  403.7 22.0 %collective-permute-done.29 = bf16[384,1536]{1,0:T(8,128)(2,1)S(1)} collective-permute-done((bf16[384,1536]{1,0:T(8,128)(2,1)S(1)}, bf16[384,1536]{1,0:T(8,128)(2,1)S(1)}, u32[]{:S(2)}, u32[]{:S(2)}) %collective-permute-start.29) | collective-permute-done | bytes 1179680 | tf_op jit(solution)/shard_map/ppermute | solution.py:514
  448.8 21.1 %collective-permute-done.49 = bf16[384,2304]{1,0:T(8,128)(2,1)S(1)} collective-permute-done((bf16[384,2304]{1,0:T(8,128)(2,1)S(1)}, bf16[384,2304]{1,0:T(8,128)(2,1)S(1)}, u32[]{:S(2)}, u32[]{:S(2)}) %collective-permute-start.49) | collective-permute-done | bytes 1769504 | tf_op jit(solution)/shard_map/ppermute | solution.py:514
  511.8 29.1 %attend.1 = (bf16[2,576,768]{2,1,0:T(8,128)(2,1)S(1)}, f32[2,6,2,576]{3,2,1,0:T(2,128)S(1)}) custom-call(s32[2]{0:T(128)S(1)} %pad_add_fusion.length_ref, bf16[2,656,2304]{2,1,0:T(8,128)(2,1)S(1)} %bitcast.592), custom_call_target="tpu_custom_call" | custom-call | flops 4643094528 | bytes 9068544 | tf_op jit(solution)/shard_map/attend/pallas_call | solution.py:468
  570.9 47.2 %attend_back.1 = bf16[2,656,2304]{2,1,0:T(8,128)(2,1)S(1)} custom-call(s32[2]{0:T(128)S(1)} %pad_add_fusion.length_ref, bf16[2,656,2304]{2,1,0:T(8,128)(2,1)S(1)} %bitcast.595, bf16[2,576,768]{2,1,0:T(8,128)(2,1)S(1)} %bitcast.596, f32[2,6,2,576]{3,2,1,0:T(2,128)S(1)} %get-tuple-element.61.log_ref), custom_call_target="tpu_custom_call" | custom-call | flops 11607736320 | bytes 15114240 | tf_op jit(solution)/shard_map/attend_back/pallas_call | solution.py:494
  666.4 14.9 %collective-permute-done.137 = bf16[192,768]{1,0:T(8,128)(2,1)S(1)} collective-permute-done((bf16[192,768]{1,0:T(8,128)(2,1)S(1)}, bf16[192,768]{1,0:T(8,128)(2,1)S(1)}, u32[]{:S(2)}, u32[]{:S(2)}) %collective-permute-start.137) | collective-permute-done | bytes 294944 | tf_op jit(solution)/shard_map/ppermute | solution.py:514
  711.5 17.6 %collective-permute-done.61 = bf16[6,24,1536]{2,1,0:T(8,128)(2,1)S(1)} collective-permute-done((bf16[6,24,1536]{2,1,0:T(8,128)(2,1)S(1)}, bf16[6,24,1536]{2,1,0:T(8,128)(2,1)S(1)}, u32[]{:S(2)}, u32[]{:S(2)}) %collective-permute-start.61) | collective-permute-done | bytes 442400 | tf_op jit(solution)/shard_map/ppermute | solution.py:518
  884.8 17.5 %fusion.367 = (f32[3072]{0:T(1024)S(1)}, f32[2,3072]{1,0:T(2,128)S(1)}, bf16[2,576,3072]{2,1,0:T(8,128)(2,1)}) fusion(bf16[2,576,3072]{2,1,0:T(8,128)(2,1)S(1)} %bitcast.611, bf16[3072,1536]{1,0:T(8,128)(2,1)} %bitcast.64, bf16[1,576,1536]{2,1,0:T(8,128)(2,1)} %bitcast.144, bf16[1,576,1536]{2,1,0:T(8,128)(2,1)} %bitcast.650), kind=kOutput, calls=%fused_computation.661 | convolution fusion | flops 10891090944 | bytes 27168768 | tf_op jit(solution)/shard_map/dot_general | solution.py:37
  920.4 13.3 %fusion.10 = f32[2,576,3072]{2,1,0:T(8,128)} fusion(bf16[2,576,3072]{2,1,0:T(8,128)(2,1)} %bitcast.608, bf16[2,576,3072]{2,1,0:T(8,128)(2,1)} %get-tuple-element.62, f32[2,3072]{1,0:T(2,128)S(1)} %subtract_divide_fusion, f32[2,3072]{1,0:T(2,128)S(1)} %copy-done.71), kind=kLoop, calls=%fused_computation.16 | loop fusion | flops 17694720 | bytes 28360704 | tf_op jit(solution)/shard_map/add | solution.py:853
  1039.5 18.9 %collective-permute-done.72 = bf16[6,24,1536]{2,1,0:T(8,128)(2,1)S(1)} collective-permute-done((bf16[6,24,1536]{2,1,0:T(8,128)(2,1)S(1)}, bf16[6,24,1536]{2,1,0:T(8,128)(2,1)S(1)}, u32[]{:S(2)}, u32[]{:S(2)}) %collective-permute-start.72) | collective-permute-done | bytes 442400 | tf_op jit(solution)/shard_map/ppermute | solution.py:518
  1060.4 10.3 collective-permute-done.73
  1081.4 20.0 %collective-permute-done.105 = bf16[768,768]{1,0:T(8,128)(2,1)S(1)} collective-permute-done((bf16[768,768]{1,0:T(8,128)(2,1)S(1)}, bf16[768,768]{1,0:T(8,128)(2,1)S(1)}, u32[]{:S(2)}, u32[]{:S(2)}) %collective-permute-start.105) | collective-permute-done | bytes 1179680 | tf_op jit(solution)/shard_map/ppermute | solution.py:514
  1108.3 18.5 %collective-permute-done.92 = bf16[384,1536]{1,0:T(8,128)(2,1)S(1)} collective-permute-done((bf16[384,1536]{1,0:T(8,128)(2,1)S(1)}, bf16[384,1536]{1,0:T(8,128)(2,1)S(1)}, u32[]{:S(2)}, u32[]{:S(2)}) %collective-permute-start.92) | collective-permute-done | bytes 1179680 | tf_op jit(solution)/shard_map/ppermute | solution.py:514
  1128.4 28.2 %collective-permute-done.80 = f32[2,4,7536]{2,1,0:T(4,128)S(1)} collective-permute-done((f32[2,4,7536]{2,1,0:T(4,128)S(1)}, f32[2,4,7536]{2,1,0:T(4,128)S(1)}, u32[]{:S(2)}, u32[]{:S(2)}) %collective-permute-start.80) | collective-permute-done | bytes 241184 | tf_op jit(solution)/shard_map/ppermute | solution.py:514
  1166.7 16.0 %collective-permute-done.82 = f32[7536]{0:T(1024)S(1)} collective-permute-done((f32[7536]{0:T(1024)S(1)}, f32[7536]{0:T(1024)S(1)}, u32[]{:S(2)}, u32[]{:S(2)}) %collective-permute-start.82) | collective-permute-done | bytes 30176 | tf_op jit(solution)/shard_map/ppermute | solution.py:518
  1201.2 13.4 %collective-permute-done.88 = bf16[2,48,1536]{2,1,0:T(8,128)(2,1)S(1)} collective-permute-done((bf16[2,48,1536]{2,1,0:T(8,128)(2,1)}, bf16[2,48,1536]{2,1,0:T(8,128)(2,1)S(1)}, u32[]{:S(2)}, u32[]{:S(2)}) %collective-permute-start.88) | collective-permute-done | bytes 294944 | tf_op jit(solution)/shard_map/ppermute | solution.py:518
  1214.6 18.0 %collective-permute-done.89 = bf16[2,48,1536]{2,1,0:T(8,128)(2,1)S(1)} collective-permute-done((bf16[2,48,1536]{2,1,0:T(8,128)(2,1)}, bf16[2,48,1536]{2,1,0:T(8,128)(2,1)S(1)}, u32[]{:S(2)}, u32[]{:S(2)}) %collective-permute-start.89) | collective-permute-done | bytes 294944 | tf_op jit(solution)/shard_map/ppermute | solution.py:518
  1252.5 11.2 collective-permute-done.108
  (994 shorter events, 786.6 us)
Async XLA Ops:
  3.4 82.8 %collective-permute-start.4 = (bf16[6,24,1536]{2,1,0:T(8,128)(2,1)}, bf16[6,24,1536]{2,1,0:T(8,128)(2,1)}, u32[]{:S(2)}, u32[]{:S(2)}) collective-permute-start(bf16[6,24,1536]{2,1,0:T(8,128)(2,1)} %get-tuple-element.145), channel_id=1, source_target_pairs={{0,1},{1,2},{2,3},{3,0},{4,5},{5,6},{6,7},{7,4},{8,9},{9,10},{10,1... | collective-permute-start | bytes 1327112 | tf_op jit(solution)/shard_map/ppermute | solution.py:518
  6.5 82.3 %collective-permute-start.5 = (bf16[6,24,1536]{2,1,0:T(8,128)(2,1)}, bf16[6,24,1536]{2,1,0:T(8,128)(2,1)}, u32[]{:S(2)}, u32[]{:S(2)}) collective-permute-start(bf16[6,24,1536]{2,1,0:T(8,128)(2,1)} %get-tuple-element.147), channel_id=1, source_target_pairs={{0,2},{1,3},{2,0},{3,1},{4,6},{5,7},{6,4},{7,5},{8,10},{9,11},{10,... | collective-permute-start | bytes 1327112 | tf_op jit(solution)/shard_map/ppermute | solution.py:518
  9.1 80.8 %collective-permute-start.6 = (bf16[6,24,1536]{2,1,0:T(8,128)(2,1)}, bf16[6,24,1536]{2,1,0:T(8,128)(2,1)}, u32[]{:S(2)}, u32[]{:S(2)}) collective-permute-start(bf16[6,24,1536]{2,1,0:T(8,128)(2,1)} %get-tuple-element.144), channel_id=1, source_target_pairs={{0,3},{1,0},{2,1},{3,2},{4,7},{5,4},{6,5},{7,6},{8,11},{9,8},{10,9... | collective-permute-start | bytes 1327112 | tf_op jit(solution)/shard_map/ppermute | solution.py:518
  125.5 60.2 %collective-permute-start.20 = (bf16[1,40,1536]{2,1,0:T(8,128)(2,1)}, bf16[1,40,1536]{2,1,0:T(8,128)(2,1)}, u32[]{:S(2)}, u32[]{:S(2)}) collective-permute-start(bf16[1,40,1536]{2,1,0:T(8,128)(2,1)} %bitcast.17), channel_id=1, source_target_pairs={{0,1},{1,2},{2,3},{3,0},{4,5},{5,6},{6,7},{7,4},{8,9},{9,10},{10,1... | collective-permute-start | bytes 368648 | tf_op jit(solution)/shard_map/ppermute | solution.py:518
  157.1 72.0 %collective-permute-start.17 = (bf16[1,192,1536]{2,1,0:T(8,128)(2,1)}, bf16[1,192,1536]{2,1,0:T(8,128)(2,1)}, u32[]{:S(2)}, u32[]{:S(2)}) collective-permute-start(bf16[1,192,1536]{2,1,0:T(8,128)(2,1)} %bitcast.16), channel_id=1, source_target_pairs={{0,1},{1,2},{2,3},{3,0},{4,5},{5,6},{6,7},{7,4},{8,9},{9,10},{10,1... | collective-permute-start | bytes 1769480 | tf_op jit(solution)/shard_map/ppermute | solution.py:518
  175.9 89.1 %collective-permute-start.13 = (bf16[384,3072]{1,0:T(8,128)(2,1)}, bf16[384,3072]{1,0:T(8,128)(2,1)}, u32[]{:S(2)}, u32[]{:S(2)}) collective-permute-start(bf16[384,3072]{1,0:T(8,128)(2,1)} %bitcast.8), channel_id=1, source_target_pairs={{0,8},{4,12},{8,0},{12,4},{16,24},{20,28},{24,16},{28,20},{1,9},{5... | collective-permute-start | bytes 7077896 | tf_op jit(solution)/shard_map/ppermute | solution.py:514
  185.8 76.4 %collective-permute-start.14 = (bf16[384,3072]{1,0:T(8,128)(2,1)}, bf16[384,3072]{1,0:T(8,128)(2,1)}, u32[]{:S(2)}, u32[]{:S(2)}) collective-permute-start(bf16[384,3072]{1,0:T(8,128)(2,1)} %bitcast.8), channel_id=1, source_target_pairs={{0,16},{4,20},{8,24},{12,28},{16,0},{20,4},{24,8},{28,12},{1,17},{... | collective-permute-start | bytes 7077896 | tf_op jit(solution)/shard_map/ppermute | solution.py:514
  204.5 55.0 %collective-permute-start.23 = (bf16[576,1536]{1,0:T(8,128)(2,1)}, bf16[576,1536]{1,0:T(8,128)(2,1)}, u32[]{:S(2)}, u32[]{:S(2)}) collective-permute-start(bf16[576,1536]{1,0:T(8,128)(2,1)} %get-tuple-element.107), channel_id=1, source_target_pairs={{0,4},{4,0},{8,12},{12,8},{16,20},{20,16},{24,28},{28,24},{1,5},{5... | collective-permute-start | bytes 5308424 | tf_op jit(solution)/shard_map/ppermute | solution.py:514
  336.1 63.2 %collective-permute-start.27 = (bf16[768,1536]{1,0:T(8,128)(2,1)S(1)}, bf16[768,1536]{1,0:T(8,128)(2,1)S(1)}, u32[]{:S(2)}, u32[]{:S(2)}) collective-permute-start(bf16[768,1536]{1,0:T(8,128)(2,1)S(1)} %bitcast.636), channel_id=1, source_target_pairs={{0,8},{4,12},{8,0},{12,4},{16,24},{20,28},{24,16},{28,20},{1,9},{5... | collective-permute-start | bytes 7077896 | tf_op jit(solution)/shard_map/ppermute | solution.py:514
  339.3 58.9 %collective-permute-start.28 = (bf16[768,1536]{1,0:T(8,128)(2,1)S(1)}, bf16[768,1536]{1,0:T(8,128)(2,1)S(1)}, u32[]{:S(2)}, u32[]{:S(2)}) collective-permute-start(bf16[768,1536]{1,0:T(8,128)(2,1)S(1)} %bitcast.637), channel_id=1, source_target_pairs={{0,16},{4,20},{8,24},{12,28},{16,0},{20,4},{24,8},{28,12},{1,17},{... | collective-permute-start | bytes 7077896 | tf_op jit(solution)/shard_map/ppermute | solution.py:514
  490.3 56.7 %collective-permute-start.55 = (bf16[192,1536]{1,0:T(8,128)(2,1)S(1)}, bf16[192,1536]{1,0:T(8,128)(2,1)}, u32[]{:S(2)}, u32[]{:S(2)}) collective-permute-start(bf16[192,1536]{1,0:T(8,128)(2,1)S(1)} %bitcast.696), channel_id=1, source_target_pairs={{0,8},{4,12},{8,0},{12,4},{16,24},{20,28},{24,16},{28,20},{1,9},{5... | collective-permute-start | bytes 1769480 | tf_op jit(solution)/shard_map/ppermute | solution.py:514
  491.6 54.1 %collective-permute-start.56 = (bf16[192,1536]{1,0:T(8,128)(2,1)S(1)}, bf16[192,1536]{1,0:T(8,128)(2,1)}, u32[]{:S(2)}, u32[]{:S(2)}) collective-permute-start(bf16[192,1536]{1,0:T(8,128)(2,1)S(1)} %bitcast.697), channel_id=1, source_target_pairs={{0,16},{4,20},{8,24},{12,28},{16,0},{20,4},{24,8},{28,12},{1,17},{... | collective-permute-start | bytes 1769480 | tf_op jit(solution)/shard_map/ppermute | solution.py:514
  562.5 99.1 %collective-permute-start.59 = (bf16[576,1536]{1,0:T(8,128)(2,1)}, bf16[576,1536]{1,0:T(8,128)(2,1)}, u32[]{:S(2)}, u32[]{:S(2)}) collective-permute-start(bf16[576,1536]{1,0:T(8,128)(2,1)} %convolution_convert_fusion.1), channel_id=1, source_target_pairs={{0,4},{4,0},{8,12},{12,8},{16,20},{20,16},{24,28},{28,24},{1,5},{5... | collective-permute-start | bytes 5308424 | tf_op jit(solution)/shard_map/ppermute | solution.py:514
  907.2 167.8 %collective-permute-start.98 = (bf16[768,768]{1,0:T(8,128)(2,1)}, bf16[768,768]{1,0:T(8,128)(2,1)}, u32[]{:S(2)}, u32[]{:S(2)}) collective-permute-start(bf16[768,768]{1,0:T(8,128)(2,1)} %fusion.110), channel_id=1, source_target_pairs={{0,8},{4,12},{8,0},{12,4},{16,24},{20,28},{24,16},{28,20},{1,9},{5... | collective-permute-start | bytes 3538952 | tf_op jit(solution)/shard_map/ppermute | solution.py:514
  913.1 63.3 %collective-permute-start.99 = (bf16[768,768]{1,0:T(8,128)(2,1)}, bf16[768,768]{1,0:T(8,128)(2,1)}, u32[]{:S(2)}, u32[]{:S(2)}) collective-permute-start(bf16[768,768]{1,0:T(8,128)(2,1)} %fusion.116), channel_id=1, source_target_pairs={{0,8},{4,12},{8,0},{12,4},{16,24},{20,28},{24,16},{28,20},{1,9},{5... | collective-permute-start | bytes 3538952 | tf_op jit(solution)/shard_map/ppermute | solution.py:514
  914.0 67.6 %collective-permute-start.104 = (bf16[768,768]{1,0:T(8,128)(2,1)S(1)}, bf16[768,768]{1,0:T(8,128)(2,1)}, u32[]{:S(2)}, u32[]{:S(2)}) collective-permute-start(bf16[768,768]{1,0:T(8,128)(2,1)S(1)} %copy-done.123), channel_id=1, source_target_pairs={{0,16},{4,20},{8,24},{12,28},{16,0},{20,4},{24,8},{28,12},{1,17},{... | collective-permute-start | bytes 3538952 | tf_op jit(solution)/shard_map/ppermute | solution.py:514
  981.6 98.7 %collective-permute-start.106 = (bf16[768,768]{1,0:T(8,128)(2,1)}, bf16[768,768]{1,0:T(8,128)(2,1)}, u32[]{:S(2)}, u32[]{:S(2)}) collective-permute-start(bf16[768,768]{1,0:T(8,128)(2,1)} %fusion.113), channel_id=1, source_target_pairs={{0,16},{4,20},{8,24},{12,28},{16,0},{20,4},{24,8},{28,12},{1,17},{... | collective-permute-start | bytes 3538952 | tf_op jit(solution)/shard_map/ppermute | solution.py:514
  989.7 118.5 %collective-permute-start.93 = (bf16[384,1536]{1,0:T(8,128)(2,1)}, bf16[384,1536]{1,0:T(8,128)(2,1)}, u32[]{:S(2)}, u32[]{:S(2)}) collective-permute-start(bf16[384,1536]{1,0:T(8,128)(2,1)} %convolution_convert_fusion.7), channel_id=1, source_target_pairs={{0,16},{4,20},{8,24},{12,28},{16,0},{20,4},{24,8},{28,12},{1,17},{... | collective-permute-start | bytes 3538952 | tf_op jit(solution)/shard_map/ppermute | solution.py:514
  995.3 79.9 %collective-permute-start.100 = (bf16[768,768]{1,0:T(8,128)(2,1)}, bf16[768,768]{1,0:T(8,128)(2,1)}, u32[]{:S(2)}, u32[]{:S(2)}) collective-permute-start(bf16[768,768]{1,0:T(8,128)(2,1)} %add_convert_fusion.2), channel_id=1, source_target_pairs={{0,16},{4,20},{8,24},{12,28},{16,0},{20,4},{24,8},{28,12},{1,17},{... | collective-permute-start | bytes 3538952 | tf_op jit(solution)/shard_map/ppermute | solution.py:514
  1075.2 90.3 %collective-permute-start.85 = (bf16[384,1536]{1,0:T(8,128)(2,1)S(1)}, bf16[384,1536]{1,0:T(8,128)(2,1)S(1)}, u32[]{:S(2)}, u32[]{:S(2)}) collective-permute-start(bf16[384,1536]{1,0:T(8,128)(2,1)S(1)} %copy-done.119), channel_id=1, source_target_pairs={{0,8},{4,12},{8,0},{12,4},{16,24},{20,28},{24,16},{28,20},{1,9},{5... | collective-permute-start | bytes 3538952 | tf_op jit(solution)/shard_map/ppermute | solution.py:514
  1080.3 85.3 %collective-permute-start.87 = (bf16[384,1536]{1,0:T(8,128)(2,1)S(1)}, bf16[384,1536]{1,0:T(8,128)(2,1)S(1)}, u32[]{:S(2)}, u32[]{:S(2)}) collective-permute-start(bf16[384,1536]{1,0:T(8,128)(2,1)S(1)} %copy-done.120), channel_id=1, source_target_pairs={{0,16},{4,20},{8,24},{12,28},{16,0},{20,4},{24,8},{28,12},{1,17},{... | collective-permute-start | bytes 3538952 | tf_op jit(solution)/shard_map/ppermute | solution.py:514
  1101.5 55.2 %collective-permute-start.80 = (f32[2,4,7536]{2,1,0:T(4,128)S(1)}, f32[2,4,7536]{2,1,0:T(4,128)S(1)}, u32[]{:S(2)}, u32[]{:S(2)}) collective-permute-start(f32[2,4,7536]{2,1,0:T(4,128)S(1)} %pad_maximum_fusion.8), channel_id=1, source_target_pairs={{0,8},{4,12},{8,0},{12,4},{16,24},{20,28},{24,16},{28,20},{1,9},{5... | collective-permute-start | bytes 723464 | tf_op jit(solution)/shard_map/ppermute | solution.py:514
  1190.0 56.1 %collective-permute-start.101 = (bf16[1,192,768]{2,1,0:T(8,128)(2,1)}, bf16[1,192,768]{2,1,0:T(8,128)(2,1)}, u32[]{:S(2)}, u32[]{:S(2)}) collective-permute-start(bf16[1,192,768]{2,1,0:T(8,128)(2,1)} %get-tuple-element.114), channel_id=1, source_target_pairs={{0,1},{1,2},{2,3},{3,0},{4,5},{5,6},{6,7},{7,4},{8,9},{9,10},{10,1... | collective-permute-start | bytes 884744 | tf_op jit(solution)/shard_map/ppermute | solution.py:518
  1190.0 57.3 %collective-permute-start.102 = (bf16[1,192,768]{2,1,0:T(8,128)(2,1)}, bf16[1,192,768]{2,1,0:T(8,128)(2,1)}, u32[]{:S(2)}, u32[]{:S(2)}) collective-permute-start(bf16[1,192,768]{2,1,0:T(8,128)(2,1)} %get-tuple-element.116), channel_id=1, source_target_pairs={{0,2},{1,3},{2,0},{3,1},{4,6},{5,7},{6,4},{7,5},{8,10},{9,11},{10,... | collective-permute-start | bytes 884744 | tf_op jit(solution)/shard_map/ppermute | solution.py:518
  (262 other events, 5804.8 us)

commit v3 on v2

--- a/solution.py
+++ b/solution.py
@@ -574,20 +574,21 @@
     return full.reshape(-1, line.shape[1])
 
 
-def reduce_owner(piece, parts, plane, place):
+def reduce_owner(pieces, parts, plane, place):
     low = jnp.bfloat16
-    far = [piece(plane ^ 3, half).astype(low) for half in range(2)]
+    first, second, last = pieces
+    far = [first(plane ^ 3, half).astype(low) for half in range(2)]
     via_x, via_y = (swap(far[0], 2), swap(far[1], 4))
-    out_x = [piece(plane ^ 1, 0).astype(low), None]
-    out_y = [None, piece(plane ^ 2, 1).astype(low)]
+    out_x = [second(plane ^ 1, 0).astype(low), None]
+    out_y = [None, second(plane ^ 2, 1).astype(low)]
     got_x, got_y = ([swap(out_x[0], 2), None], [None, swap(out_y[1], 4)])
-    out_x[1] = (piece(plane ^ 1, 1) + via_y.astype(jnp.float32)).astype(low)
-    out_y[0] = (piece(plane ^ 2, 0) + via_x.astype(jnp.float32)).astype(low)
+    out_x[1] = (second(plane ^ 1, 1) + via_y.astype(jnp.float32)).astype(low)
+    out_y[0] = (second(plane ^ 2, 0) + via_x.astype(jnp.float32)).astype(low)
     got_x[1], got_y[0] = (swap(out_x[1], 2), swap(out_y[0], 4))
     results = []
     for half in range(2):
         total = (
-            piece(plane, half)
+            last(plane, half)
             + got_x[half].astype(jnp.float32)
             + got_y[half].astype(jnp.float32)
         )
@@ -691,18 +692,14 @@
     f32, low = (jnp.float32, jnp.bfloat16)
 
     small = jnp.concatenate(
-        [conv_weight.reshape(-1), vectors.reshape(-1), hidden_vecs.reshape(-1)]
-    )
-    small_all = gather_small(small, plane, core, place).astype(f32)
+        [
+            conv_weight.reshape(-1),
+            vectors.reshape(-1),
+            hidden_vecs.reshape(-1),
+            time_weight.reshape(-1),
+        ]
+    )
     col_rows, col_width = (9 + vectors.shape[0], conv_weight.shape[1])
-    col_all = small_all[..., : col_rows * col_width]
-    col_all = col_all.reshape(LINE, PLANE, 2, col_rows, col_width).transpose(3, 1, 2, 0, 4)
-    col_all = col_all.reshape(col_rows, channels)
-    taps, vecs = (col_all[:9], col_all[9:])
-    hidden_all = pick(small_all[..., col_rows * col_width :], core, 2)
-    hidden_all = hidden_all.reshape(LINE, PLANE, 3, -1).transpose(2, 1, 0, 3)
-    hidden_all = hidden_all.reshape(3, half_hidden)
-
     def with_partner(value, axis):
         kept = core_half(value, axis, core)
         got = swap(core_half(value, axis, 1 - core), 1)
@@ -718,26 +715,26 @@
         return groups.reshape(groups.shape[:-2] + (-1,))
 
     up_shard = with_partner(up_weight, 1)
-    attn_shard = attn_order(jnp.moveaxis(with_partner(attn_in, 2), 1, 0))
-
-    latent = spread_line(latents, place).reshape(height, columns, channels)
+    up_shard, small, latents_held = held(up_shard, small, latents)
+    latent = spread_line(latents_held, place).reshape(height, columns, channels)
     up_line = flat_line(up_shard, place)
-    up_line, latent, down_shard, map_shard, time_shard = held(
-        up_line, latent, down_weight[None], map_weight[None], time_weight
+    small_all = gather_small(small, plane, core, place)
+    up_line, latent, small_all, clip_text, attn_in, embedding = held(
+        up_line, latent, small_all, clip_text, attn_in, embedding
     )
     up_full = flat_plane(up_line, plane)
-    down_line = flat_line(down_shard, place)
-    map_line = flat_line(map_shard, place)
-    time_all = gather_small(time_shard, plane, core, place).transpose(3, 1, 2, 0, 4)
-    time_all = time_all.reshape(time_rank, 2 * channels)
-    clip_own = pick(clip_text, place).astype(f32)
-    words_own = jax.nn.silu(clip_own).astype(low)
-    text_pad = -(-text_len // 16) * 16
-    words_own = jnp.pad(words_own, ((0, text_pad - text_len), (0, 0)))
-    words = pair(words_own).reshape(2 * text_pad, clip_width)
-    words_half = core_half(words, 1, core)
-    lengths_two = pair(pick(lengths, place))
-    embed_own = pick(embedding, place)
+    small_all, time_low = (small_all.astype(f32), small_all)
+    col_all = small_all[..., : col_rows * col_width]
+    col_all = col_all.reshape(LINE, PLANE, 2, col_rows, col_width).transpose(3, 1, 2, 0, 4)
+    col_all = col_all.reshape(col_rows, channels)
+    taps, vecs = (col_all[:9], col_all[9:])
+    time_at = col_rows * col_width + hidden_vecs.size
+    hidden_all = pick(small_all[..., col_rows * col_width : time_at], core, 2)
+    hidden_all = hidden_all.reshape(LINE, PLANE, 3, -1).transpose(2, 1, 0, 3)
+    hidden_all = hidden_all.reshape(3, half_hidden)
+
+    time_all = time_low[..., time_at:].reshape(LINE, PLANE, 2, time_rank, -1)
+    time_all = time_all.transpose(3, 1, 2, 0, 4).reshape(time_rank, 2 * channels)
 
     framed = jnp.pad(latent, ((1, 1), (1, 1), (0, 0)))
     conv_out = jnp.broadcast_to(vecs[0], latent.shape)
@@ -748,12 +745,15 @@
         ].astype(f32)
     first_norm, first_inv = norm_parts(conv_out.reshape(pixels, channels))
     first_in = pair(first_norm.astype(low)).reshape(2 * pixels, channels)
-    up_full, down_line, map_line, first_in, words_half, attn_shard = held(
-        up_full, down_line, map_line, first_in, words_half, attn_shard
+    first_in, down_shard, mixed_shard = held(
+        first_in, down_weight[None], jnp.concatenate([map_weight, out_weight])[None]
+    )
+    down_line = flat_line(down_shard, place)
+    mixed_line = flat_line(mixed_shard, place)
+    up_full, down_line, mixed_line, first_in, attn_in, clip_text = held(
+        up_full, down_line, mixed_line, first_in, attn_in, clip_text
     )
     down_full = flat_plane(down_line, plane)
-    map_full = flat_plane(map_line, plane)
-    attn_line = flat_line(attn_shard, place)
     up_out = product(first_in, up_full) + hidden_all[0]
     below = 0.5 + 0.5 * lax.erf(up_out * 0.5**0.5)
     slope = below + up_out * ((0.5 / jnp.pi) ** 0.5 * jnp.exp(-0.5 * up_out * up_out))
@@ -767,25 +767,38 @@
     grn_out = (
         gamma_vec * (active_lat * grn_ratio[:, None]) + hidden_all[2] + active_lat
     ).astype(low)
-    grn_out, down_full, map_full, attn_line, out_shard = held(
-        grn_out, down_full, map_full, attn_line, out_weight[None]
-    )
+    grn_out, attn_in = held(grn_out, attn_in)
+    attn_shard = attn_order(jnp.moveaxis(with_partner(attn_in, 2), 1, 0))
+    attn_line = flat_line(attn_shard, place)
+    grn_out, down_full, attn_line, mixed_line, clip_text = held(
+        grn_out, down_full, attn_line, mixed_line, clip_text
+    )
+    mixed_full = flat_plane(mixed_line, plane).reshape(PLANE * LINE, -1, channels)
+    map_rows = map_weight.shape[0]
+    map_full = mixed_full[:, :map_rows].reshape(-1, channels)
+    out_full = mixed_full[:, map_rows:].reshape(-1, channels)
     attn_full = flat_plane(attn_line, plane)
-    out_line = flat_line(out_shard, place)
     lowered = own_sum(product(grn_out[0], down_full), product(grn_out[1], down_full))
     first_sum = latent.reshape(pixels, channels).astype(f32) + (lowered + vecs[1])
+    embed_own = pick(embedding, place)
     modulation = product(embed_own[None], time_all)[0]
     scale_vec = modulation[:channels] + vecs[2]
     shift_vec = modulation[channels:] + vecs[3]
     second = first_sum * (1.0 + scale_vec) + shift_vec
     second_norm, second_inv = norm_parts(second)
+    clip_own = pick(clip_text, place).astype(f32)
+    words_own = jax.nn.silu(clip_own).astype(low)
+    text_pad = -(-text_len // 16) * 16
+    words_own = jnp.pad(words_own, ((0, text_pad - text_len), (0, 0)))
+    words = pair(words_own).reshape(2 * text_pad, clip_width)
+    words_half = core_half(words, 1, core)
+    lengths_two = pair(pick(lengths, place))
     mapped = pair_sum(product(words_half, map_full).reshape(2, text_pad, channels))
     mapped = (mapped + vecs[4]).astype(low)
     sources = jnp.concatenate([pair(second_norm.astype(low)), mapped], axis=1)
     keys = pixels + text_pad
-    sources, attn_full, out_line, grad_shard = held(sources, attn_full, out_line, grad_out)
+    sources, attn_full, out_full, grad_shard = held(sources, attn_full, out_full, grad_out)
     sources = sources.reshape(2 * keys, channels)
-    out_full = flat_plane(out_line, plane)
     grad_own = spread_line(grad_shard, place).reshape(pixels, channels)
     bias = jnp.stack([vecs[5], jnp.zeros((channels,), f32), vecs[6]])
     bias = attn_order(core_half(bias, 1, core))
@@ -794,42 +807,41 @@
     mixed, log_totals = attend(rows_qkv, lengths_two, pixels)
     attended = own_sum(product(mixed[0], out_full), product(mixed[1], out_full))
     layer_own = (second + (attended + vecs[7])).astype(low)
-    layer_out = spread_line(layer_own.reshape(latents.shape), place)
-
     grad_two = pair(grad_own)
     g_mixed = product_nt(grad_two.reshape(2 * pixels, channels), out_full).astype(low)
     g_mixed = g_mixed.reshape(2, pixels, half_channels)
 
-    def owner_sums(left, right, parts):
+    def owner_sums(left, right, parts, *gates):
         block = left.shape[1] // PLANE
         half = right.shape[1] // 2
 
-        def piece(chip, which):
-            cut = lax.dynamic_slice_in_dim(left, chip * block, block, 1)
-            return product_tn(cut, right[:, which * half : (which + 1) * half])
-
-        return reduce_owner(piece, parts, plane, place)
-
-    out_grad = owner_sums(
-        mixed.reshape(2 * pixels, half_channels), grad_two.reshape(2 * pixels, channels), 1
-    )[0]
+        def pieces_of(left_op, right_op):
+            def piece(chip, which):
+                taken = lax.dynamic_slice_in_dim(left_op, chip * block, block, 1)
+                return product_tn(taken, right_op[:, which * half : (which + 1) * half])
+
+            return piece
+
+        pieces = [pieces_of(left, right)]
+        for gate in gates:
+            left, right, _ = held(left, right, gate)
+            pieces.append(pieces_of(left, right))
+        pieces += [pieces[-1]] * (3 - len(pieces))
+        return reduce_owner(pieces, parts, plane, place)
+
     g_rows = attend_back_pairs(rows_qkv, g_mixed, log_totals, lengths_two, pixels)
     g_second_in = own_sum(
         product_nt(g_rows[0, :pixels], attn_full), product_nt(g_rows[1, :pixels], attn_full)
     )
-    g_text = g_rows[:, pixels:].reshape(2 * text_pad, 3 * half_channels)
-    g_mapped = pair_sum(product_nt(g_text, attn_full).reshape(2, text_pad, channels))
-    g_mapped = g_mapped.astype(low).reshape(2 * text_pad, channels)
+    out_grad = owner_sums(
+        mixed.reshape(2 * pixels, half_channels),
+        grad_two.reshape(2 * pixels, channels),
+        1,
+        g_rows,
+        g_second_in,
+    )[0]
+    g_second_in, g_rows = held(g_second_in, g_rows)
     g_flat = g_rows.reshape(2 * keys, 3 * half_channels)
-    attn_grad = owner_sums(sources, g_flat, 2)
-    map_grad = owner_sums(words_half, g_mapped, 1)[0]
-    g_words = product_nt(g_mapped, map_full).reshape(2, text_pad, -1)[:, :text_len]
-    g_words = core_merge(g_words[0], swap(g_words[1], 1), 1, core)
-    sigmoid_text = jax.nn.sigmoid(clip_own)
-    text_own = (g_words * (sigmoid_text * (1.0 + clip_own * (1.0 - sigmoid_text)))).astype(low)
-    text_own = text_own.reshape(text_len, LINE, clip_width // LINE).transpose(1, 0, 2)
-    text_grad = spread_line(text_own, place)
-
     grad_float = grad_own.astype(f32)
     g_second = grad_float + norm_back(g_second_in, second_norm, second_inv)
     g_scale = jnp.sum(g_second * first_sum, axis=0)
@@ -839,11 +851,11 @@
     g_first = g_second * (1.0 + scale_vec)
     g_down_own = g_first.astype(low)
     g_down = pair(g_down_own).reshape(2 * pixels, channels)
-    down_grad = owner_sums(grn_out.reshape(2 * pixels, half_hidden), g_down, 1)[0]
     g_grn = product_nt(g_down, down_full).reshape(2, pixels, half_hidden)
     g_grn_active = jnp.sum(g_grn * active_lat, axis=1)
     g_grn_sum = jnp.sum(g_grn, axis=(0, 1))
     g_grn, g_grn_active, grad_beta = held(g_grn.astype(low), g_grn_active, g_grn_sum)
+    g_grn_low = g_grn
     g_grn = g_grn.astype(f32)
     grad_gamma = jnp.sum(g_grn_active * grn_ratio, axis=0)
     g_ratio = g_grn_active * gamma_vec
@@ -854,11 +866,27 @@
         + active_lat * (g_strength / strength)[:, None]
     )
     g_up = (g_active.reshape(2 * pixels, half_hidden) * slope.astype(f32)).astype(low)
+    attn_grad = owner_sums(sources, g_flat, 2, g_down, g_grn_low)
+    down_grad = owner_sums(
+        grn_out.reshape(2 * pixels, half_hidden), g_down, 1, g_grn_low, g_up
+    )[0]
+    layer_own, g_text, _ = held(layer_own, g_rows[:, pixels:], g_down)
+    layer_out = spread_line(layer_own.reshape(latents.shape), place)
+    g_text = g_text.reshape(2 * text_pad, 3 * half_channels)
+    g_mapped = pair_sum(product_nt(g_text, attn_full).reshape(2, text_pad, channels))
+    g_mapped = g_mapped.astype(low).reshape(2 * text_pad, channels)
+    map_grad = owner_sums(words_half, g_mapped, 1, g_grn_low, g_up)[0]
+    g_words = product_nt(g_mapped, map_full).reshape(2, text_pad, -1)[:, :text_len]
+    g_words = core_merge(g_words[0], swap(g_words[1], 1), 1, core)
+    sigmoid_text = jax.nn.sigmoid(clip_own)
+    text_own = (g_words * (sigmoid_text * (1.0 + clip_own * (1.0 - sigmoid_text)))).astype(low)
+    text_own = text_own.reshape(text_len, LINE, clip_width // LINE).transpose(1, 0, 2)
+    text_grad = spread_line(text_own, place)
     g_first_in = own_sum(
         product_nt(g_up[:pixels], up_full), product_nt(g_up[pixels:], up_full)
     )
     g_conv = norm_back(g_first_in, first_norm, first_inv).astype(low).reshape(latent.shape)
-    up_grad = owner_sums(first_in, g_up, 2)
+    up_grad = owner_sums(first_in, g_up, 2, g_conv)
     g_framed = jnp.pad(g_conv, ((1, 1), (1, 1), (0, 0)))
     g_conv_f = g_conv.astype(f32)
     back_sum = g_first.reshape(latent.shape)

time: 1290 us -> 1310 us (1.016)
  other arithmetic: 106 us -> 133 us
  local copies, waits for them, and re-layouts: 218 us -> 195 us
  waiting for transfers between devices: 445 us -> 467 us
    ppermute x69 -> x63, waiting for transfers between devices: 208 us -> 267 us  [rotate(): lax.ppermute(value, 'band', [(i, (i + step) % LINE) for i in range(LINE)])]
    ppermute x78 -> x71, waiting for transfers between devices: 238 us -> 200 us  [swap(): return lax.ppermute(value, 'dp', [(i, i ^ bit) for i in range(2 * PLANE)])]
    dynamic_update_slice x75 -> x58, local copies, waits for them, and re-layouts: 89.4 us -> 55.2 us  [put(): return lax.dynamic_update_index_in_dim(buffer, value, index, axis)]
    ppermute x69 -> x63, starting transfers between devices: 137 us -> 147 us  [rotate(): lax.ppermute(value, 'band', [(i, (i + step) % LINE) for i in range(LINE)])]
    ppermute x78 -> x71, starting transfers between devices: 65.1 us -> 56.5 us  [swap(): return lax.ppermute(value, 'dp', [(i, i ^ bit) for i in range(2 * PLANE)])]
  transfers between devices with their start and end apart: 147 -> 134, of which waited for: 54 -> 47; matrix products, arithmetic and copies ran while one was open for 38% -> 39% of each run, Pallas kernels for 6% -> 2%
where the time goes in v3:
time: 1310 us; the launch traced here: 1300 us
  waiting for transfers between devices  467 us (36%)
  matrix products  225 us (17%)
  starting transfers between devices  204 us (16%)
  local copies, waits for them, and re-layouts  195 us (15%)
  other arithmetic  133 us (10%)
  Pallas kernels  76.5 us (6%)
    ppermute x63, waiting for transfers between devices, rotate(): lax.ppermute(value, 'band', [(i, (i + step) % LINE) for i in range(LINE)])  267 us
    ppermute x71, waiting for transfers between devices, swap(): return lax.ppermute(value, 'dp', [(i, i ^ bit) for i in range(2 * PLANE)])  200 us
    ppermute x63, starting transfers between devices, rotate(): lax.ppermute(value, 'band', [(i, (i + step) % LINE) for i in range(LINE)])  147 us
    dot_general x40, matrix products, product_tn(): lax.dot_general(left_op, right_op, (((0,), (0,)), ((), ())), preferred_el...  101 us
    dot_general x8, matrix products, product(): return jnp.dot(left_op, right_op, preferred_element_type=jnp.float32)  63.8 us
    dot_general x8, matrix products, product_nt(): lax.dot_general(left_op, right_op, (((1,), (1,)), ((), ())), preferred_el...  60.4 us
    ppermute x71, starting transfers between devices, swap(): return lax.ppermute(value, 'dp', [(i, i ^ bit) for i in range(2 * PLANE)])  56.5 us
    dynamic_update_slice x58, local copies, waits for them, and re-layouts, put(): return lax.dynamic_update_index_in_dim(buffer, value, index, axis)  55.2 us
  transfers between devices with their start and end apart: 134, of which 47 were waited for; matrix products, arithmetic and copies ran while one was open for 39% of the time, Pallas kernels for 2%

profile of v3, /device:TPU:0, one launch (start us, length us, event | category | flops | bytes accessed | tf_op | source)
XLA Modules:
  0.0 1304.0 jit_solution(13416646787009495716)
XLA Ops:
  41.8 26.1 %collective-permute-done.10 = bf16[4,2,7536]{2,1,0:T(2,128)(2,1)S(1)} collective-permute-done((bf16[4,2,7536]{2,1,0:T(2,128)(2,1)S(1)}, bf16[4,2,7536]{2,1,0:T(2,128)(2,1)S(1)}, u32[]{:S(2)}, u32[]{:S(2)}) %collective-permute-start.10) | collective-permute-done | bytes 120608 | tf_op jit(solution)/shard_map/ppermute | solution.py:518
  67.9 14.6 %collective-permute-start.11 = (bf16[4,2,7536]{2,1,0:T(2,128)(2,1)S(1)}, bf16[4,2,7536]{2,1,0:T(2,128)(2,1)S(1)}, u32[]{:S(2)}, u32[]{:S(2)}) collective-permute-start(bf16[4,2,7536]{2,1,0:T(2,128)(2,1)S(1)} %constant_dynamic-update-slice_fusion), channel_id=1, source_target_pairs={{0,2},{1,3},{2,0},{3,1},{4,6},{5,7},{6,4},{7,5},{8,10},{9,11},{10,... | collective-permute-start | bytes 361736 | tf_op jit(solution)/shard_map/ppermute | solution.py:518
  105.8 18.8 %collective-permute-done.5 = bf16[6,24,1536]{2,1,0:T(8,128)(2,1)S(1)} collective-permute-done((bf16[6,24,1536]{2,1,0:T(8,128)(2,1)}, bf16[6,24,1536]{2,1,0:T(8,128)(2,1)S(1)}, u32[]{:S(2)}, u32[]{:S(2)}) %collective-permute-start.5) | collective-permute-done | bytes 442400 | tf_op jit(solution)/shard_map/ppermute | solution.py:518
  177.2 17.8 %collective-permute-done.21 = bf16[1,88,1536]{2,1,0:T(8,128)(2,1)S(1)} collective-permute-done((bf16[1,88,1536]{2,1,0:T(8,128)(2,1)S(1)}, bf16[1,88,1536]{2,1,0:T(8,128)(2,1)S(1)}, u32[]{:S(2)}, u32[]{:S(2)}) %collective-permute-start.21) | collective-permute-done | bytes 270368 | tf_op jit(solution)/shard_map/ppermute | solution.py:518
  199.2 14.2 %collective-permute-start.18 = (bf16[1,192,1536]{2,1,0:T(8,128)(2,1)S(1)}, bf16[1,192,1536]{2,1,0:T(8,128)(2,1)S(1)}, u32[]{:S(2)}, u32[]{:S(2)}) collective-permute-start(bf16[1,192,1536]{2,1,0:T(8,128)(2,1)S(1)} %bitcast.699), channel_id=1, source_target_pairs={{0,1},{1,2},{2,3},{3,0},{4,5},{5,6},{6,7},{7,4},{8,9},{9,10},{10,1... | collective-permute-start | bytes 1769480 | tf_op jit(solution)/shard_map/ppermute | solution.py:518
  217.5 26.1 %collective-permute-done.18 = bf16[1,192,1536]{2,1,0:T(8,128)(2,1)S(1)} collective-permute-done((bf16[1,192,1536]{2,1,0:T(8,128)(2,1)S(1)}, bf16[1,192,1536]{2,1,0:T(8,128)(2,1)S(1)}, u32[]{:S(2)}, u32[]{:S(2)}) %collective-permute-start.18) | collective-permute-done | bytes 589856 | tf_op jit(solution)/shard_map/ppermute | solution.py:518
  243.6 22.6 %collective-permute-done.19 = bf16[1,192,1536]{2,1,0:T(8,128)(2,1)S(1)} collective-permute-done((bf16[1,192,1536]{2,1,0:T(8,128)(2,1)S(1)}, bf16[1,192,1536]{2,1,0:T(8,128)(2,1)S(1)}, u32[]{:S(2)}, u32[]{:S(2)}) %collective-permute-start.19) | collective-permute-done | bytes 589856 | tf_op jit(solution)/shard_map/ppermute | solution.py:518
  274.2 20.6 %collective-permute-done.15 = bf16[192,3072]{1,0:T(8,128)(2,1)S(1)} collective-permute-done((bf16[192,3072]{1,0:T(8,128)(2,1)S(1)}, bf16[192,3072]{1,0:T(8,128)(2,1)S(1)}, u32[]{:S(2)}, u32[]{:S(2)}) %collective-permute-start.15) | collective-permute-done | bytes 1179680 | tf_op jit(solution)/shard_map/ppermute | solution.py:514
  304.8 28.1 %fusion.4 = (bf16[1152,3072]{1,0:T(8,128)(2,1)}, bf16[1152,3072]{1,0:T(8,128)(2,1)S(1)}) fusion(f32[3072]{0:T(1024)S(1)} %copy-done.114, bf16[1152,1536]{1,0:T(8,128)(2,1)S(1)} %bitcast.661, bf16[1536,3072]{1,0:T(8,128)(2,1)S(1)} %bitcast.609), kind=kOutput, calls=%fused_computation.10 | convolution fusion | flops 10914103296 | bytes 27144192 | tf_op jit(solution)/shard_map/dot_general | solution.py:27
  361.5 26.4 %collective-permute-done.30 = bf16[2,48,2304]{2,1,0:T(8,128)(2,1)S(1)} collective-permute-done((bf16[2,48,2304]{2,1,0:T(8,128)(2,1)}, bf16[2,48,2304]{2,1,0:T(8,128)(2,1)S(1)}, u32[]{:S(2)}, u32[]{:S(2)}) %collective-permute-start.30) | collective-permute-done | bytes 442400 | tf_op jit(solution)/shard_map/ppermute | solution.py:518
  409.2 17.5 %collective-permute-done.27 = bf16[384,1536]{1,0:T(8,128)(2,1)S(1)} collective-permute-done((bf16[384,1536]{1,0:T(8,128)(2,1)S(1)}, bf16[384,1536]{1,0:T(8,128)(2,1)S(1)}, u32[]{:S(2)}, u32[]{:S(2)}) %collective-permute-start.27) | collective-permute-done | bytes 1179680 | tf_op jit(solution)/shard_map/ppermute | solution.py:514
  466.3 38.1 %collective-permute-done.39 = bf16[176,1536]{1,0:T(8,128)(2,1)S(1)} collective-permute-done((bf16[176,1536]{1,0:T(8,128)(2,1)S(1)}, bf16[176,1536]{1,0:T(8,128)(2,1)S(1)}, u32[]{:S(2)}, u32[]{:S(2)}) %collective-permute-start.39) | collective-permute-done | bytes 540704 | tf_op jit(solution)/shard_map/ppermute | solution.py:514
  529.8 14.3 %collective-permute-done.44 = bf16[192,2304]{1,0:T(8,128)(2,1)S(1)} collective-permute-done((bf16[192,2304]{1,0:T(8,128)(2,1)S(1)}, bf16[192,2304]{1,0:T(8,128)(2,1)S(1)}, u32[]{:S(2)}, u32[]{:S(2)}) %collective-permute-start.44) | collective-permute-done | bytes 884768 | tf_op jit(solution)/shard_map/ppermute | solution.py:514
  567.9 29.1 %attend.1 = (bf16[2,576,768]{2,1,0:T(8,128)(2,1)S(1)}, f32[2,6,2,576]{3,2,1,0:T(2,128)S(1)}) custom-call(s32[2]{0:T(128)S(1)} %pad_add_fusion.length_ref, bf16[2,656,2304]{2,1,0:T(8,128)(2,1)S(1)} %bitcast.564), custom_call_target="tpu_custom_call" | custom-call | flops 4643094528 | bytes 9068544 | tf_op jit(solution)/shard_map/attend/pallas_call | solution.py:468
  620.9 47.4 %attend_back.1 = bf16[2,656,2304]{2,1,0:T(8,128)(2,1)S(1)} custom-call(s32[2]{0:T(128)S(1)} %pad_add_fusion.length_ref, bf16[2,656,2304]{2,1,0:T(8,128)(2,1)S(1)} %bitcast.567, bf16[2,576,768]{2,1,0:T(8,128)(2,1)S(1)} %bitcast.568, f32[2,6,2,576]{3,2,1,0:T(2,128)S(1)} %get-tuple-element.101.log_ref), custom_call_target="tpu_custom_call" | custom-call | flops 11607736320 | bytes 15114240 | tf_op jit(solution)/shard_map/attend_back/pallas_call | solution.py:494
  750.6 19.1 %fusion.377 = (f32[3072]{0:T(1024)}, f32[2,3072]{1,0:T(2,128)S(1)}, bf16[2,576,3072]{2,1,0:T(8,128)(2,1)}) fusion(bf16[2,576,3072]{2,1,0:T(8,128)(2,1)} %bitcast.580, bf16[3072,1536]{1,0:T(8,128)(2,1)} %bitcast.613, bf16[1,576,1536]{2,1,0:T(8,128)(2,1)} %bitcast.117, bf16[1,576,1536]{2,1,0:T(8,128)(2,1)} %bitcast.116), kind=kOutput, calls=%fused_computation.647 | convolution fusion | flops 10891090944 | bytes 27168768 | tf_op jit(solution)/shard_map/dot_general | solution.py:37
  829.3 13.3 %fusion.10 = f32[2,576,3072]{2,1,0:T(8,128)} fusion(bf16[2,576,3072]{2,1,0:T(8,128)(2,1)} %bitcast.581, bf16[2,576,3072]{2,1,0:T(8,128)(2,1)} %get-tuple-element.105, f32[2,3072]{1,0:T(2,128)S(1)} %subtract_divide_fusion, f32[2,3072]{1,0:T(2,128)S(1)} %copy-done.81), kind=kLoop, calls=%fused_computation.16 | loop fusion | flops 17694720 | bytes 28360704 | tf_op jit(solution)/shard_map/add | solution.py:865
  883.8 14.7 %collective-permute-done.111 = bf16[384,1152]{1,0:T(8,128)(2,1)S(1)} collective-permute-done((bf16[384,1152]{1,0:T(8,128)(2,1)S(1)}, bf16[384,1152]{1,0:T(8,128)(2,1)S(1)}, u32[]{:S(2)}, u32[]{:S(2)}) %collective-permute-start.111) | collective-permute-done | bytes 884768 | tf_op jit(solution)/shard_map/ppermute | solution.py:514
  982.3 16.8 %collective-permute-done.97 = bf16[160,768]{1,0:T(8,128)(2,1)S(1)} collective-permute-done((bf16[160,768]{1,0:T(8,128)(2,1)}, bf16[160,768]{1,0:T(8,128)(2,1)S(1)}, u32[]{:S(2)}, u32[]{:S(2)}) %collective-permute-start.97) | collective-permute-done | bytes 245792 | tf_op jit(solution)/shard_map/ppermute | solution.py:514
  1084.2 19.4 %collective-permute-done.59 = bf16[6,24,1536]{2,1,0:T(8,128)(2,1)S(1)} collective-permute-done((bf16[6,24,1536]{2,1,0:T(8,128)(2,1)S(1)}, bf16[6,24,1536]{2,1,0:T(8,128)(2,1)S(1)}, u32[]{:S(2)}, u32[]{:S(2)}) %collective-permute-start.59) | collective-permute-done | bytes 442400 | tf_op jit(solution)/shard_map/ppermute | solution.py:518
  1123.0 28.1 %collective-permute-done.67 = f32[2,4,7536]{2,1,0:T(4,128)S(1)} collective-permute-done((f32[2,4,7536]{2,1,0:T(4,128)S(1)}, f32[2,4,7536]{2,1,0:T(4,128)S(1)}, u32[]{:S(2)}, u32[]{:S(2)}) %collective-permute-start.67) | collective-permute-done | bytes 241184 | tf_op jit(solution)/shard_map/ppermute | solution.py:514
  1155.3 25.7 %collective-permute-done.68 = f32[4,7536]{1,0:T(4,128)S(1)} collective-permute-done((f32[4,7536]{1,0:T(4,128)S(1)}, f32[4,7536]{1,0:T(4,128)S(1)}, u32[]{:S(2)}, u32[]{:S(2)}) %collective-permute-start.68) | collective-permute-done | bytes 120608 | tf_op jit(solution)/shard_map/ppermute | solution.py:514
  1224.9 14.0 %collective-permute-start.82 = (bf16[2,48,1536]{2,1,0:T(8,128)(2,1)S(1)}, bf16[2,48,1536]{2,1,0:T(8,128)(2,1)S(1)}, u32[]{:S(2)}, u32[]{:S(2)}) collective-permute-start(bf16[2,48,1536]{2,1,0:T(8,128)(2,1)S(1)} %get-tuple-element.183), channel_id=1, source_target_pairs={{0,2},{1,3},{2,0},{3,1},{4,6},{5,7},{6,4},{7,5},{8,10},{9,11},{10,... | collective-permute-start | bytes 884744 | tf_op jit(solution)/shard_map/ppermute | solution.py:518
  1238.9 13.1 %collective-permute-done.76 = bf16[2,48,1536]{2,1,0:T(8,128)(2,1)S(1)} collective-permute-done((bf16[2,48,1536]{2,1,0:T(8,128)(2,1)S(1)}, bf16[2,48,1536]{2,1,0:T(8,128)(2,1)S(1)}, u32[]{:S(2)}, u32[]{:S(2)}) %collective-permute-start.76) | collective-permute-done | bytes 294944 | tf_op jit(solution)/shard_map/ppermute | solution.py:518
  (992 shorter events, 773.8 us)
Async XLA Ops:
  11.6 117.4 %collective-permute-start.3 = (bf16[2,48,3072]{2,1,0:T(8,128)(2,1)S(1)}, bf16[2,48,3072]{2,1,0:T(8,128)(2,1)S(1)}, u32[]{:S(2)}, u32[]{:S(2)}) collective-permute-start(bf16[2,48,3072]{2,1,0:T(8,128)(2,1)S(1)} %bitcast_dynamic-update-slice_fusion.44), channel_id=1, source_target_pairs={{0,3},{1,0},{2,1},{3,2},{4,7},{5,4},{6,5},{7,6},{8,11},{9,8},{10,9... | collective-permute-start | bytes 1769480 | tf_op jit(solution)/shard_map/ppermute | solution.py:518
  16.6 111.6 %collective-permute-start.2 = (bf16[2,48,3072]{2,1,0:T(8,128)(2,1)S(1)}, bf16[2,48,3072]{2,1,0:T(8,128)(2,1)S(1)}, u32[]{:S(2)}, u32[]{:S(2)}) collective-permute-start(bf16[2,48,3072]{2,1,0:T(8,128)(2,1)S(1)} %bitcast_dynamic-update-slice_fusion.44), channel_id=1, source_target_pairs={{0,2},{1,3},{2,0},{3,1},{4,6},{5,7},{6,4},{7,5},{8,10},{9,11},{10,... | collective-permute-start | bytes 1769480 | tf_op jit(solution)/shard_map/ppermute | solution.py:518
  16.6 109.2 %collective-permute-start.1 = (bf16[2,48,3072]{2,1,0:T(8,128)(2,1)S(1)}, bf16[2,48,3072]{2,1,0:T(8,128)(2,1)}, u32[]{:S(2)}, u32[]{:S(2)}) collective-permute-start(bf16[2,48,3072]{2,1,0:T(8,128)(2,1)S(1)} %bitcast_dynamic-update-slice_fusion.44), channel_id=1, source_target_pairs={{0,1},{1,2},{2,3},{3,0},{4,5},{5,6},{6,7},{7,4},{8,9},{9,10},{10,1... | collective-permute-start | bytes 1769480 | tf_op jit(solution)/shard_map/ppermute | solution.py:518
  20.2 104.4 %collective-permute-start.6 = (bf16[6,24,1536]{2,1,0:T(8,128)(2,1)}, bf16[6,24,1536]{2,1,0:T(8,128)(2,1)}, u32[]{:S(2)}, u32[]{:S(2)}) collective-permute-start(bf16[6,24,1536]{2,1,0:T(8,128)(2,1)} %get-tuple-element.206), channel_id=1, source_target_pairs={{0,3},{1,0},{2,1},{3,2},{4,7},{5,4},{6,5},{7,6},{8,11},{9,8},{10,9... | collective-permute-start | bytes 1327112 | tf_op jit(solution)/shard_map/ppermute | solution.py:518
  130.6 135.8 %collective-permute-start.14 = (bf16[384,3072]{1,0:T(8,128)(2,1)}, bf16[384,3072]{1,0:T(8,128)(2,1)}, u32[]{:S(2)}, u32[]{:S(2)}) collective-permute-start(bf16[384,3072]{1,0:T(8,128)(2,1)} %bitcast.8), channel_id=1, source_target_pairs={{0,16},{4,20},{8,24},{12,28},{16,0},{20,4},{24,8},{28,12},{1,17},{... | collective-permute-start | bytes 7077896 | tf_op jit(solution)/shard_map/ppermute | solution.py:514
  132.1 136.2 %collective-permute-start.13 = (bf16[384,3072]{1,0:T(8,128)(2,1)}, bf16[384,3072]{1,0:T(8,128)(2,1)}, u32[]{:S(2)}, u32[]{:S(2)}) collective-permute-start(bf16[384,3072]{1,0:T(8,128)(2,1)} %bitcast.8), channel_id=1, source_target_pairs={{0,8},{4,12},{8,0},{12,4},{16,24},{20,28},{24,16},{28,20},{1,9},{5... | collective-permute-start | bytes 7077896 | tf_op jit(solution)/shard_map/ppermute | solution.py:514
  195.0 71.3 %collective-permute-start.20 = (bf16[1,192,1536]{2,1,0:T(8,128)(2,1)S(1)}, bf16[1,192,1536]{2,1,0:T(8,128)(2,1)S(1)}, u32[]{:S(2)}, u32[]{:S(2)}) collective-permute-start(bf16[1,192,1536]{2,1,0:T(8,128)(2,1)S(1)} %bitcast.698), channel_id=1, source_target_pairs={{0,3},{1,0},{2,1},{3,2},{4,7},{5,4},{6,5},{7,6},{8,11},{9,8},{10,9... | collective-permute-start | bytes 1769480 | tf_op jit(solution)/shard_map/ppermute | solution.py:518
  296.6 101.1 %collective-permute-start.26 = (bf16[768,1536]{1,0:T(8,128)(2,1)S(1)}, bf16[768,1536]{1,0:T(8,128)(2,1)}, u32[]{:S(2)}, u32[]{:S(2)}) collective-permute-start(bf16[768,1536]{1,0:T(8,128)(2,1)S(1)} %bitcast.615), channel_id=1, source_target_pairs={{0,16},{4,20},{8,24},{12,28},{16,0},{20,4},{24,8},{28,12},{1,17},{... | collective-permute-start | bytes 7077896 | tf_op jit(solution)/shard_map/ppermute | solution.py:514
  297.2 103.0 %collective-permute-start.25 = (bf16[768,1536]{1,0:T(8,128)(2,1)S(1)}, bf16[768,1536]{1,0:T(8,128)(2,1)}, u32[]{:S(2)}, u32[]{:S(2)}) collective-permute-start(bf16[768,1536]{1,0:T(8,128)(2,1)S(1)} %bitcast.616), channel_id=1, source_target_pairs={{0,8},{4,12},{8,0},{12,4},{16,24},{20,28},{24,16},{28,20},{1,9},{5... | collective-permute-start | bytes 7077896 | tf_op jit(solution)/shard_map/ppermute | solution.py:514
  432.4 89.9 %collective-permute-start.43 = (bf16[384,2304]{1,0:T(8,128)(2,1)}, bf16[384,2304]{1,0:T(8,128)(2,1)S(1)}, u32[]{:S(2)}, u32[]{:S(2)}) collective-permute-start(bf16[384,2304]{1,0:T(8,128)(2,1)} %bitcast.69), channel_id=1, source_target_pairs={{0,16},{4,20},{8,24},{12,28},{16,0},{20,4},{24,8},{28,12},{1,17},{... | collective-permute-start | bytes 5308424 | tf_op jit(solution)/shard_map/ppermute | solution.py:514
  433.0 90.8 %collective-permute-start.42 = (bf16[384,2304]{1,0:T(8,128)(2,1)}, bf16[384,2304]{1,0:T(8,128)(2,1)}, u32[]{:S(2)}, u32[]{:S(2)}) collective-permute-start(bf16[384,2304]{1,0:T(8,128)(2,1)} %bitcast.69), channel_id=1, source_target_pairs={{0,8},{4,12},{8,0},{12,4},{16,24},{20,28},{24,16},{28,20},{1,9},{5... | collective-permute-start | bytes 5308424 | tf_op jit(solution)/shard_map/ppermute | solution.py:514
  743.0 78.6 %collective-permute-start.110 = (bf16[384,1152]{1,0:T(8,128)(2,1)}, bf16[384,1152]{1,0:T(8,128)(2,1)}, u32[]{:S(2)}, u32[]{:S(2)}) collective-permute-start(bf16[384,1152]{1,0:T(8,128)(2,1)} %fusion.74), channel_id=1, source_target_pairs={{0,8},{4,12},{8,0},{12,4},{16,24},{20,28},{24,16},{28,20},{1,9},{5... | collective-permute-start | bytes 2654216 | tf_op jit(solution)/shard_map/ppermute | solution.py:514
  796.5 84.9 %collective-permute-start.55 = (bf16[6,24,1536]{2,1,0:T(8,128)(2,1)}, bf16[6,24,1536]{2,1,0:T(8,128)(2,1)}, u32[]{:S(2)}, u32[]{:S(2)}) collective-permute-start(bf16[6,24,1536]{2,1,0:T(8,128)(2,1)} %get-tuple-element.198), channel_id=1, source_target_pairs={{0,3},{1,0},{2,1},{3,2},{4,7},{5,4},{6,5},{7,6},{8,11},{9,8},{10,9... | collective-permute-start | bytes 1327112 | tf_op jit(solution)/shard_map/ppermute | solution.py:518
  799.1 80.3 %collective-permute-start.54 = (bf16[6,24,1536]{2,1,0:T(8,128)(2,1)}, bf16[6,24,1536]{2,1,0:T(8,128)(2,1)}, u32[]{:S(2)}, u32[]{:S(2)}) collective-permute-start(bf16[6,24,1536]{2,1,0:T(8,128)(2,1)} %get-tuple-element.199), channel_id=1, source_target_pairs={{0,2},{1,3},{2,0},{3,1},{4,6},{5,7},{6,4},{7,5},{8,10},{9,11},{10,... | collective-permute-start | bytes 1327112 | tf_op jit(solution)/shard_map/ppermute | solution.py:518
  808.9 68.6 %collective-permute-start.53 = (bf16[6,24,1536]{2,1,0:T(8,128)(2,1)}, bf16[6,24,1536]{2,1,0:T(8,128)(2,1)}, u32[]{:S(2)}, u32[]{:S(2)}) collective-permute-start(bf16[6,24,1536]{2,1,0:T(8,128)(2,1)} %get-tuple-element.200), channel_id=1, source_target_pairs={{0,1},{1,2},{2,3},{3,0},{4,5},{5,6},{6,7},{7,4},{8,9},{9,10},{10,1... | collective-permute-start | bytes 1327112 | tf_op jit(solution)/shard_map/ppermute | solution.py:518
  827.2 73.4 %collective-permute-start.117 = (bf16[384,1152]{1,0:T(8,128)(2,1)}, bf16[384,1152]{1,0:T(8,128)(2,1)S(1)}, u32[]{:S(2)}, u32[]{:S(2)}) collective-permute-start(bf16[384,1152]{1,0:T(8,128)(2,1)} %convolution_convert_fusion.3), channel_id=1, source_target_pairs={{0,16},{4,20},{8,24},{12,28},{16,0},{20,4},{24,8},{28,12},{1,17},{... | collective-permute-start | bytes 2654216 | tf_op jit(solution)/shard_map/ppermute | solution.py:514
  882.6 65.4 %collective-permute-start.86 = (bf16[768,768]{1,0:T(8,128)(2,1)}, bf16[768,768]{1,0:T(8,128)(2,1)}, u32[]{:S(2)}, u32[]{:S(2)}) collective-permute-start(bf16[768,768]{1,0:T(8,128)(2,1)} %fusion.154), channel_id=1, source_target_pairs={{0,8},{4,12},{8,0},{12,4},{16,24},{20,28},{24,16},{28,20},{1,9},{5... | collective-permute-start | bytes 3538952 | tf_op jit(solution)/shard_map/ppermute | solution.py:514
  963.4 155.9 %collective-permute-start.85 = (bf16[768,768]{1,0:T(8,128)(2,1)}, bf16[768,768]{1,0:T(8,128)(2,1)}, u32[]{:S(2)}, u32[]{:S(2)}) collective-permute-start(bf16[768,768]{1,0:T(8,128)(2,1)} %fusion.144), channel_id=1, source_target_pairs={{0,8},{4,12},{8,0},{12,4},{16,24},{20,28},{24,16},{28,20},{1,9},{5... | collective-permute-start | bytes 3538952 | tf_op jit(solution)/shard_map/ppermute | solution.py:514
  1009.9 142.4 %collective-permute-start.93 = (bf16[768,768]{1,0:T(8,128)(2,1)}, bf16[768,768]{1,0:T(8,128)(2,1)}, u32[]{:S(2)}, u32[]{:S(2)}) collective-permute-start(bf16[768,768]{1,0:T(8,128)(2,1)} %fusion.149), channel_id=1, source_target_pairs={{0,16},{4,20},{8,24},{12,28},{16,0},{20,4},{24,8},{28,12},{1,17},{... | collective-permute-start | bytes 3538952 | tf_op jit(solution)/shard_map/ppermute | solution.py:514
  1027.5 125.7 %collective-permute-start.92 = (bf16[768,768]{1,0:T(8,128)(2,1)}, bf16[768,768]{1,0:T(8,128)(2,1)}, u32[]{:S(2)}, u32[]{:S(2)}) collective-permute-start(bf16[768,768]{1,0:T(8,128)(2,1)} %add_convert_fusion.1), channel_id=1, source_target_pairs={{0,8},{4,12},{8,0},{12,4},{16,24},{20,28},{24,16},{28,20},{1,9},{5... | collective-permute-start | bytes 3538952 | tf_op jit(solution)/shard_map/ppermute | solution.py:514
  1117.7 80.6 %collective-permute-start.72 = (bf16[384,1536]{1,0:T(8,128)(2,1)}, bf16[384,1536]{1,0:T(8,128)(2,1)}, u32[]{:S(2)}, u32[]{:S(2)}) collective-permute-start(bf16[384,1536]{1,0:T(8,128)(2,1)} %convolution_convert_fusion.6), channel_id=1, source_target_pairs={{0,8},{4,12},{8,0},{12,4},{16,24},{20,28},{24,16},{28,20},{1,9},{5... | collective-permute-start | bytes 3538952 | tf_op jit(solution)/shard_map/ppermute | solution.py:514
  1119.3 85.6 %collective-permute-start.80 = (bf16[384,1536]{1,0:T(8,128)(2,1)}, bf16[384,1536]{1,0:T(8,128)(2,1)S(1)}, u32[]{:S(2)}, u32[]{:S(2)}) collective-permute-start(bf16[384,1536]{1,0:T(8,128)(2,1)} %convolution_convert_fusion.5), channel_id=1, source_target_pairs={{0,16},{4,20},{8,24},{12,28},{16,0},{20,4},{24,8},{28,12},{1,17},{... | collective-permute-start | bytes 3538952 | tf_op jit(solution)/shard_map/ppermute | solution.py:514
  1193.8 75.2 %collective-permute-start.88 = (bf16[1,192,768]{2,1,0:T(8,128)(2,1)}, bf16[1,192,768]{2,1,0:T(8,128)(2,1)}, u32[]{:S(2)}, u32[]{:S(2)}) collective-permute-start(bf16[1,192,768]{2,1,0:T(8,128)(2,1)} %get-tuple-element.176), channel_id=1, source_target_pairs={{0,1},{1,2},{2,3},{3,0},{4,5},{5,6},{6,7},{7,4},{8,9},{9,10},{10,1... | collective-permute-start | bytes 884744 | tf_op jit(solution)/shard_map/ppermute | solution.py:518
  1198.3 76.8 %collective-permute-start.90 = (bf16[1,192,768]{2,1,0:T(8,128)(2,1)}, bf16[1,192,768]{2,1,0:T(8,128)(2,1)S(1)}, u32[]{:S(2)}, u32[]{:S(2)}) collective-permute-start(bf16[1,192,768]{2,1,0:T(8,128)(2,1)} %get-tuple-element.177), channel_id=1, source_target_pairs={{0,3},{1,0},{2,1},{3,2},{4,7},{5,4},{6,5},{7,6},{8,11},{9,8},{10,9... | collective-permute-start | bytes 884744 | tf_op jit(solution)/shard_map/ppermute | solution.py:518
  (263 other events, 4395.4 us)

commit v4 on v2

--- a/solution.py
+++ b/solution.py
@@ -574,31 +574,24 @@
     return full.reshape(-1, line.shape[1])
 
 
-def reduce_owner(piece, parts, plane, place):
-    low = jnp.bfloat16
-    far = [piece(plane ^ 3, half).astype(low) for half in range(2)]
-    via_x, via_y = (swap(far[0], 2), swap(far[1], 4))
-    out_x = [piece(plane ^ 1, 0).astype(low), None]
-    out_y = [None, piece(plane ^ 2, 1).astype(low)]
-    got_x, got_y = ([swap(out_x[0], 2), None], [None, swap(out_y[1], 4)])
-    out_x[1] = (piece(plane ^ 1, 1) + via_y.astype(jnp.float32)).astype(low)
-    out_y[0] = (piece(plane ^ 2, 0) + via_x.astype(jnp.float32)).astype(low)
-    got_x[1], got_y[0] = (swap(out_x[1], 2), swap(out_y[0], 4))
-    results = []
-    for half in range(2):
-        total = (
-            piece(plane, half)
-            + got_x[half].astype(jnp.float32)
-            + got_y[half].astype(jnp.float32)
-        )
-        rows, cols = total.shape
-        total = total.reshape(parts, LINE, rows // (parts * LINE), cols)
-        summed = pick(total, place, 1)
-        for step in range(1, LINE):
-            sent = pick(total, (place + step) % LINE, 1).astype(low)
-            summed = summed + rotate(sent, step).astype(jnp.float32)
-        results.append(summed)
-    return jnp.concatenate(results, axis=-1)
+def reduce_owner(pieces, parts, plane, place):
+    low, f32 = (jnp.bfloat16, jnp.float32)
+    first, second, last = pieces
+    far = first(plane ^ 3).astype(low)
+    half = far.shape[1] // 2
+    via_x, via_y = (swap(far[:, :half], 2), swap(far[:, half:], 4))
+    left = jnp.pad(via_x.astype(f32), ((0, 0), (0, half)))
+    right = jnp.pad(via_y.astype(f32), ((0, 0), (half, 0)))
+    got_x = swap((second(plane ^ 1) + right).astype(low), 2)
+    got_y = swap((second(plane ^ 2) + left).astype(low), 4)
+    total = last(plane) + got_x.astype(f32) + got_y.astype(f32)
+    rows, cols = total.shape
+    shaped = total.reshape(parts, LINE, rows // (parts * LINE), cols)
+    summed = pick(shaped, place, 1)
+    for step in range(1, LINE):
+        sent = pick(shaped, (place + step) % LINE, 1).astype(low)
+        summed = summed + rotate(sent, step).astype(f32)
+    return (summed, total)
 
 
 def gather_small(value, plane, core, place):
@@ -691,15 +684,22 @@
     f32, low = (jnp.float32, jnp.bfloat16)
 
     small = jnp.concatenate(
-        [conv_weight.reshape(-1), vectors.reshape(-1), hidden_vecs.reshape(-1)]
-    )
-    small_all = gather_small(small, plane, core, place).astype(f32)
+        [
+            conv_weight.reshape(-1),
+            vectors.reshape(-1),
+            hidden_vecs.reshape(-1),
+            time_weight.reshape(-1),
+        ]
+    )
+    small_low = gather_small(small, plane, core, place)
+    small_all = small_low.astype(f32)
+    time_at = small.size - time_weight.size
     col_rows, col_width = (9 + vectors.shape[0], conv_weight.shape[1])
     col_all = small_all[..., : col_rows * col_width]
     col_all = col_all.reshape(LINE, PLANE, 2, col_rows, col_width).transpose(3, 1, 2, 0, 4)
     col_all = col_all.reshape(col_rows, channels)
     taps, vecs = (col_all[:9], col_all[9:])
-    hidden_all = pick(small_all[..., col_rows * col_width :], core, 2)
+    hidden_all = pick(small_all[..., col_rows * col_width : time_at], core, 2)
     hidden_all = hidden_all.reshape(LINE, PLANE, 3, -1).transpose(2, 1, 0, 3)
     hidden_all = hidden_all.reshape(3, half_hidden)
 
@@ -722,13 +722,13 @@
 
     latent = spread_line(latents, place).reshape(height, columns, channels)
     up_line = flat_line(up_shard, place)
-    up_line, latent, down_shard, map_shard, time_shard = held(
-        up_line, latent, down_weight[None], map_weight[None], time_weight
+    up_line, latent, down_shard, map_shard, time_low = held(
+        up_line, latent, down_weight[None], map_weight[None], small_low[..., time_at:]
     )
     up_full = flat_plane(up_line, plane)
     down_line = flat_line(down_shard, place)
     map_line = flat_line(map_shard, place)
-    time_all = gather_small(time_shard, plane, core, place).transpose(3, 1, 2, 0, 4)
+    time_all = time_low.reshape(LINE, PLANE, 2, time_rank, -1).transpose(3, 1, 2, 0, 4)
     time_all = time_all.reshape(time_rank, 2 * channels)
     clip_own = pick(clip_text, place).astype(f32)
     words_own = jax.nn.silu(clip_own).astype(low)
@@ -794,42 +794,42 @@
     mixed, log_totals = attend(rows_qkv, lengths_two, pixels)
     attended = own_sum(product(mixed[0], out_full), product(mixed[1], out_full))
     layer_own = (second + (attended + vecs[7])).astype(low)
-    layer_out = spread_line(layer_own.reshape(latents.shape), place)
-
     grad_two = pair(grad_own)
     g_mixed = product_nt(grad_two.reshape(2 * pixels, channels), out_full).astype(low)
     g_mixed = g_mixed.reshape(2, pixels, half_channels)
 
-    def owner_sums(left, right, parts):
+    def owner_sums(left, right, parts, *gates):
         block = left.shape[1] // PLANE
-        half = right.shape[1] // 2
-
-        def piece(chip, which):
-            cut = lax.dynamic_slice_in_dim(left, chip * block, block, 1)
-            return product_tn(cut, right[:, which * half : (which + 1) * half])
-
-        return reduce_owner(piece, parts, plane, place)
-
-    out_grad = owner_sums(
-        mixed.reshape(2 * pixels, half_channels), grad_two.reshape(2 * pixels, channels), 1
-    )[0]
+
+        def pieces_of(left_op, right_op):
+            def piece(chip):
+                taken = lax.dynamic_slice_in_dim(left_op, chip * block, block, 1)
+                return product_tn(taken, right_op)
+
+            return piece
+
+        pieces = [pieces_of(left, right)]
+        for gate in gates:
+            left, right, _ = held(left, right, gate)
+            pieces.append(pieces_of(left, right))
+        pieces += [pieces[-1]] * (3 - len(pieces))
+        return reduce_owner(pieces, parts, plane, place)
+
     g_rows = attend_back_pairs(rows_qkv, g_mixed, log_totals, lengths_two, pixels)
+    layer_out = spread_line(layer_own.reshape(latents.shape), place)
+    g_rows, layer_out = held(g_rows, layer_out)
     g_second_in = own_sum(
         product_nt(g_rows[0, :pixels], attn_full), product_nt(g_rows[1, :pixels], attn_full)
     )
-    g_text = g_rows[:, pixels:].reshape(2 * text_pad, 3 * half_channels)
-    g_mapped = pair_sum(product_nt(g_text, attn_full).reshape(2, text_pad, channels))
-    g_mapped = g_mapped.astype(low).reshape(2 * text_pad, channels)
+    out_grad = owner_sums(
+        mixed.reshape(2 * pixels, half_channels),
+        grad_two.reshape(2 * pixels, channels),
+        1,
+        g_rows,
+        g_second_in,
+    )[0][0]
+    g_second_in, g_rows = held(g_second_in, g_rows)
     g_flat = g_rows.reshape(2 * keys, 3 * half_channels)
-    attn_grad = owner_sums(sources, g_flat, 2)
-    map_grad = owner_sums(words_half, g_mapped, 1)[0]
-    g_words = product_nt(g_mapped, map_full).reshape(2, text_pad, -1)[:, :text_len]
-    g_words = core_merge(g_words[0], swap(g_words[1], 1), 1, core)
-    sigmoid_text = jax.nn.sigmoid(clip_own)
-    text_own = (g_words * (sigmoid_text * (1.0 + clip_own * (1.0 - sigmoid_text)))).astype(low)
-    text_own = text_own.reshape(text_len, LINE, clip_width // LINE).transpose(1, 0, 2)
-    text_grad = spread_line(text_own, place)
-
     grad_float = grad_own.astype(f32)
     g_second = grad_float + norm_back(g_second_in, second_norm, second_inv)
     g_scale = jnp.sum(g_second * first_sum, axis=0)
@@ -839,11 +839,11 @@
     g_first = g_second * (1.0 + scale_vec)
     g_down_own = g_first.astype(low)
     g_down = pair(g_down_own).reshape(2 * pixels, channels)
-    down_grad = owner_sums(grn_out.reshape(2 * pixels, half_hidden), g_down, 1)[0]
     g_grn = product_nt(g_down, down_full).reshape(2, pixels, half_hidden)
     g_grn_active = jnp.sum(g_grn * active_lat, axis=1)
     g_grn_sum = jnp.sum(g_grn, axis=(0, 1))
     g_grn, g_grn_active, grad_beta = held(g_grn.astype(low), g_grn_active, g_grn_sum)
+    g_grn_low = g_grn
     g_grn = g_grn.astype(f32)
     grad_gamma = jnp.sum(g_grn_active * grn_ratio, axis=0)
     g_ratio = g_grn_active * gamma_vec
@@ -854,11 +854,26 @@
         + active_lat * (g_strength / strength)[:, None]
     )
     g_up = (g_active.reshape(2 * pixels, half_hidden) * slope.astype(f32)).astype(low)
+    attn_grad, _ = owner_sums(sources, g_flat, 2, g_down, g_grn_low)
+    down_grad = owner_sums(
+        grn_out.reshape(2 * pixels, half_hidden), g_down, 1, g_grn_low, g_up
+    )[0][0]
+    g_text, _ = held(g_rows[:, pixels:], g_down)
+    g_text = g_text.reshape(2 * text_pad, 3 * half_channels)
+    g_mapped = pair_sum(product_nt(g_text, attn_full).reshape(2, text_pad, channels))
+    g_mapped = g_mapped.astype(low).reshape(2 * text_pad, channels)
+    map_grad = owner_sums(words_half, g_mapped, 1, g_grn_low, g_up)[0][0]
+    g_words = product_nt(g_mapped, map_full).reshape(2, text_pad, -1)[:, :text_len]
+    g_words = core_merge(g_words[0], swap(g_words[1], 1), 1, core)
+    sigmoid_text = jax.nn.sigmoid(clip_own)
+    text_own = (g_words * (sigmoid_text * (1.0 + clip_own * (1.0 - sigmoid_text)))).astype(low)
+    text_own = text_own.reshape(text_len, LINE, clip_width // LINE).transpose(1, 0, 2)
+    text_grad = spread_line(text_own, place)
     g_first_in = own_sum(
         product_nt(g_up[:pixels], up_full), product_nt(g_up[pixels:], up_full)
     )
     g_conv = norm_back(g_first_in, first_norm, first_inv).astype(low).reshape(latent.shape)
-    up_grad = owner_sums(first_in, g_up, 2)
+    up_grad, up_total = owner_sums(first_in, g_up, 2, g_conv)
     g_framed = jnp.pad(g_conv, ((1, 1), (1, 1), (0, 0)))
     g_conv_f = g_conv.astype(f32)
     back_sum = g_first.reshape(latent.shape)
@@ -903,6 +918,7 @@
     time_part = time_part.reshape(time_rank, PLANE, 2, LINE, -1).transpose(1, 2, 3, 0, 4)
     time_part = time_part.reshape(PLANE, 2, LINE, -1)
     core_parts = jnp.concatenate([col_parts, time_part], axis=-1)
+    core_parts, _ = held(core_parts, up_total)
     core_sum = pick(core_parts, core, 1) + swap(pick(core_parts, 1 - core, 1), 1)
     hidden_parts = jnp.stack([column_sums(g_up), grad_gamma, grad_beta])
     hidden_parts = hidden_parts.reshape(3, PLANE, LINE, -1).transpose(1, 2, 0, 3)

time: 1290 us -> 1190 us (0.922)
  waiting for transfers between devices: 445 us -> 396 us
  local copies, waits for them, and re-layouts: 218 us -> 172 us
  matrix products: 222 us -> 209 us
    ppermute x78 -> x65, waiting for transfers between devices: 238 us -> 190 us  [swap(): return lax.ppermute(value, 'dp', [(i, i ^ bit) for i in range(2 * PLANE)])]
    dynamic_update_slice x75 -> x65, local copies, waits for them, and re-layouts: 89.4 us -> 61.4 us  [put(): return lax.dynamic_update_index_in_dim(buffer, value, index, axis)]
    dot_general x40 -> x20, matrix products: 113 us -> 90.9 us  [product_tn(): lax.dot_general(left_op, right_op, (((0,), (0,)), ((), ())), preferred_el...]
    ppermute x69 -> x51, starting transfers between devices: 137 us -> 156 us  [rotate(): lax.ppermute(value, 'band', [(i, (i + step) % LINE) for i in range(LINE)])]
    ppermute x78 -> x65, starting transfers between devices: 65.1 us -> 50.1 us  [swap(): return lax.ppermute(value, 'dp', [(i, i ^ bit) for i in range(2 * PLANE)])]
    ppermute x69 -> x51, waiting for transfers between devices: 208 us -> 207 us  [rotate(): lax.ppermute(value, 'band', [(i, (i + step) % LINE) for i in range(LINE)])]
  transfers between devices with their start and end apart: 147 -> 116, of which waited for: 54 -> 36; matrix products, arithmetic and copies ran while one was open for 38% -> 39% of each run, Pallas kernels for 6% -> 6%
where the time goes in v4:
time: 1190 us; the launch traced here: 1180 us
  waiting for transfers between devices  396 us (33%)
  matrix products  209 us (18%)
  starting transfers between devices  206 us (17%)
  local copies, waits for them, and re-layouts  172 us (14%)
  other arithmetic  114 us (10%)
  Pallas kernels  76 us (6%)
    ppermute x51, waiting for transfers between devices, rotate(): lax.ppermute(value, 'band', [(i, (i + step) % LINE) for i in range(LINE)])  207 us
    ppermute x65, waiting for transfers between devices, swap(): return lax.ppermute(value, 'dp', [(i, i ^ bit) for i in range(2 * PLANE)])  190 us
    ppermute x51, starting transfers between devices, rotate(): lax.ppermute(value, 'band', [(i, (i + step) % LINE) for i in range(LINE)])  156 us
    dot_general x20, matrix products, product_tn(): lax.dot_general(left_op, right_op, (((0,), (0,)), ((), ())), preferred_el...  90.9 us
    dot_general x8, matrix products, product_nt(): lax.dot_general(left_op, right_op, (((1,), (1,)), ((), ())), preferred_el...  67.1 us
    dynamic_update_slice x65, local copies, waits for them, and re-layouts, put(): return lax.dynamic_update_index_in_dim(buffer, value, index, axis)  61.4 us
    dot_general x8, matrix products, product(): return jnp.dot(left_op, right_op, preferred_element_type=jnp.float32)  51.5 us
    ppermute x65, starting transfers between devices, swap(): return lax.ppermute(value, 'dp', [(i, i ^ bit) for i in range(2 * PLANE)])  50.1 us
  transfers between devices with their start and end apart: 116, of which 36 were waited for; matrix products, arithmetic and copies ran while one was open for 39% of the time, Pallas kernels for 6%

profile of v4, /device:TPU:0, one launch (start us, length us, event | category | flops | bytes accessed | tf_op | source)
XLA Modules:
  0.0 1177.6 jit_solution(16829526146721014978)
XLA Ops:
  63.6 9.9 collective-permute-start.12
  105.8 31.0 %collective-permute-done.2 = bf16[2,48,3072]{2,1,0:T(8,128)(2,1)S(1)} collective-permute-done((bf16[2,48,3072]{2,1,0:T(8,128)(2,1)S(1)}, bf16[2,48,3072]{2,1,0:T(8,128)(2,1)S(1)}, u32[]{:S(2)}, u32[]{:S(2)}) %collective-permute-start.2) | collective-permute-done | bytes 589856 | tf_op jit(solution)/shard_map/ppermute | solution.py:518
  137.8 9.8 collective-permute-done.3
  204.5 21.8 %collective-permute-done.20 = bf16[1,192,1536]{2,1,0:T(8,128)(2,1)S(1)} collective-permute-done((bf16[1,192,1536]{2,1,0:T(8,128)(2,1)}, bf16[1,192,1536]{2,1,0:T(8,128)(2,1)S(1)}, u32[]{:S(2)}, u32[]{:S(2)}) %collective-permute-start.20) | collective-permute-done | bytes 589856 | tf_op jit(solution)/shard_map/ppermute | solution.py:518
  242.6 21.6 %collective-permute-done.16 = bf16[192,3072]{1,0:T(8,128)(2,1)S(1)} collective-permute-done((bf16[192,3072]{1,0:T(8,128)(2,1)S(1)}, bf16[192,3072]{1,0:T(8,128)(2,1)S(1)}, u32[]{:S(2)}, u32[]{:S(2)}) %collective-permute-start.16) | collective-permute-done | bytes 1179680 | tf_op jit(solution)/shard_map/ppermute | solution.py:514
  269.3 17.9 %fusion.4 = (bf16[1152,3072]{1,0:T(8,128)(2,1)}, bf16[1152,3072]{1,0:T(8,128)(2,1)S(1)}) fusion(f32[3072]{0:T(1024)S(1)} %copy-done.99, bf16[1152,1536]{1,0:T(8,128)(2,1)S(1)} %bitcast.554, bf16[1536,3072]{1,0:T(8,128)(2,1)S(1)} %bitcast.549), kind=kOutput, calls=%fused_computation.10 | convolution fusion | flops 10914103296 | bytes 27144192 | tf_op jit(solution)/shard_map/dot_general | solution.py:27
  319.1 49.8 %collective-permute-done.34 = bf16[80,1536]{1,0:T(8,128)(2,1)S(1)} collective-permute-done((bf16[80,1536]{1,0:T(8,128)(2,1)S(1)}, bf16[80,1536]{1,0:T(8,128)(2,1)S(1)}, u32[]{:S(2)}, u32[]{:S(2)}) %collective-permute-start.34) | collective-permute-done | bytes 245792 | tf_op jit(solution)/shard_map/ppermute | solution.py:514
  374.2 21.8 %collective-permute-done.30 = bf16[384,1536]{1,0:T(8,128)(2,1)S(1)} collective-permute-done((bf16[384,1536]{1,0:T(8,128)(2,1)S(1)}, bf16[384,1536]{1,0:T(8,128)(2,1)S(1)}, u32[]{:S(2)}, u32[]{:S(2)}) %collective-permute-start.30) | collective-permute-done | bytes 1179680 | tf_op jit(solution)/shard_map/ppermute | solution.py:514
  428.4 12.3 %collective-permute-done.43 = bf16[384,2304]{1,0:T(8,128)(2,1)S(1)} collective-permute-done((bf16[384,2304]{1,0:T(8,128)(2,1)S(1)}, bf16[384,2304]{1,0:T(8,128)(2,1)S(1)}, u32[]{:S(2)}, u32[]{:S(2)}) %collective-permute-start.43) | collective-permute-done | bytes 1769504 | tf_op jit(solution)/shard_map/ppermute | solution.py:514
  441.6 14.5 %collective-permute-done.42 = bf16[384,2304]{1,0:T(8,128)(2,1)S(1)} collective-permute-done((bf16[384,2304]{1,0:T(8,128)(2,1)S(1)}, bf16[384,2304]{1,0:T(8,128)(2,1)S(1)}, u32[]{:S(2)}, u32[]{:S(2)}) %collective-permute-start.42) | collective-permute-done | bytes 1769504 | tf_op jit(solution)/shard_map/ppermute | solution.py:514
  457.9 16.2 %collective-permute-done.44 = bf16[192,2304]{1,0:T(8,128)(2,1)S(1)} collective-permute-done((bf16[192,2304]{1,0:T(8,128)(2,1)S(1)}, bf16[192,2304]{1,0:T(8,128)(2,1)S(1)}, u32[]{:S(2)}, u32[]{:S(2)}) %collective-permute-start.44) | collective-permute-done | bytes 884768 | tf_op jit(solution)/shard_map/ppermute | solution.py:514
  485.5 10.0 fusion.12
  495.5 29.1 %attend.1 = (bf16[2,576,768]{2,1,0:T(8,128)(2,1)S(1)}, f32[2,6,2,576]{3,2,1,0:T(2,128)S(1)}) custom-call(s32[2]{0:T(128)S(1)} %pad_add_fusion.length_ref, bf16[2,656,2304]{2,1,0:T(8,128)(2,1)S(1)} %bitcast.508), custom_call_target="tpu_custom_call" | custom-call | flops 4643094528 | bytes 9068544 | tf_op jit(solution)/shard_map/attend/pallas_call | solution.py:468
  552.8 47.0 %attend_back.1 = bf16[2,656,2304]{2,1,0:T(8,128)(2,1)S(1)} custom-call(s32[2]{0:T(128)S(1)} %pad_add_fusion.length_ref, bf16[2,656,2304]{2,1,0:T(8,128)(2,1)S(1)} %bitcast.511, bf16[2,576,768]{2,1,0:T(8,128)(2,1)S(1)} %bitcast.512, f32[2,6,2,576]{3,2,1,0:T(2,128)S(1)} %get-tuple-element.84.log_ref), custom_call_target="tpu_custom_call" | custom-call | flops 11607736320 | bytes 15114240 | tf_op jit(solution)/shard_map/attend_back/pallas_call | solution.py:494
  601.9 29.4 %collective-permute-done.59 = bf16[6,24,1536]{2,1,0:T(8,128)(2,1)S(1)} collective-permute-done((bf16[6,24,1536]{2,1,0:T(8,128)(2,1)S(1)}, bf16[6,24,1536]{2,1,0:T(8,128)(2,1)S(1)}, u32[]{:S(2)}, u32[]{:S(2)}) %collective-permute-start.59) | collective-permute-done | bytes 442400 | tf_op jit(solution)/shard_map/ppermute | solution.py:518
  712.2 18.2 %fusion.212 = (f32[3072]{0:T(1024)S(1)}, f32[2,3072]{1,0:T(2,128)S(1)}, bf16[2,576,3072]{2,1,0:T(8,128)(2,1)}) fusion(bf16[2,576,3072]{2,1,0:T(8,128)(2,1)} %bitcast.519, bf16[3072,1536]{1,0:T(8,128)(2,1)} %bitcast.66, bf16[1,576,1536]{2,1,0:T(8,128)(2,1)} %bitcast.136, bf16[1,576,1536]{2,1,0:T(8,128)(2,1)S(1)} %bitcast.564), kind=kOutput, calls=%fused_computation.481 | convolution fusion | flops 10891090944 | bytes 27168768 | tf_op jit(solution)/shard_map/dot_general | solution.py:37
  770.9 13.2 %fusion.10 = f32[2,576,3072]{2,1,0:T(8,128)} fusion(bf16[2,576,3072]{2,1,0:T(8,128)(2,1)} %bitcast.520, bf16[2,576,3072]{2,1,0:T(8,128)(2,1)} %get-tuple-element.89, f32[2,3072]{1,0:T(2,128)S(1)} %subtract_divide_fusion, f32[2,3072]{1,0:T(2,128)S(1)} %copy-done.66), kind=kLoop, calls=%fused_computation.16 | loop fusion | flops 17694720 | bytes 28360704 | tf_op jit(solution)/shard_map/add | solution.py:853
  792.3 11.8 %fusion.59 = bf16[576,1536]{1,0:T(8,128)(2,1)} fusion(bf16[1536,3072]{1,0:T(8,128)(2,1)} %bitcast.550, bf16[1152,3072]{1,0:T(8,128)(2,1)S(1)} %get-tuple-element.95), kind=kOutput, calls=%fused_computation.137 | convolution fusion | flops 5436702720 | bytes 14745600 | tf_op jit(solution)/shard_map/dot_general | solution.py:37
  949.4 24.6 %collective-permute-start.66 = (bf16[6,24,1536]{2,1,0:T(8,128)(2,1)S(1)}, bf16[6,24,1536]{2,1,0:T(8,128)(2,1)}, u32[]{:S(2)}, u32[]{:S(2)}) collective-permute-start(bf16[6,24,1536]{2,1,0:T(8,128)(2,1)S(1)} %get-tuple-element.178), channel_id=1, source_target_pairs={{0,2},{1,3},{2,0},{3,1},{4,6},{5,7},{6,4},{7,5},{8,10},{9,11},{10,... | collective-permute-start | bytes 1327112 | tf_op jit(solution)/shard_map/ppermute | solution.py:518
  974.0 12.3 %collective-permute-start.65 = (bf16[6,24,1536]{2,1,0:T(8,128)(2,1)}, bf16[6,24,1536]{2,1,0:T(8,128)(2,1)}, u32[]{:S(2)}, u32[]{:S(2)}) collective-permute-start(bf16[6,24,1536]{2,1,0:T(8,128)(2,1)} %get-tuple-element.179), channel_id=1, source_target_pairs={{0,1},{1,2},{2,3},{3,0},{4,5},{5,6},{6,7},{7,4},{8,9},{9,10},{10,1... | collective-permute-start | bytes 1327112 | tf_op jit(solution)/shard_map/ppermute | solution.py:518
  1049.0 10.0 collective-permute-start.91
  1068.1 35.0 %collective-permute-done.83 = bf16[2,48,3072]{2,1,0:T(8,128)(2,1)S(1)} collective-permute-done((bf16[2,48,3072]{2,1,0:T(8,128)(2,1)S(1)}, bf16[2,48,3072]{2,1,0:T(8,128)(2,1)S(1)}, u32[]{:S(2)}, u32[]{:S(2)}) %collective-permute-start.83) | collective-permute-done | bytes 589856 | tf_op jit(solution)/shard_map/ppermute | solution.py:518
  1103.2 25.3 %collective-permute-start.92 = (bf16[1,192,1536]{2,1,0:T(8,128)(2,1)S(1)}, bf16[1,192,1536]{2,1,0:T(8,128)(2,1)S(1)}, u32[]{:S(2)}, u32[]{:S(2)}) collective-permute-start(bf16[1,192,1536]{2,1,0:T(8,128)(2,1)S(1)} %get-tuple-element.164), channel_id=1, source_target_pairs={{0,2},{1,3},{2,0},{3,1},{4,6},{5,7},{6,4},{7,5},{8,10},{9,11},{10,... | collective-permute-start | bytes 1769480 | tf_op jit(solution)/shard_map/ppermute | solution.py:518
  1129.6 23.9 %collective-permute-done.84 = bf16[2,48,3072]{2,1,0:T(8,128)(2,1)S(1)} collective-permute-done((bf16[2,48,3072]{2,1,0:T(8,128)(2,1)S(1)}, bf16[2,48,3072]{2,1,0:T(8,128)(2,1)S(1)}, u32[]{:S(2)}, u32[]{:S(2)}) %collective-permute-start.84) | collective-permute-done | bytes 589856 | tf_op jit(solution)/shard_map/ppermute | solution.py:518
  (863 shorter events, 657.2 us)
Async XLA Ops:
  14.3 80.4 %collective-permute-start.1 = (bf16[48,3072]{1,0:T(8,128)(2,1)}, bf16[48,3072]{1,0:T(8,128)(2,1)}, u32[]{:S(2)}, u32[]{:S(2)}) collective-permute-start(bf16[48,3072]{1,0:T(8,128)(2,1)} %bitcast.222), channel_id=1, source_target_pairs={{0,4},{4,0},{8,12},{12,8},{16,20},{20,16},{24,28},{28,24},{1,5},{5... | collective-permute-start | bytes 884744 | tf_op jit(solution)/shard_map/ppermute | solution.py:514
  24.0 80.8 %collective-permute-start.7 = (bf16[6,24,1536]{2,1,0:T(8,128)(2,1)}, bf16[6,24,1536]{2,1,0:T(8,128)(2,1)}, u32[]{:S(2)}, u32[]{:S(2)}) collective-permute-start(bf16[6,24,1536]{2,1,0:T(8,128)(2,1)} %get-tuple-element.189), channel_id=1, source_target_pairs={{0,3},{1,0},{2,1},{3,2},{4,7},{5,4},{6,5},{7,6},{8,11},{9,8},{10,9... | collective-permute-start | bytes 1327112 | tf_op jit(solution)/shard_map/ppermute | solution.py:518
  38.7 63.4 %collective-permute-start.5 = (bf16[6,24,1536]{2,1,0:T(8,128)(2,1)}, bf16[6,24,1536]{2,1,0:T(8,128)(2,1)}, u32[]{:S(2)}, u32[]{:S(2)}) collective-permute-start(bf16[6,24,1536]{2,1,0:T(8,128)(2,1)} %get-tuple-element.190), channel_id=1, source_target_pairs={{0,1},{1,2},{2,3},{3,0},{4,5},{5,6},{6,7},{7,4},{8,9},{9,10},{10,1... | collective-permute-start | bytes 1327112 | tf_op jit(solution)/shard_map/ppermute | solution.py:518
  39.1 64.6 %collective-permute-start.6 = (bf16[6,24,1536]{2,1,0:T(8,128)(2,1)}, bf16[6,24,1536]{2,1,0:T(8,128)(2,1)}, u32[]{:S(2)}, u32[]{:S(2)}) collective-permute-start(bf16[6,24,1536]{2,1,0:T(8,128)(2,1)} %get-tuple-element.192), channel_id=1, source_target_pairs={{0,2},{1,3},{2,0},{3,1},{4,6},{5,7},{6,4},{7,5},{8,10},{9,11},{10,... | collective-permute-start | bytes 1327112 | tf_op jit(solution)/shard_map/ppermute | solution.py:518
  96.4 52.1 %collective-permute-start.4 = (bf16[2,48,3072]{2,1,0:T(8,128)(2,1)}, bf16[2,48,3072]{2,1,0:T(8,128)(2,1)S(1)}, u32[]{:S(2)}, u32[]{:S(2)}) collective-permute-start(bf16[2,48,3072]{2,1,0:T(8,128)(2,1)} %bitcast_dynamic-update-slice_fusion.47), channel_id=1, source_target_pairs={{0,3},{1,0},{2,1},{3,2},{4,7},{5,4},{6,5},{7,6},{8,11},{9,8},{10,9... | collective-permute-start | bytes 1769480 | tf_op jit(solution)/shard_map/ppermute | solution.py:518
  306.7 62.3 %collective-permute-start.29 = (bf16[768,1536]{1,0:T(8,128)(2,1)}, bf16[768,1536]{1,0:T(8,128)(2,1)S(1)}, u32[]{:S(2)}, u32[]{:S(2)}) collective-permute-start(bf16[768,1536]{1,0:T(8,128)(2,1)} %bitcast.38), channel_id=1, source_target_pairs={{0,16},{4,20},{8,24},{12,28},{16,0},{20,4},{24,8},{28,12},{1,17},{... | collective-permute-start | bytes 7077896 | tf_op jit(solution)/shard_map/ppermute | solution.py:514
  310.3 59.4 %collective-permute-start.28 = (bf16[768,1536]{1,0:T(8,128)(2,1)}, bf16[768,1536]{1,0:T(8,128)(2,1)S(1)}, u32[]{:S(2)}, u32[]{:S(2)}) collective-permute-start(bf16[768,1536]{1,0:T(8,128)(2,1)} %bitcast.38), channel_id=1, source_target_pairs={{0,8},{4,12},{8,0},{12,4},{16,24},{20,28},{24,16},{28,20},{1,9},{5... | collective-permute-start | bytes 7077896 | tf_op jit(solution)/shard_map/ppermute | solution.py:514
  314.5 54.3 %collective-permute-start.34 = (bf16[80,1536]{1,0:T(8,128)(2,1)S(1)}, bf16[80,1536]{1,0:T(8,128)(2,1)S(1)}, u32[]{:S(2)}, u32[]{:S(2)}) collective-permute-start(bf16[80,1536]{1,0:T(8,128)(2,1)S(1)} %slice.453), channel_id=1, source_target_pairs={{0,8},{4,12},{8,0},{12,4},{16,24},{20,28},{24,16},{28,20},{1,9},{5... | collective-permute-start | bytes 737288 | tf_op jit(solution)/shard_map/ppermute | solution.py:514
  317.0 51.9 %collective-permute-start.35 = (bf16[80,1536]{1,0:T(8,128)(2,1)S(1)}, bf16[80,1536]{1,0:T(8,128)(2,1)S(1)}, u32[]{:S(2)}, u32[]{:S(2)}) collective-permute-start(bf16[80,1536]{1,0:T(8,128)(2,1)S(1)} %slice.454), channel_id=1, source_target_pairs={{0,16},{4,20},{8,24},{12,28},{16,0},{20,4},{24,8},{28,12},{1,17},{... | collective-permute-start | bytes 737288 | tf_op jit(solution)/shard_map/ppermute | solution.py:514
  476.9 51.6 %collective-permute-start.53 = (bf16[192,1536]{1,0:T(8,128)(2,1)S(1)}, bf16[192,1536]{1,0:T(8,128)(2,1)S(1)}, u32[]{:S(2)}, u32[]{:S(2)}) collective-permute-start(bf16[192,1536]{1,0:T(8,128)(2,1)S(1)} %bitcast.589), channel_id=1, source_target_pairs={{0,8},{4,12},{8,0},{12,4},{16,24},{20,28},{24,16},{28,20},{1,9},{5... | collective-permute-start | bytes 1769480 | tf_op jit(solution)/shard_map/ppermute | solution.py:514
  741.2 78.5 %collective-permute-start.68 = (f32[2,80,1536]{2,1,0:T(8,128)}, f32[2,80,1536]{2,1,0:T(8,128)}, u32[]{:S(2)}, u32[]{:S(2)}) collective-permute-start(f32[2,80,1536]{2,1,0:T(8,128)} %fusion.15), channel_id=1, source_target_pairs={{0,4},{4,0},{8,12},{12,8},{16,20},{20,16},{24,28},{28,24},{1,5},{5... | collective-permute-start | bytes 2949128 | tf_op jit(solution)/shard_map/ppermute | solution.py:514
  749.2 124.8 %collective-permute-start.102 = (bf16[384,2304]{1,0:T(8,128)(2,1)}, bf16[384,2304]{1,0:T(8,128)(2,1)}, u32[]{:S(2)}, u32[]{:S(2)}) collective-permute-start(bf16[384,2304]{1,0:T(8,128)(2,1)} %add_convert_fusion.5), channel_id=1, source_target_pairs={{0,8},{4,12},{8,0},{12,4},{16,24},{20,28},{24,16},{28,20},{1,9},{5... | collective-permute-start | bytes 5308424 | tf_op jit(solution)/shard_map/ppermute | solution.py:514
  755.8 119.1 %collective-permute-start.104 = (bf16[384,2304]{1,0:T(8,128)(2,1)}, bf16[384,2304]{1,0:T(8,128)(2,1)}, u32[]{:S(2)}, u32[]{:S(2)}) collective-permute-start(bf16[384,2304]{1,0:T(8,128)(2,1)} %add_convert_fusion.4), channel_id=1, source_target_pairs={{0,16},{4,20},{8,24},{12,28},{16,0},{20,4},{24,8},{28,12},{1,17},{... | collective-permute-start | bytes 5308424 | tf_op jit(solution)/shard_map/ppermute | solution.py:514
  763.7 61.1 %collective-permute-start.87 = (bf16[768,768]{1,0:T(8,128)(2,1)}, bf16[768,768]{1,0:T(8,128)(2,1)}, u32[]{:S(2)}, u32[]{:S(2)}) collective-permute-start(bf16[768,768]{1,0:T(8,128)(2,1)} %get-tuple-element.171), channel_id=1, source_target_pairs={{0,16},{4,20},{8,24},{12,28},{16,0},{20,4},{24,8},{28,12},{1,17},{... | collective-permute-start | bytes 3538952 | tf_op jit(solution)/shard_map/ppermute | solution.py:514
  769.6 75.7 %collective-permute-start.89 = (bf16[768,768]{1,0:T(8,128)(2,1)}, bf16[768,768]{1,0:T(8,128)(2,1)}, u32[]{:S(2)}, u32[]{:S(2)}) collective-permute-start(bf16[768,768]{1,0:T(8,128)(2,1)} %get-tuple-element.172), channel_id=1, source_target_pairs={{0,8},{4,12},{8,0},{12,4},{16,24},{20,28},{24,16},{28,20},{1,9},{5... | collective-permute-start | bytes 3538952 | tf_op jit(solution)/shard_map/ppermute | solution.py:514
  870.1 56.8 %collective-permute-start.75 = (bf16[384,1536]{1,0:T(8,128)(2,1)}, bf16[384,1536]{1,0:T(8,128)(2,1)}, u32[]{:S(2)}, u32[]{:S(2)}) collective-permute-start(bf16[384,1536]{1,0:T(8,128)(2,1)} %get-tuple-element.174), channel_id=1, source_target_pairs={{0,8},{4,12},{8,0},{12,4},{16,24},{20,28},{24,16},{28,20},{1,9},{5... | collective-permute-start | bytes 3538952 | tf_op jit(solution)/shard_map/ppermute | solution.py:514
  874.0 151.5 %collective-permute-start.90 = (bf16[768,1536]{1,0:T(8,128)(2,1)}, bf16[768,1536]{1,0:T(8,128)(2,1)}, u32[]{:S(2)}, u32[]{:S(2)}) collective-permute-start(bf16[768,1536]{1,0:T(8,128)(2,1)} %add_convert_fusion), channel_id=1, source_target_pairs={{0,16},{4,20},{8,24},{12,28},{16,0},{20,4},{24,8},{28,12},{1,17},{... | collective-permute-start | bytes 7077896 | tf_op jit(solution)/shard_map/ppermute | solution.py:514
  875.0 150.6 %collective-permute-start.88 = (bf16[768,1536]{1,0:T(8,128)(2,1)}, bf16[768,1536]{1,0:T(8,128)(2,1)}, u32[]{:S(2)}, u32[]{:S(2)}) collective-permute-start(bf16[768,1536]{1,0:T(8,128)(2,1)} %add_convert_fusion.1), channel_id=1, source_target_pairs={{0,8},{4,12},{8,0},{12,4},{16,24},{20,28},{24,16},{28,20},{1,9},{5... | collective-permute-start | bytes 7077896 | tf_op jit(solution)/shard_map/ppermute | solution.py:514
  949.4 55.2 %collective-permute-start.66 = (bf16[6,24,1536]{2,1,0:T(8,128)(2,1)S(1)}, bf16[6,24,1536]{2,1,0:T(8,128)(2,1)}, u32[]{:S(2)}, u32[]{:S(2)}) collective-permute-start(bf16[6,24,1536]{2,1,0:T(8,128)(2,1)S(1)} %get-tuple-element.178), channel_id=1, source_target_pairs={{0,2},{1,3},{2,0},{3,1},{4,6},{5,7},{6,4},{7,5},{8,10},{9,11},{10,... | collective-permute-start | bytes 1327112 | tf_op jit(solution)/shard_map/ppermute | solution.py:518
  1049.0 110.6 %collective-permute-start.91 = (bf16[1,192,1536]{2,1,0:T(8,128)(2,1)S(1)}, bf16[1,192,1536]{2,1,0:T(8,128)(2,1)S(1)}, u32[]{:S(2)}, u32[]{:S(2)}) collective-permute-start(bf16[1,192,1536]{2,1,0:T(8,128)(2,1)S(1)} %get-tuple-element.162), channel_id=1, source_target_pairs={{0,1},{1,2},{2,3},{3,0},{4,5},{5,6},{6,7},{7,4},{8,9},{9,10},{10,1... | collective-permute-start | bytes 1769480 | tf_op jit(solution)/shard_map/ppermute | solution.py:518
  1059.0 104.6 %collective-permute-start.93 = (bf16[1,192,1536]{2,1,0:T(8,128)(2,1)S(1)}, bf16[1,192,1536]{2,1,0:T(8,128)(2,1)S(1)}, u32[]{:S(2)}, u32[]{:S(2)}) collective-permute-start(bf16[1,192,1536]{2,1,0:T(8,128)(2,1)S(1)} %get-tuple-element.163), channel_id=1, source_target_pairs={{0,3},{1,0},{2,1},{3,2},{4,7},{5,4},{6,5},{7,6},{8,11},{9,8},{10,9... | collective-permute-start | bytes 1769480 | tf_op jit(solution)/shard_map/ppermute | solution.py:518
  1064.0 64.5 %collective-permute-start.85 = (bf16[2,48,3072]{2,1,0:T(8,128)(2,1)S(1)}, bf16[2,48,3072]{2,1,0:T(8,128)(2,1)S(1)}, u32[]{:S(2)}, u32[]{:S(2)}) collective-permute-start(bf16[2,48,3072]{2,1,0:T(8,128)(2,1)S(1)} %get-tuple-element.166), channel_id=1, source_target_pairs={{0,3},{1,0},{2,1},{3,2},{4,7},{5,4},{6,5},{7,6},{8,11},{9,8},{10,9... | collective-permute-start | bytes 1769480 | tf_op jit(solution)/shard_map/ppermute | solution.py:518
  1067.8 85.7 %collective-permute-start.84 = (bf16[2,48,3072]{2,1,0:T(8,128)(2,1)S(1)}, bf16[2,48,3072]{2,1,0:T(8,128)(2,1)S(1)}, u32[]{:S(2)}, u32[]{:S(2)}) collective-permute-start(bf16[2,48,3072]{2,1,0:T(8,128)(2,1)S(1)} %get-tuple-element.167), channel_id=1, source_target_pairs={{0,2},{1,3},{2,0},{3,1},{4,6},{5,7},{6,4},{7,5},{8,10},{9,11},{10,... | collective-permute-start | bytes 1769480 | tf_op jit(solution)/shard_map/ppermute | solution.py:518
  1103.2 64.4 %collective-permute-start.92 = (bf16[1,192,1536]{2,1,0:T(8,128)(2,1)S(1)}, bf16[1,192,1536]{2,1,0:T(8,128)(2,1)S(1)}, u32[]{:S(2)}, u32[]{:S(2)}) collective-permute-start(bf16[1,192,1536]{2,1,0:T(8,128)(2,1)S(1)} %get-tuple-element.164), channel_id=1, source_target_pairs={{0,2},{1,3},{2,0},{3,1},{4,6},{5,7},{6,4},{7,5},{8,10},{9,11},{10,... | collective-permute-start | bytes 1769480 | tf_op jit(solution)/shard_map/ppermute | solution.py:518
  (216 other events, 4867.1 us)
